TPU v7x, 32 devices: a whole 2x2x4 slice. The times are simulated.
32 devices in a mesh: dp: 8 (over z, y), tensor: 4 (over x, core).
Axes of the slice: x: 2, y: 2, z: 4, core: 2. Of those that a mesh axis runs over, the one named last changes fastest.
Arguments:
- layer_input: bfloat16 [8192, 1024], P(('dp', 'tensor')), may hold values from -22 to 22
- out_grad: bfloat16 [8192, 1024], P(('dp', 'tensor')), may hold values from -6 to 6
- segment_ids: int32 [8192], P('dp'), may hold values from 0 to 24, as said below
- valid_mask: int32 [8192], P(('dp', 'tensor')), may hold values from 0 to 1, as said below
- doc_start: int32 [8192], P('dp'), may hold values from 0 to 1023, as said below
- norm_gains: bfloat16 [2, 1024], P(None, ('dp', 'tensor')), may hold values from 0.099609375 to 1.8984375
- conv_weight: bfloat16 [4, 1792], P(None, ('dp', 'tensor')), may hold values from -3 to 3
- conv_bias: bfloat16 [1792], P(('dp', 'tensor')), may hold values from -3 to 3
- mixer_gain: bfloat16 [1536], P(('dp', 'tensor')), may hold values from 0.099609375 to 1.8984375
- shared_proj: bfloat16 [1024, 512], P(('dp', 'tensor')), may hold values from -0.1875 to 0.1875
- step_bias: float32 [24], replicated, may hold values from -5 to -1
- decay_log: float32 [24], replicated, may hold values from -2 to 1.5
- skip_gain: float32 [24], replicated, may hold values from 0.5 to 1.5
- mamba_gate: bfloat16 [1024, 1536], P('dp', 'tensor'), may hold values from -0.1875 to 0.1875
- mamba_input: bfloat16 [1024, 1536], P('dp', 'tensor'), may hold values from -0.1875 to 0.1875
- mamba_step: bfloat16 [1024, 24], P('dp', 'tensor'), may hold values from -0.1875 to 0.1875
- query_proj: bfloat16 [1024, 512], P('dp', 'tensor'), may hold values from -0.1875 to 0.1875
- mamba_out: bfloat16 [1536, 1024], P('tensor', 'dp'), may hold values from -0.15625 to 0.15625
- attention_out: bfloat16 [512, 1024], P('tensor', 'dp'), may hold values from -2 to 2
- swiglu_gate: bfloat16 [1024, 2048], P('dp', 'tensor'), may hold values from -0.1875 to 0.1875
- swiglu_up: bfloat16 [1024, 2048], P('dp', 'tensor'), may hold values from -0.1875 to 0.1875
- swiglu_down: bfloat16 [2048, 1024], P('tensor', 'dp'), may hold values from -0.125 to 0.125
Outputs:
- layer_output: bfloat16 [8192, 1024], P(('dp', 'tensor'))
- input_grad: float32 [8192, 1024], P(('dp', 'tensor'))
- norm_gains_grad: float32 [2, 1024], P(None, ('dp', 'tensor'))
- conv_weight_grad: float32 [4, 1792], P(None, ('dp', 'tensor'))
- conv_bias_grad: float32 [1792], P(('dp', 'tensor'))
- mixer_gain_grad: float32 [1536], P(('dp', 'tensor'))
- shared_proj_grad: float32 [1024, 512], P(('dp', 'tensor'))
- step_bias_grad: float32 [24], replicated
- decay_log_grad: float32 [24], replicated
- skip_gain_grad: float32 [24], replicated
- mamba_gate_grad: float32 [1024, 1536], P('dp', 'tensor')
- mamba_input_grad: float32 [1024, 1536], P('dp', 'tensor')
- mamba_step_grad: float32 [1024, 24], P('dp', 'tensor')
- query_proj_grad: float32 [1024, 512], P('dp', 'tensor')
- mamba_out_grad: float32 [1536, 1024], P('tensor', 'dp')
- attention_out_grad: float32 [512, 1024], P('tensor', 'dp')
- swiglu_gate_grad: float32 [1024, 2048], P('dp', 'tensor')
- swiglu_up_grad: float32 [1024, 2048], P('dp', 'tensor')
- swiglu_down_grad: float32 [2048, 1024], P('tensor', 'dp')
- residual_rms: float32 [5], replicated
Inputs may be any that keep to these rules, and one draw needn't show every extreme that they name: `segment_ids`: within each sequence of 1024 tokens the ids start at 0 and never fall; the padding at a sequence's end, 16 to 128 tokens, has id 24. `valid_mask`: 1 exactly where the segment id is below 24. `doc_start`: the position in its sequence of the token's first document token; for padding, the first padding position.
All inputs are finite; a program needn't handle non-finite values.
Results may differ from a plain program's by a relative error of at most 0.02.
Values may be sent and summed in bfloat16 or wider, within the bound.
No kernel may reach another device: no remote copies, remote signals or barrier semaphores. Data moves between devices by JAX's collectives and lax.ppermute only.
A program may use at most 192 MiB of HBM per device.

v0:
```python
import math

import jax
import jax.numpy as jnp
from jax import lax
from jax.sharding import PartitionSpec as P

D = 1024
MH = 24
HEAD_SIZE = 64
MAMBA_STATES = 128
CONV = 4
QUERY_HEADS = 8
KEY_VALUE_HEADS = 2
SEQUENCE_TOKENS = 1024
DSSM = 1536


EPS = 1e-05
ROPE_BASE = 100000000000.0
NEG_FILL = -1e30
HIGH = lax.Precision.HIGHEST


def rms_scale(values):
    return lax.rsqrt(jnp.mean(values * values, axis=-1, keepdims=True) + EPS)


def norm_back(values, row_scale, gain_row, grad_in):
    scaled_grad = grad_in * gain_row
    gain_grad = jnp.sum(grad_in * values * row_scale, axis=0)
    value_grad = row_scale * scaled_grad - values * (row_scale * row_scale * row_scale) * jnp.mean(
        scaled_grad * values, axis=-1, keepdims=True
    )
    return (value_grad, gain_grad)


def product(left, right):
    return jnp.dot(left, right, preferred_element_type=jnp.float32)


def product_tn(left, right):
    return lax.dot_general(
        left, right, (((0,), (0,)), ((), ())), preferred_element_type=jnp.float32
    )


def product_nt(left, right):
    return lax.dot_general(
        left, right, (((1,), (1,)), ((), ())), preferred_element_type=jnp.float32
    )


def rope_tables(position):
    half_width = HEAD_SIZE // 2
    inverse = jnp.exp(
        jnp.arange(half_width, dtype=jnp.float32) * (-2.0 * math.log(ROPE_BASE) / HEAD_SIZE)
    )
    angles = position.astype(jnp.float32)[:, None] * inverse[None, :]
    return (jnp.cos(angles), jnp.sin(angles))


def apply_rotary(values, cosine_table, sine_table):
    half_width = values.shape[-1] // 2
    first_half = values[..., :half_width]
    second_half = values[..., half_width:]
    cos_col = cosine_table[:, None, :]
    sin_col = sine_table[:, None, :]
    return jnp.concatenate(
        [
            first_half * cos_col - second_half * sin_col,
            second_half * cos_col + first_half * sin_col,
        ],
        axis=-1,
    )


def rotate_back(grads_in, cosine_table, sine_table):
    half_width = grads_in.shape[-1] // 2
    first_half = grads_in[..., :half_width]
    second_half = grads_in[..., half_width:]
    cos_col = cosine_table[:, None, :]
    sin_col = sine_table[:, None, :]
    return jnp.concatenate(
        [
            first_half * cos_col + second_half * sin_col,
            second_half * cos_col - first_half * sin_col,
        ],
        axis=-1,
    )


def mamba_sequence(
    x_part, bc_part, raw_part, segments, conv_w, conv_b, bias_part, decay_part, skip_part
):
    length = x_part.shape[0]
    head_count = raw_part.shape[1]
    head_width = x_part.shape[1] // head_count
    state_size = bc_part.shape[1] // 2
    conv_input = jnp.concatenate([x_part, bc_part], axis=1)
    tap_count = conv_w.shape[0]
    conv_sum = conv_b[None, :] + conv_w[tap_count - 1][None, :] * conv_input
    for lag_steps in range(1, tap_count):
        lagged = jnp.concatenate(
            [
                jnp.zeros((lag_steps, conv_input.shape[1]), conv_input.dtype),
                conv_input[:-lag_steps],
            ],
            axis=0,
        )
        prior_seg = jnp.concatenate(
            [jnp.full((lag_steps,), -1, jnp.int32), segments[:-lag_steps]], axis=0
        )
        same_doc = (prior_seg == segments).astype(conv_input.dtype)[:, None]
        conv_sum = conv_sum + conv_w[tap_count - 1 - lag_steps][None, :] * lagged * same_doc
    activated = jax.nn.silu(conv_sum)
    inner_width = head_count * head_width
    conv_x = activated[:, :inner_width].reshape(length, head_count, head_width)
    state_in = activated[:, inner_width : inner_width + state_size]
    state_out = activated[:, inner_width + state_size :]
    step_size = jax.nn.softplus(raw_part + bias_part[None, :])
    decay_rate = step_size * (-jnp.exp(decay_part))[None, :]
    log_decay = jnp.cumsum(decay_rate, axis=0).T
    pair_dot = jnp.dot(state_out, state_in.T, precision=HIGH)
    positions = jnp.arange(length, dtype=jnp.int32)
    allowed = (positions[:, None] >= positions[None, :]) & (segments[:, None] == segments[None, :])
    decay_gap = jnp.where(allowed[None], log_decay[:, :, None] - log_decay[:, None, :], 0.0)
    decay_mat = jnp.where(allowed[None], jnp.exp(decay_gap), 0.0) * pair_dot[None]
    driven = conv_x * step_size[:, :, None]
    mixing = jnp.einsum("hij,jhp->ihp", decay_mat, driven, precision=HIGH)
    return (mixing + skip_part[None, :, None] * conv_x).reshape(length, inner_width)


def allowed_pairs(segments):
    positions = jnp.arange(segments.shape[0], dtype=jnp.int32)
    return (positions[:, None] >= positions[None, :]) & (segments[:, None] == segments[None, :])


def attention_forward(query_rot, key_sel, value_sel, segments):
    allowed = allowed_pairs(segments)
    score_scale = 1.0 / math.sqrt(HEAD_SIZE)
    scores = (
        jnp.einsum("ihd,jhd->hij", query_rot, key_sel, preferred_element_type=jnp.float32)
        * score_scale
    )
    masked = jnp.where(allowed[None], scores, NEG_FILL)
    row_peak = jnp.max(masked, axis=-1, keepdims=True)
    shifted_exp = jnp.exp(masked - row_peak)
    row_total = jnp.sum(shifted_exp, axis=-1, keepdims=True)
    attn_probs = (shifted_exp / row_total).astype(jnp.bfloat16)
    attended = jnp.einsum("hij,jhd->ihd", attn_probs, value_sel, preferred_element_type=jnp.float32)
    return (attended.astype(jnp.bfloat16), (row_peak + jnp.log(row_total))[..., 0])


def attention_backward(query_rot, key_sel, value_sel, segments, log_total, attended_grad):
    allowed = allowed_pairs(segments)
    score_scale = 1.0 / math.sqrt(HEAD_SIZE)
    scores = (
        jnp.einsum("ihd,jhd->hij", query_rot, key_sel, preferred_element_type=jnp.float32)
        * score_scale
    )
    masked = jnp.where(allowed[None], scores, NEG_FILL)
    attn_probs = jnp.exp(masked - log_total[..., None])
    prob_grad = jnp.einsum(
        "ihd,jhd->hij", attended_grad, value_sel, preferred_element_type=jnp.float32
    )
    score_grad = (
        attn_probs * (prob_grad - jnp.sum(attn_probs * prob_grad, axis=-1, keepdims=True))
    ).astype(jnp.bfloat16)
    query_grad = (
        jnp.einsum("hij,jhd->ihd", score_grad, key_sel, preferred_element_type=jnp.float32)
        * score_scale
    )
    key_grad = (
        jnp.einsum("hij,ihd->jhd", score_grad, query_rot, preferred_element_type=jnp.float32)
        * score_scale
    )
    value_grad = jnp.einsum(
        "hij,ihd->jhd",
        attn_probs.astype(jnp.bfloat16),
        attended_grad,
        preferred_element_type=jnp.float32,
    )
    return (query_grad, key_grad, value_grad)


def ffn_forward(inputs_b, gate_w, up_w, down_w):
    gate_act = product(inputs_b, gate_w)
    up_act = product(inputs_b, up_w)
    hidden_b = (jax.nn.silu(gate_act) * up_act).astype(jnp.bfloat16)
    return (gate_act, up_act, hidden_b, product(hidden_b, down_w))


def ffn_backward(inputs_b, gate_act, up_act, hidden_b, gate_w, up_w, down_w, grad_b):
    down_grad = product_tn(hidden_b, grad_b)
    hidden_grad = product_nt(grad_b, down_w)
    sigmoid_gate = jax.nn.sigmoid(gate_act)
    gate_grad = (
        hidden_grad * up_act * sigmoid_gate * (1.0 + gate_act * (1.0 - sigmoid_gate))
    ).astype(jnp.bfloat16)
    up_grad = (hidden_grad * jax.nn.silu(gate_act)).astype(jnp.bfloat16)
    input_part = product_nt(gate_grad, gate_w) + product_nt(up_grad, up_w)
    return (input_part, product_tn(inputs_b, gate_grad), product_tn(inputs_b, up_grad), down_grad)


def seq_gather(values):
    return lax.all_gather(values, "tensor", axis=0, tiled=True)


def seq_reduce(values):
    return lax.psum_scatter(
        values.astype(jnp.bfloat16), "tensor", scatter_dimension=0, tiled=True
    ).astype(jnp.float32)


def width_total(values):
    return lax.psum(values, "tensor")


def local(
    layer_input,
    out_grad,
    segment_ids,
    valid_mask,
    doc_start,
    norm_gains,
    conv_weight,
    conv_bias,
    mixer_gain,
    shared_proj,
    step_bias,
    decay_log,
    skip_gain,
    mamba_gate,
    mamba_input,
    mamba_step,
    query_proj,
    mamba_out,
    attention_out,
    swiglu_gate,
    swiglu_up,
    swiglu_down,
):
    tensor_position = lax.axis_index("tensor")
    gains_all, conv_all, shift_all, mixer_gain_all, shared_w = (
        lax.all_gather(norm_gains, ("dp", "tensor"), axis=1, tiled=True),
        lax.all_gather(conv_weight, ("dp", "tensor"), axis=1, tiled=True),
        lax.all_gather(conv_bias, ("dp", "tensor"), axis=0, tiled=True),
        lax.all_gather(mixer_gain, ("dp", "tensor"), axis=0, tiled=True),
        lax.all_gather(shared_proj, ("dp", "tensor"), axis=0, tiled=True),
    )
    gate_w, input_w, step_w, query_w, mamba_out_w, attend_out_w = (
        lax.all_gather(mamba_gate, "dp", axis=0, tiled=True),
        lax.all_gather(mamba_input, "dp", axis=0, tiled=True),
        lax.all_gather(mamba_step, "dp", axis=0, tiled=True),
        lax.all_gather(query_proj, "dp", axis=0, tiled=True),
        lax.all_gather(mamba_out, "dp", axis=1, tiled=True),
        lax.all_gather(attention_out, "dp", axis=1, tiled=True),
    )
    ffn_gate_w, ffn_up_w, ffn_down_w = (
        lax.all_gather(swiglu_gate, "dp", axis=0, tiled=True),
        lax.all_gather(swiglu_up, "dp", axis=0, tiled=True),
        lax.all_gather(swiglu_down, "dp", axis=1, tiled=True),
    )
    tokens_f = layer_input.astype(jnp.float32)
    gains_f = gains_all.astype(jnp.float32)
    scale_one = rms_scale(tokens_f)
    first_b = (tokens_f * scale_one * gains_f[0]).astype(jnp.bfloat16)
    first_full = seq_gather(first_b)
    tokens_per_group = first_full.shape[0]
    seq_count = tokens_per_group // SEQUENCE_TOKENS
    head_local = step_w.shape[1]
    local_width = gate_w.shape[1]
    query_slice = query_w.shape[1] // HEAD_SIZE
    channel_start = tensor_position * local_width
    head_start = tensor_position * head_local
    gate_z = product(first_full, gate_w)
    mamba_x = product(first_full, input_w)
    step_raw = product(first_full, step_w)
    query_act = product(first_full, query_w)
    common_input = product(first_full, shared_w)
    conv_f = conv_all.astype(jnp.float32)
    shift_f = shift_all.astype(jnp.float32)
    own_conv = jnp.concatenate(
        [lax.dynamic_slice_in_dim(conv_f, channel_start, local_width, 1), conv_f[:, DSSM:]], axis=1
    )
    own_shift = jnp.concatenate(
        [lax.dynamic_slice_in_dim(shift_f, channel_start, local_width, 0), shift_f[DSSM:]], axis=0
    )
    own_bias = lax.dynamic_slice_in_dim(step_bias, head_start, head_local, 0)
    own_decay = lax.dynamic_slice_in_dim(decay_log, head_start, head_local, 0)
    own_skip = lax.dynamic_slice_in_dim(skip_gain, head_start, head_local, 0)
    own_gain = lax.dynamic_slice_in_dim(
        mixer_gain_all.astype(jnp.float32), channel_start, local_width, 0
    )
    seg_stack = segment_ids.reshape(seq_count, SEQUENCE_TOKENS)

    def mamba_group(x_part, bc_part, raw_part, conv_w, conv_b, bias_part, decay_part, skip_part):

        def one_sequence(pieces):
            return mamba_sequence(
                pieces[0],
                pieces[1],
                pieces[2],
                pieces[3],
                conv_w,
                conv_b,
                bias_part,
                decay_part,
                skip_part,
            )

        outputs = lax.map(
            jax.checkpoint(one_sequence),
            (
                x_part.reshape(seq_count, SEQUENCE_TOKENS, -1),
                bc_part.reshape(seq_count, SEQUENCE_TOKENS, -1),
                raw_part.reshape(seq_count, SEQUENCE_TOKENS, -1),
                seg_stack,
            ),
        )
        return outputs.reshape(tokens_per_group, -1)

    mamba_y, mamba_pull = jax.vjp(
        mamba_group,
        mamba_x,
        common_input[:, : 2 * MAMBA_STATES],
        step_raw,
        own_conv,
        own_shift,
        own_bias,
        own_decay,
        own_skip,
    )
    silu_z = jax.nn.silu(gate_z)
    gated_y = mamba_y * silu_z
    square_sum = width_total(jnp.sum(gated_y * gated_y, axis=1))
    gate_scale = lax.rsqrt(square_sum / DSSM + EPS)[:, None]
    normed_b = (gated_y * gate_scale * own_gain).astype(jnp.bfloat16)
    position = jnp.tile(jnp.arange(SEQUENCE_TOKENS, dtype=jnp.int32), seq_count) - doc_start
    cosine_table, sine_table = rope_tables(position)
    key_value_index = (
        tensor_position * query_slice + jnp.arange(query_slice, dtype=jnp.int32)
    ) // (QUERY_HEADS // KEY_VALUE_HEADS)
    picker_mask = key_value_index[:, None] == jnp.arange(KEY_VALUE_HEADS, dtype=jnp.int32)[None, :]
    select_b = picker_mask.astype(jnp.bfloat16)
    select_f = picker_mask.astype(jnp.float32)
    query_rot = apply_rotary(
        query_act.reshape(tokens_per_group, query_slice, HEAD_SIZE), cosine_table, sine_table
    ).astype(jnp.bfloat16)
    rotated_key = apply_rotary(
        common_input[:, 2 * MAMBA_STATES : 2 * MAMBA_STATES + KEY_VALUE_HEADS * HEAD_SIZE].reshape(
            tokens_per_group, KEY_VALUE_HEADS, HEAD_SIZE
        ),
        cosine_table,
        sine_table,
    ).astype(jnp.bfloat16)
    value_lowered = (
        common_input[:, 2 * MAMBA_STATES + KEY_VALUE_HEADS * HEAD_SIZE :]
        .reshape(tokens_per_group, KEY_VALUE_HEADS, HEAD_SIZE)
        .astype(jnp.bfloat16)
    )
    key_sel = jnp.einsum(
        "lkd,hk->lhd", rotated_key, select_b, preferred_element_type=jnp.float32
    ).astype(jnp.bfloat16)
    value_sel = jnp.einsum(
        "lkd,hk->lhd", value_lowered, select_b, preferred_element_type=jnp.float32
    ).astype(jnp.bfloat16)

    def per_seq(values):
        return values.reshape((seq_count, SEQUENCE_TOKENS) + values.shape[1:])

    def attend_one(pieces):
        return attention_forward(pieces[0], pieces[1], pieces[2], pieces[3])

    attended_b, log_total = lax.map(
        attend_one, (per_seq(query_rot), per_seq(key_sel), per_seq(value_sel), seg_stack)
    )
    attended_flat = attended_b.reshape(tokens_per_group, query_slice * HEAD_SIZE)
    mixer_sum = seq_reduce(product(normed_b, mamba_out_w) + product(attended_flat, attend_out_w))
    middle = tokens_f + mixer_sum
    scale_two = rms_scale(middle)
    second_b = (middle * scale_two * gains_f[1]).astype(jnp.bfloat16)
    ffn_in = seq_gather(second_b)
    gate_act, up_act, hidden_b, ffn_part = ffn_forward(ffn_in, ffn_gate_w, ffn_up_w, ffn_down_w)
    ffn_out = seq_reduce(ffn_part)
    result = middle + ffn_out
    valid_f = valid_mask.astype(jnp.float32)
    out_cot = out_grad.astype(jnp.float32) * valid_f[:, None]
    cot_b = out_cot.astype(jnp.bfloat16)
    ffn_grad_in = seq_gather(cot_b)
    second_part, gate_w_grad, up_w_grad, down_w_grad = ffn_backward(
        ffn_in, gate_act, up_act, hidden_b, ffn_gate_w, ffn_up_w, ffn_down_w, ffn_grad_in
    )
    second_grad = seq_reduce(second_part)
    gate_w_grad, up_w_grad, down_w_grad = (
        lax.psum_scatter(
            gate_w_grad.astype(jnp.bfloat16), "dp", scatter_dimension=0, tiled=True
        ).astype(jnp.float32),
        lax.psum_scatter(
            up_w_grad.astype(jnp.bfloat16), "dp", scatter_dimension=0, tiled=True
        ).astype(jnp.float32),
        lax.psum_scatter(
            down_w_grad.astype(jnp.bfloat16), "dp", scatter_dimension=1, tiled=True
        ).astype(jnp.float32),
    )
    second_value_grad, gain_two_grad = norm_back(middle, scale_two, gains_f[1], second_grad)
    middle_grad = out_cot + second_value_grad
    mixer_grad_full = seq_gather(middle_grad.astype(jnp.bfloat16))
    mamba_out_grad = product_tn(normed_b, mixer_grad_full)
    attend_out_grad = product_tn(attended_flat, mixer_grad_full)
    normed_grad = product_nt(mixer_grad_full, mamba_out_w)
    attended_grad = (
        product_nt(mixer_grad_full, attend_out_w)
        .astype(jnp.bfloat16)
        .reshape(tokens_per_group, query_slice, HEAD_SIZE)
    )
    scaled_normed = normed_grad * own_gain
    own_gain_grad = jnp.sum(normed_grad * gated_y * gate_scale, axis=0)
    inner_sum = width_total(jnp.sum(scaled_normed * gated_y, axis=1))
    gated_grad = (
        gate_scale * scaled_normed
        - gated_y * (gate_scale * gate_scale * gate_scale) * (inner_sum / DSSM)[:, None]
    )
    sigmoid_z = jax.nn.sigmoid(gate_z)
    mamba_y_grad = gated_grad * silu_z
    gate_z_grad = (gated_grad * mamba_y * sigmoid_z * (1.0 + gate_z * (1.0 - sigmoid_z))).astype(
        jnp.bfloat16
    )
    x_grad, bc_grad, raw_grad, conv_grad, shift_grad, bias_grad, decay_grad, skip_grad = mamba_pull(
        mamba_y_grad
    )

    def attend_back(pieces):
        return attention_backward(pieces[0], pieces[1], pieces[2], pieces[3], pieces[4], pieces[5])

    query_rot_grad, key_sel_grad, value_sel_grad = lax.map(
        attend_back,
        (
            per_seq(query_rot),
            per_seq(key_sel),
            per_seq(value_sel),
            seg_stack,
            log_total,
            per_seq(attended_grad),
        ),
    )
    key_gradient_heads = jnp.einsum(
        "lhd,hk->lkd", key_sel_grad.reshape(tokens_per_group, query_slice, HEAD_SIZE), select_f
    )
    value_gradient_heads = jnp.einsum(
        "lhd,hk->lkd", value_sel_grad.reshape(tokens_per_group, query_slice, HEAD_SIZE), select_f
    )
    key_gradient_heads = rotate_back(key_gradient_heads, cosine_table, sine_table)
    query_grad = (
        rotate_back(
            query_rot_grad.reshape(tokens_per_group, query_slice, HEAD_SIZE),
            cosine_table,
            sine_table,
        )
        .reshape(tokens_per_group, query_slice * HEAD_SIZE)
        .astype(jnp.bfloat16)
    )
    shared_grad = jnp.concatenate(
        [
            bc_grad,
            key_gradient_heads.reshape(tokens_per_group, KEY_VALUE_HEADS * HEAD_SIZE),
            value_gradient_heads.reshape(tokens_per_group, KEY_VALUE_HEADS * HEAD_SIZE),
        ],
        axis=1,
    ).astype(jnp.bfloat16)
    x_grad_b = x_grad.astype(jnp.bfloat16)
    raw_grad_b = raw_grad.astype(jnp.bfloat16)
    first_part = (
        product_nt(gate_z_grad, gate_w)
        + product_nt(x_grad_b, input_w)
        + product_nt(raw_grad_b, step_w)
        + product_nt(query_grad, query_w)
        + product_nt(shared_grad, shared_w)
    )
    first_grad = seq_reduce(first_part)
    first_value_grad, gain_one_grad = norm_back(tokens_f, scale_one, gains_f[0], first_grad)
    input_grad = middle_grad + first_value_grad
    (
        gate_proj_grad,
        input_proj_grad,
        step_proj_grad,
        query_proj_grad,
        mamba_out_grad,
        attend_out_grad,
    ) = (
        lax.psum_scatter(
            product_tn(first_full, gate_z_grad).astype(jnp.bfloat16),
            "dp",
            scatter_dimension=0,
            tiled=True,
        ).astype(jnp.float32),
        lax.psum_scatter(
            product_tn(first_full, x_grad_b).astype(jnp.bfloat16),
            "dp",
            scatter_dimension=0,
            tiled=True,
        ).astype(jnp.float32),
        lax.psum_scatter(
            product_tn(first_full, raw_grad_b).astype(jnp.bfloat16),
            "dp",
            scatter_dimension=0,
            tiled=True,
        ).astype(jnp.float32),
        lax.psum_scatter(
            product_tn(first_full, query_grad).astype(jnp.bfloat16),
            "dp",
            scatter_dimension=0,
            tiled=True,
        ).astype(jnp.float32),
        lax.psum_scatter(
            mamba_out_grad.astype(jnp.bfloat16), "dp", scatter_dimension=1, tiled=True
        ).astype(jnp.float32),
        lax.psum_scatter(
            attend_out_grad.astype(jnp.bfloat16), "dp", scatter_dimension=1, tiled=True
        ).astype(jnp.float32),
    )
    conv_full_grad = jnp.concatenate(
        [
            lax.dynamic_update_slice_in_dim(
                jnp.zeros((CONV, DSSM), jnp.float32), conv_grad[:, :local_width], channel_start, 1
            ),
            conv_grad[:, local_width:],
        ],
        axis=1,
    )
    shift_full_grad = jnp.concatenate(
        [
            lax.dynamic_update_slice_in_dim(
                jnp.zeros((DSSM,), jnp.float32), shift_grad[:local_width], channel_start, 0
            ),
            shift_grad[local_width:],
        ],
        axis=0,
    )
    gain_full_grad = lax.dynamic_update_slice_in_dim(
        jnp.zeros((DSSM,), jnp.float32), own_gain_grad, channel_start, 0
    )
    gains_grad = jnp.stack([gain_one_grad, gain_two_grad], axis=0)
    gains_grad, conv_full_grad, shift_full_grad, gain_full_grad, shared_proj_grad = (
        lax.psum_scatter(gains_grad, ("dp", "tensor"), scatter_dimension=1, tiled=True),
        lax.psum_scatter(conv_full_grad, ("dp", "tensor"), scatter_dimension=1, tiled=True),
        lax.psum_scatter(shift_full_grad, ("dp", "tensor"), scatter_dimension=0, tiled=True),
        lax.psum_scatter(gain_full_grad, ("dp", "tensor"), scatter_dimension=0, tiled=True),
        lax.psum_scatter(
            product_tn(first_full, shared_grad), ("dp", "tensor"), scatter_dimension=0, tiled=True
        ),
    )
    bias_full = lax.dynamic_update_slice_in_dim(
        jnp.zeros((MH,), jnp.float32), bias_grad, head_start, 0
    )
    decay_full = lax.dynamic_update_slice_in_dim(
        jnp.zeros((MH,), jnp.float32), decay_grad, head_start, 0
    )
    skip_full = lax.dynamic_update_slice_in_dim(
        jnp.zeros((MH,), jnp.float32), skip_grad, head_start, 0
    )
    tracked = (tokens_f, mixer_sum, middle, ffn_out, result)
    stat_terms = jnp.stack(
        [jnp.sum(valid_f * jnp.sum(tracked_arr * tracked_arr, axis=1)) for tracked_arr in tracked]
    )
    stat_totals, count_all, bias_total, decay_total, skip_total = lax.psum(
        (stat_terms, jnp.sum(valid_f), bias_full, decay_full, skip_full), ("dp", "tensor")
    )
    residual_rms = jnp.sqrt(stat_totals / (count_all * D))
    return (
        result.astype(jnp.bfloat16),
        input_grad,
        gains_grad,
        conv_full_grad,
        shift_full_grad,
        gain_full_grad,
        shared_proj_grad,
        bias_total,
        decay_total,
        skip_total,
        gate_proj_grad,
        input_proj_grad,
        step_proj_grad,
        query_proj_grad,
        mamba_out_grad,
        attend_out_grad,
        gate_w_grad,
        up_w_grad,
        down_w_grad,
        residual_rms,
    )


def solution(mesh):
    in_specs = (
        P(("dp", "tensor"), None),
        P(("dp", "tensor"), None),
        P("dp"),
        P(("dp", "tensor")),
        P("dp"),
        P(None, ("dp", "tensor")),
        P(None, ("dp", "tensor")),
        P(("dp", "tensor")),
        P(("dp", "tensor")),
        P(("dp", "tensor"), None),
        P(),
        P(),
        P(),
        P("dp", "tensor"),
        P("dp", "tensor"),
        P("dp", "tensor"),
        P("dp", "tensor"),
        P("tensor", "dp"),
        P("tensor", "dp"),
        P("dp", "tensor"),
        P("dp", "tensor"),
        P("tensor", "dp"),
    )
    out_specs = (
        P(("dp", "tensor"), None),
        P(("dp", "tensor"), None),
        P(None, ("dp", "tensor")),
        P(None, ("dp", "tensor")),
        P(("dp", "tensor")),
        P(("dp", "tensor")),
        P(("dp", "tensor"), None),
        P(),
        P(),
        P(),
        P("dp", "tensor"),
        P("dp", "tensor"),
        P("dp", "tensor"),
        P("dp", "tensor"),
        P("tensor", "dp"),
        P("tensor", "dp"),
        P("dp", "tensor"),
        P("dp", "tensor"),
        P("tensor", "dp"),
        P(),
    )
    return jax.shard_map(local, mesh=mesh, in_specs=in_specs, out_specs=out_specs, check_vma=False)
```

profile of v0, /device:TPU:0, one launch (start us, length us, event | category | flops | bytes accessed | tf_op | source)
XLA Modules:
  0.0 1733.4 jit_solution(9928088505092876206)
XLA Ops:
  8.8 43.2 %all-gather.1 = bf16[32,32,2]{1,2,0:T(2,128)(2,1)S(1)} all-gather(bf16[1,32,2]{1,2,0:T(2,128)(2,1)} %bitcast.302), channel_id=1, replica_groups=mesh['dp'=8,'tensor'=4] {'dp','tensor'}, dimensions={0}, use_global_device_ids=true | all-gather | bytes 4224 | tf_op jit(solution)/shard_map/all_gather | solution.py:246
  60.4 37.0 %all-reduce.26 = (bf16[1792]{0:T(1024)(128)(2,1)S(1)}, bf16[1536]{0:T(1024)(128)(2,1)S(1)}) all-reduce(bf16[1792]{0:T(1024)(128)(2,1)S(1)} %dynamic-update-slice, bf16[1536]{0:T(1024)(128)(2,1)S(1)} %dynamic-update-slice.1), channel_id=1, replica_groups=mesh['dp'=8,'tensor'=4] {'dp','tensor'}, use_global_device_ids=true, to_apply=%add.20 | all-reduce | flops 3328 | bytes 13312
  97.5 40.7 %all-gather = bf16[32,56,4]{1,2,0:T(4,128)(2,1)S(1)} all-gather(bf16[1,56,4]{1,2,0:T(4,128)(2,1)} %bitcast.301), channel_id=1, replica_groups=mesh['dp'=8,'tensor'=4] {'dp','tensor'}, dimensions={0}, use_global_device_ids=true | all-gather | bytes 14784 | tf_op jit(solution)/shard_map/all_gather | solution.py:247
  142.9 26.7 %all_gather.60 = bf16[1024,6]{0,1:T(8,128)(2,1)} all-gather(bf16[128,6]{0,1:T(8,128)(2,1)S(1)} %copy-done.116), channel_id=1, replica_groups=mesh['dp'=8,'tensor'=4] {'dp'}, dimensions={0}, use_global_device_ids=true | all-gather | bytes 13824 | tf_op jit(solution)/shard_map/all_gather | solution.py:255
  172.0 30.7 %all_gather.64 = bf16[1024,128]{1,0:T(8,128)(2,1)S(1)} all-gather(bf16[128,128]{1,0:T(8,128)(2,1)S(1)} %copy-done.78), channel_id=1, replica_groups=mesh['dp'=8,'tensor'=4] {'dp'}, dimensions={0}, use_global_device_ids=true | all-gather | bytes 294912 | tf_op jit(solution)/shard_map/all_gather | solution.py:256
  202.7 26.8 %all_gather.65 = bf16[128,1024]{1,0:T(8,128)(2,1)S(1)} all-gather(bf16[128,128]{1,0:T(8,128)(2,1)S(1)} %copy-done.79), channel_id=1, replica_groups=mesh['dp'=8,'tensor'=4] {'dp'}, dimensions={1}, use_global_device_ids=true | all-gather | bytes 294912 | tf_op jit(solution)/shard_map/all_gather | solution.py:258
  231.4 32.4 %all_gather.61 = bf16[1024,384]{1,0:T(8,128)(2,1)S(1)} all-gather(bf16[128,384]{1,0:T(8,128)(2,1)S(1)} %copy-done.66), channel_id=1, replica_groups=mesh['dp'=8,'tensor'=4] {'dp'}, dimensions={0}, use_global_device_ids=true | all-gather | bytes 884736 | tf_op jit(solution)/shard_map/all_gather | solution.py:253
  263.9 34.4 %all_gather.58 = bf16[1024,384]{1,0:T(8,128)(2,1)} all-gather(bf16[128,384]{1,0:T(8,128)(2,1)S(1)} %copy-done.67), channel_id=1, replica_groups=mesh['dp'=8,'tensor'=4] {'dp'}, dimensions={0}, use_global_device_ids=true | all-gather | bytes 884736 | tf_op jit(solution)/shard_map/all_gather | solution.py:254
  298.3 29.2 %all_gather.63 = bf16[384,1024]{1,0:T(8,128)(2,1)} all-gather(bf16[384,128]{1,0:T(8,128)(2,1)S(1)} %copy-done.68), channel_id=1, replica_groups=mesh['dp'=8,'tensor'=4] {'dp'}, dimensions={1}, use_global_device_ids=true | all-gather | bytes 884736 | tf_op jit(solution)/shard_map/all_gather | solution.py:257
  327.5 3.1 fusion.158
  335.8 3.3 divide_multiply_fusion
  339.2 5.1 fusion.91
  346.8 4.1 reduce-window.36
  359.8 27.6 %bitcast_add_fusion = f32[1024,6,64]{0,2,1:T(8,128)S(1)} fusion(f32[1024,6,64]{0,2,1:T(8,128)S(1)} %bitcast.247, f32[1024,1024]{1,0:T(8,128)S(1)} %copy-done.22, f32[6,1024]{1,0:T(8,128)S(1)} %bitcast.293, pred[1024,1024]{1,0:T(8,128)(4,1)S(1)} %copy-done.48, f32[6]{0:T(128)S(1)} %copy-done.122, f32[1024,6]{0,1:T(8,128)S(1)} %copy-done.77), kind=kOutput, calls=%fused_computation.92 | convolution fusion | flops 4858183680 | bytes 8437784 | tf_op jit(solution)/shard_map/jvp()/while/body/eval_jaxpr/hij,jhp->ihp/dot_general | solution.py:130
  387.4 3.5 multiply_reduce_fusion.9
  391.0 5.9 psum.49
  397.4 3.2 fusion.156
  410.8 28.1 %reduce-scatter.27.cloned.1.call-done = bf16[256,1024]{1,0:T(8,128)(2,1)} async-done(((bf16[1024,1024]{1,0:T(8,128)(2,1)}), bf16[256,1024]{1,0:T(8,128)(2,1)}) %reduce-scatter.27.cloned.1.call-update) | async-done | bytes 524304 | tf_op jit(solution)/shard_map/reduce_scatter | solution.py:211
  445.2 5.4 all-gather.19.cloned.1.call-done
  450.6 23.1 %all-gather.15.cloned.1.call-done = bf16[1024,1024]{1,0:T(8,128)(2,1)} async-done(((bf16[256,1024]{1,0:T(8,128)(2,1)}), bf16[1024,1024]{1,0:T(8,128)(2,1)}) %all-gather.15.cloned.1.call-update) | async-done | bytes 2097168 | tf_op jit(solution)/shard_map/all_gather | solution.py:207
  473.7 4.4 fusion.162
  478.1 38.2 %all-gather.17.cloned.1.call-done = bf16[1024,512]{1,0:T(8,128)(2,1)} async-done(((bf16[128,512]{1,0:T(8,128)(2,1)}), bf16[1024,512]{1,0:T(8,128)(2,1)}) %all-gather.17.cloned.1.call-update) | async-done | bytes 1048592 | tf_op jit(solution)/shard_map/all_gather | solution.py:261
  516.3 4.5 fusion.161
  520.8 35.8 %all-gather.21.cloned.1.call-done = bf16[512,1024]{1,0:T(8,128)(2,1)} async-done(((bf16[512,128]{1,0:T(8,128)(2,1)}), bf16[512,1024]{1,0:T(8,128)(2,1)}) %all-gather.21.cloned.1.call-update) | async-done | bytes 1048592 | tf_op jit(solution)/shard_map/all_gather | solution.py:263
  556.6 23.7 %all-gather.23.cloned.1.call-done = bf16[1024,1024]{1,0:T(8,128)(2,1)} async-done(((bf16[256,1024]{1,0:T(8,128)(2,1)}), bf16[1024,1024]{1,0:T(8,128)(2,1)}) %all-gather.23.cloned.1.call-update) | async-done | bytes 2097168 | tf_op jit(solution)/shard_map/all_gather | solution.py:207
  580.3 6.7 multiply_convert_fusion.1
  590.8 3.0 fusion.163
  596.5 25.8 %reduce-scatter.29.cloned.1.call-done = bf16[256,1024]{1,0:T(8,128)(2,1)} async-done(((bf16[1024,1024]{1,0:T(8,128)(2,1)}), bf16[256,1024]{1,0:T(8,128)(2,1)}) %reduce-scatter.29.cloned.1.call-update) | async-done | bytes 524304 | tf_op jit(solution)/shard_map/reduce_scatter | solution.py:211
  622.3 33.8 %reduce-scatter.31.cloned.1.call-done = bf16[256,1024]{1,0:T(8,128)(2,1)} async-done(((bf16[1024,1024]{1,0:T(8,128)(2,1)}), bf16[256,1024]{1,0:T(8,128)(2,1)}) %reduce-scatter.31.cloned.1.call-update) | async-done | bytes 524304 | tf_op jit(solution)/shard_map/reduce_scatter | solution.py:211
  656.1 3.2 fusion.75
  662.0 22.4 %all-gather.25.cloned.1.call-done = bf16[1024,1024]{1,0:T(8,128)(2,1)} async-done(((bf16[256,1024]{1,0:T(8,128)(2,1)}), bf16[1024,1024]{1,0:T(8,128)(2,1)}) %all-gather.25.cloned.1.call-update) | async-done | bytes 2097168 | tf_op jit(solution)/shard_map/all_gather | solution.py:207
  684.4 4.7 multiply_reduce_fusion.7
  689.2 6.0 psum.50
  695.2 4.8 fusion.46
  705.3 3.8 copy.164
  710.4 4.0 fusion.40
  714.4 5.1 fusion.97
  720.7 35.1 %fusion.11 = (f32[6,1024]{1,0:T(8,128)S(1)}, f32[6,1024]{1,0:T(8,128)}, f32[1024,1024]{1,0:T(8,128)S(1)}) fusion(f32[1024,1024]{1,0:T(8,128)} %fusion.97, f32[6,1024]{1,0:T(8,128)S(1)} %bitcast.292, pred[1024,1024]{1,0:T(8,128)(4,1)S(1)} %copy-done.49, f32[6,64,1024]{2,1,0:T(8,128)S(1)} %bitcast.248, f32[1024,6,64]{0,2,1:T(8,128)S(1)} %bitcast.261, ...), kind=kOutput, calls=%fused_computation.13 | convolution fusion | flops 4900376576 | bytes 12681216 | tf_op jit(solution)/shard_map/transpose(jvp())/while/body/eval_jaxpr/checkpoint/hij,jhp->ihp/dot_general | solution.py:130
  755.9 3.2 fusion.99
  759.1 5.3 fusion.102
  764.4 26.2 %fusion.42 = (f32[1024,6,64]{0,2,1:T(8,128)}, f32[1024,6]{0,1:T(8,128)}) fusion(f32[1024,6,64]{0,2,1:T(8,128)S(1)} %bitcast.249, f32[6]{0:T(128)S(1)} %copy-done.123, f32[1024,6]{0,1:T(8,128)} %get-tuple-element.357, f32[1024,6,64]{0,2,1:T(8,128)} %bitcast.262, f32[6,64,1024]{2,1,0:T(8,128)S(1)} %bitcast.250, f32[1024,1024]{1,0:T(8,128)} %fusion.97, ...), kind=kOutput, calls=%fused_computation.85 | convolution fusion | flops 4858963968 | bytes 11608088 | tf_op jit(solution)/shard_map/transpose(jvp())/while/body/eval_jaxpr/checkpoint/hij,jhp->ihp/dot_general | solution.py:130
  790.6 3.4 multiply_reduce_fusion.5
  800.5 4.8 fusion.88
  816.6 3.2 fusion.164
  819.9 7.4 reduce-window.40
  835.9 3.2 convolution_convert_fusion.1
  840.6 3.9 convolution_convert_fusion.2
  844.5 4.4 convolution_convert_fusion.3
  857.9 4.0 convolution_convert_fusion.4
  866.6 3.3 convolution_convert_fusion.5
  872.6 3.6 fusion.104
  876.3 58.9 %reduce-scatter.55.cloned.1.call-done = bf16[128,512]{1,0:T(8,128)(2,1)} async-done(((bf16[1024,512]{1,0:T(8,128)(2,1)}), bf16[128,512]{1,0:T(8,128)(2,1)}) %reduce-scatter.55.cloned.1.call-update) | async-done | bytes 131088
  937.0 64.6 %reduce-scatter.45.cloned.1.call-done = bf16[128,512]{1,0:T(8,128)(2,1)} async-done(((bf16[1024,512]{1,0:T(8,128)(2,1)}), bf16[128,512]{1,0:T(8,128)(2,1)}) %reduce-scatter.45.cloned.1.call-update) | async-done | bytes 131088 | tf_op jit(solution)/shard_map/reduce_scatter | solution.py:400
  1003.2 64.9 %reduce-scatter.43.cloned.1.call-done = bf16[128,512]{1,0:T(8,128)(2,1)} async-done(((bf16[1024,512]{1,0:T(8,128)(2,1)}), bf16[128,512]{1,0:T(8,128)(2,1)}) %reduce-scatter.43.cloned.1.call-update) | async-done | bytes 131088 | tf_op jit(solution)/shard_map/reduce_scatter | solution.py:397
  1069.7 3.2 stack.35
  1074.4 41.4 %all-reduce.25 = (f32[4,1792]{1,0:T(4,128)S(1)}, f32[1792]{0:T(1024)S(1)}, f32[1536]{0:T(1024)S(1)}, f32[24]{0:T(128)}, f32[24]{0:T(128)}, /*index=5*/f32[24]{0:T(128)}, f32[5]{0:T(128)S(1)}, f32[]{:T(128)}) all-reduce(f32[4,1792]{1,0:T(4,128)S(1)} %pad_maximum_fusion.10, ...), channel_id=7, replica_groups=mesh['dp'=8,'tensor'=4] {'dp','tensor'}, use_global_device_ids=true, to_apply=%region_32.33.clone | all-reduce | flops 10574 | bytes 84592
  1118.8 13.3 reduce-scatter.49.cloned.1.call-done
  1133.5 62.6 %reduce-scatter.53.cloned.1.call-done = bf16[128,128]{1,0:T(8,128)(2,1)} async-done(((bf16[1024,128]{1,0:T(8,128)(2,1)}), bf16[128,128]{1,0:T(8,128)(2,1)}) %reduce-scatter.53.cloned.1.call-update) | async-done | bytes 32784
  1197.7 62.5 %reduce-scatter.41.cloned.1.call-done = bf16[128,128]{1,0:T(8,128)(2,1)} async-done(((bf16[1024,128]{1,0:T(8,128)(2,1)}), bf16[128,128]{1,0:T(8,128)(2,1)}) %reduce-scatter.41.cloned.1.call-update) | async-done | bytes 32784 | tf_op jit(solution)/shard_map/reduce_scatter | solution.py:510
  1261.5 63.9 %reduce-scatter.51.cloned.1.call-done = bf16[128,384]{1,0:T(8,128)(2,1)} async-done(((bf16[1024,384]{1,0:T(8,128)(2,1)}), bf16[128,384]{1,0:T(8,128)(2,1)}) %reduce-scatter.51.cloned.1.call-update) | async-done | bytes 98320
  1327.1 63.2 %reduce-scatter.37.cloned.1.call-done = bf16[128,384]{1,0:T(8,128)(2,1)} async-done(((bf16[1024,384]{1,0:T(8,128)(2,1)}), bf16[128,384]{1,0:T(8,128)(2,1)}) %reduce-scatter.37.cloned.1.call-update) | async-done | bytes 98320 | tf_op jit(solution)/shard_map/reduce_scatter | solution.py:492
  1391.9 63.7 %reduce-scatter.39.cloned.1.call-done = bf16[128,384]{1,0:T(8,128)(2,1)} async-done(((bf16[1024,384]{1,0:T(8,128)(2,1)}), bf16[128,384]{1,0:T(8,128)(2,1)}) %reduce-scatter.39.cloned.1.call-update) | async-done | bytes 98320 | tf_op jit(solution)/shard_map/reduce_scatter | solution.py:498
  1459.0 131.6 %reduce-scatter.47.cloned.1.call-done = f32[32,2]{1,0:T(8,128)} async-done(((f32[1024,2]{1,0:T(8,128)}), f32[32,2]{1,0:T(8,128)}) %reduce-scatter.47.cloned.1.call-update) | async-done | bytes 272
  1592.0 134.1 %reduce-scatter.35.cloned.1.call-done = f32[32,512]{1,0:T(8,128)} async-done(((f32[1024,512]{1,0:T(8,128)}), f32[32,512]{1,0:T(8,128)}) %reduce-scatter.35.cloned.1.call-update) | async-done | bytes 65552 | tf_op jit(solution)/shard_map/reduce_scatter | solution.py:550
  (473 shorter events, 132.8 us)
Async XLA Ops:
  8.0 319.5 %all-gather.13.cloned.1.call-start = ((), (), s32[]{:S(2)}) async-start(), calls=%async_computation.16 | async-start | bytes 1081344 | tf_op jit(solution)/shard_map/all_gather | solution.py:250
  8.8 318.8 %all-gather.11.cloned.1.call-start = ((), (), s32[]{:S(2)}) async-start(), calls=%async_computation.15 | async-start | bytes 2621440 | tf_op jit(solution)/shard_map/all_gather | solution.py:207
  53.3 89.5 %copy-start.116 = (bf16[128,6]{0,1:T(8,128)(2,1)S(1)}, bf16[128,6]{0,1:T(8,128)(2,1)}, u32[]{:S(2)}) copy-start(bf16[128,6]{0,1:T(8,128)(2,1)} %param.37) | copy-start | bytes 4612
  53.4 116.8 %copy-start.120 = (f32[24]{0:T(128)S(1)}, f32[24]{0:T(128)}, u32[]{:S(2)}) copy-start(f32[24]{0:T(128)} %param.33) | copy-start | bytes 292
  53.4 118.6 %copy-start.78 = (bf16[128,128]{1,0:T(8,128)(2,1)S(1)}, bf16[128,128]{1,0:T(8,128)(2,1)}, u32[]{:S(2)}) copy-start(bf16[128,128]{1,0:T(8,128)(2,1)} %param.38) | copy-start | bytes 98308
  53.9 43.5 %copy-start.69 = (f32[1,1024]{1,0:T(1,128)}, f32[1,1024]{1,0:T(1,128)S(1)}, u32[]{:S(2)}) copy-start(f32[1,1024]{1,0:T(1,128)S(1)} %get-tuple-element.360) | copy-start | bytes 12292
  53.9 148.8 %copy-start.79 = (bf16[128,128]{1,0:T(8,128)(2,1)S(1)}, bf16[128,128]{1,0:T(8,128)(2,1)}, u32[]{:S(2)}) copy-start(bf16[128,128]{1,0:T(8,128)(2,1)} %param.40) | copy-start | bytes 98308
  53.9 175.6 %copy-start.111 = (s32[1024]{0:T(1024)S(1)}, s32[1024]{0:T(1024)}, u32[]{:S(2)}) copy-start(s32[1024]{0:T(1024)} %param.26) | copy-start | bytes 12292
  53.9 175.6 %copy-start.56 = (s32[1024]{0:T(1024)S(1)}, s32[1024]{0:T(1024)}, u32[]{:S(2)}) copy-start(s32[1024]{0:T(1024)} %param.24) | copy-start | bytes 12292
  56.1 175.3 %copy-start.66 = (bf16[128,384]{1,0:T(8,128)(2,1)S(1)}, bf16[128,384]{1,0:T(8,128)(2,1)}, u32[]{:S(2)}) copy-start(bf16[128,384]{1,0:T(8,128)(2,1)} %param.35) | copy-start | bytes 294916
  56.2 382.8 %reduce-scatter.27.cloned.1.call-start = ((), (), s32[]{:S(2)}) async-start(), calls=%async_computation.17 | async-start | bytes 2621440 | tf_op jit(solution)/shard_map/reduce_scatter | solution.py:211
  97.4 166.5 %copy-start.67 = (bf16[128,384]{1,0:T(8,128)(2,1)S(1)}, bf16[128,384]{1,0:T(8,128)(2,1)}, u32[]{:S(2)}) copy-start(bf16[128,384]{1,0:T(8,128)(2,1)} %param.36) | copy-start | bytes 294916
  138.2 33.7 %copy-start.73 = (f32[4,256]{1,0:T(4,128)}, f32[4,256]{1,0:T(4,128)S(1)}, u32[]{:S(2)}) copy-start(f32[4,256]{1,0:T(4,128)S(1)} %slice.277) | copy-start | bytes 12292
  139.6 187.9 %copy-start.23 = (pred[1024,1024]{0,1:T(8,128)(4,1)}, pred[1024,1024]{0,1:T(8,128)(4,1)S(1)}, u32[]{:S(2)}) copy-start(pred[1024,1024]{0,1:T(8,128)(4,1)S(1)} %fusion.28) | copy-start | bytes 3145732
  139.6 158.7 %copy-start.68 = (bf16[384,128]{1,0:T(8,128)(2,1)S(1)}, bf16[384,128]{1,0:T(8,128)(2,1)}, u32[]{:S(2)}) copy-start(bf16[384,128]{1,0:T(8,128)(2,1)} %param.39) | copy-start | bytes 294916
  202.7 154.3 %copy-start.31 = (bf16[1024,128]{1,0:T(8,128)(2,1)}, bf16[1024,128]{1,0:T(8,128)(2,1)S(1)}, u32[]{:S(2)}) copy-start(bf16[1024,128]{1,0:T(8,128)(2,1)S(1)} %all_gather.64) | copy-start | bytes 786436
  229.6 176.1 %copy-start.28 = (bf16[128,1024]{1,0:T(8,128)(2,1)}, bf16[128,1024]{1,0:T(8,128)(2,1)S(1)}, u32[]{:S(2)}) copy-start(bf16[128,1024]{1,0:T(8,128)(2,1)S(1)} %all_gather.65) | copy-start | bytes 786436
  231.4 126.5 %copy-start.39 = (f32[1024,32]{0,1:T(8,128)}, f32[1024,32]{0,1:T(8,128)S(1)}, u32[]{:S(2)}) copy-start(f32[1024,32]{0,1:T(8,128)S(1)} %get-tuple-element.361) | copy-start | bytes 393220
  263.9 123.5 %copy-start.24 = (bf16[1024,384]{1,0:T(8,128)(2,1)}, bf16[1024,384]{1,0:T(8,128)(2,1)S(1)}, u32[]{:S(2)}) copy-start(bf16[1024,384]{1,0:T(8,128)(2,1)S(1)} %all_gather.61) | copy-start | bytes 2359300
  359.3 38.1 %copy-start.54 = (bf16[1024,2,64]{0,1,2:T(2,128)(2,1)}, bf16[1024,2,64]{0,1,2:T(2,128)(2,1)S(1)}, u32[]{:S(2)}) copy-start(bf16[1024,2,64]{0,1,2:T(2,128)(2,1)S(1)} %fusion.65) | copy-start | bytes 786436
  407.3 31.7 %copy-start.7 = (bf16[256,1024]{1,0:T(8,128)(2,1)S(1)}, bf16[256,1024]{1,0:T(8,128)(2,1)}, u32[]{:S(2)}) copy-start(bf16[256,1024]{1,0:T(8,128)(2,1)} %param.22) | copy-start | bytes 1572868
  410.2 33.5 %copy-start.112 = (s32[256]{0:T(256)S(1)}, s32[256]{0:T(256)}, u32[]{:S(2)}) copy-start(s32[256]{0:T(256)} %param.25) | copy-start | bytes 3076
  410.2 33.6 %copy-start.18 = (bf16[256,1024]{1,0:T(8,128)(2,1)S(1)}, bf16[256,1024]{1,0:T(8,128)(2,1)}, u32[]{:S(2)}) copy-start(bf16[256,1024]{1,0:T(8,128)(2,1)} %param.23) | copy-start | bytes 1572868
  410.2 40.4 %all-gather.19.cloned.1.call-start = ((), (), s32[]{:S(2)}) async-start(), calls=%async_computation.20 | async-start | bytes 1179648 | tf_op jit(solution)/shard_map/all_gather | solution.py:262
  410.8 62.9 %all-gather.15.cloned.1.call-start = ((), (), s32[]{:S(2)}) async-start(), calls=%async_computation.18 | async-start | bytes 2621440 | tf_op jit(solution)/shard_map/all_gather | solution.py:207
  442.3 73.9 %all-gather.17.cloned.1.call-start = ((), (), s32[]{:S(2)}) async-start(), calls=%async_computation.19 | async-start | bytes 1179648 | tf_op jit(solution)/shard_map/all_gather | solution.py:261
  442.9 113.7 %all-gather.21.cloned.1.call-start = ((), (), s32[]{:S(2)}) async-start(), calls=%async_computation.21 | async-start | bytes 1179648 | tf_op jit(solution)/shard_map/all_gather | solution.py:263
  443.7 136.7 %all-gather.23.cloned.1.call-start = ((), (), s32[]{:S(2)}) async-start(), calls=%async_computation.23 | async-start | bytes 2621440 | tf_op jit(solution)/shard_map/all_gather | solution.py:207
  443.7 216.8 %copy-start.96 = (f32[256]{0:T(256)}, f32[256]{0:T(256)S(1)}, u32[]{:S(2)}) copy-start(f32[256]{0:T(256)S(1)} %convert_element_type.247) | copy-start | bytes 3076
  444.7 177.5 %reduce-scatter.29.cloned.1.call-start = ((), (), s32[]{:S(2)}) async-start(), calls=%async_computation.22 | async-start | bytes 2621440 | tf_op jit(solution)/shard_map/reduce_scatter | solution.py:211
  590.7 65.4 %reduce-scatter.31.cloned.1.call-start = ((), (), s32[]{:S(2)}) async-start(), calls=%async_computation.24 | async-start | bytes 2621440 | tf_op jit(solution)/shard_map/reduce_scatter | solution.py:211
  593.7 62.4 %copy-start.10 = (bf16[256,1024]{1,0:T(8,128)(2,1)S(1)}, bf16[256,1024]{1,0:T(8,128)(2,1)}, u32[]{:S(2)}) copy-start(bf16[256,1024]{1,0:T(8,128)(2,1)} %reduce-scatter.27.cloned.1.call-done) | copy-start | bytes 1572868
  596.4 62.9 %copy-start.106 = (f32[256]{0:T(256)S(1)}, f32[256]{0:T(256)}, u32[]{:S(2)}) copy-start(f32[256]{0:T(256)} %copy-done.105) | copy-start | bytes 3076
  596.4 65.5 %copy-start.74 = (f32[4,256]{1,0:T(4,128)S(1)}, f32[4,256]{1,0:T(4,128)}, u32[]{:S(2)}) copy-start(f32[4,256]{1,0:T(4,128)} %copy-done.73) | copy-start | bytes 12292
  596.4 65.5 %copy-start.85 = (f32[2,1024]{1,0:T(2,128)S(1)}, f32[2,1024]{1,0:T(2,128)}, u32[]{:S(2)}) copy-start(f32[2,1024]{1,0:T(2,128)} %copy-done.84) | copy-start | bytes 24580
  596.4 88.0 %copy-start.72 = (f32[1024]{0:T(1024)S(1)}, f32[1024]{0:T(1024)}, u32[]{:S(2)}) copy-start(f32[1024]{0:T(1024)} %copy-done.71) | copy-start | bytes 12292
  596.4 88.0 %all-gather.25.cloned.1.call-start = ((), (), s32[]{:S(2)}) async-start(), calls=%async_computation.25 | async-start | bytes 2621440 | tf_op jit(solution)/shard_map/all_gather | solution.py:207
  659.3 29.9 %copy-start.101 = (f32[256]{0:T(256)}, f32[256]{0:T(256)S(1)}, u32[]{:S(2)}) copy-start(f32[256]{0:T(256)S(1)} %broadcast_multiply_fusion.5) | copy-start | bytes 3076
  660.6 28.6 %copy-start.103 = (f32[256]{0:T(256)}, f32[256]{0:T(256)S(1)}, u32[]{:S(2)}) copy-start(f32[256]{0:T(256)S(1)} %get-tuple-element.371) | copy-start | bytes 3076
  661.9 208.1 %reduce-scatter.33.cloned.1.call-start = ((), (), s32[]{:S(2)}) async-start(), calls=%async_computation.26 | async-start | bytes 2621440 | tf_op jit(solution)/shard_map/reduce_scatter | solution.py:211
  662.0 33.2 %copy-start.88 = (f32[1024]{0:T(1024)S(1)}, f32[1024]{0:T(1024)}, u32[]{:S(2)}) copy-start(f32[1024]{0:T(1024)} %get-tuple-element.366) | copy-start | bytes 12292
  720.4 35.5 %copy-start.38 = (f32[1024,384]{0,1:T(8,128)}, f32[1024,384]{0,1:T(8,128)S(1)}, u32[]{:S(2)}) copy-start(f32[1024,384]{0,1:T(8,128)S(1)} %get-tuple-element.336) | copy-start | bytes 4718596
  835.9 99.3 %reduce-scatter.55.cloned.1.call-start = ((), (), s32[]{:S(2)}) async-start(), calls=%async_computation.37 | async-start | bytes 1179648
  840.5 161.0 %reduce-scatter.45.cloned.1.call-start = ((), (), s32[]{:S(2)}) async-start(), calls=%async_computation.32 | async-start | bytes 1179648 | tf_op jit(solution)/shard_map/reduce_scatter | solution.py:400
  844.5 223.6 %reduce-scatter.43.cloned.1.call-start = ((), (), s32[]{:S(2)}) async-start(), calls=%async_computation.31 | async-start | bytes 1179648 | tf_op jit(solution)/shard_map/reduce_scatter | solution.py:397
  849.0 283.1 %reduce-scatter.49.cloned.1.call-start = ((), (), s32[]{:S(2)}) async-start(), calls=%async_computation.34 | async-start | bytes 294912
  850.4 345.8 %reduce-scatter.53.cloned.1.call-start = ((), (), s32[]{:S(2)}) async-start(), calls=%async_computation.36 | async-start | bytes 294912
  855.3 404.8 %reduce-scatter.41.cloned.1.call-start = ((), (), s32[]{:S(2)}) async-start(), calls=%async_computation.30 | async-start | bytes 294912 | tf_op jit(solution)/shard_map/reduce_scatter | solution.py:510
  857.8 467.6 %reduce-scatter.51.cloned.1.call-start = ((), (), s32[]{:S(2)}) async-start(), calls=%async_computation.35 | async-start | bytes 884736
  864.2 526.1 %reduce-scatter.37.cloned.1.call-start = ((), (), s32[]{:S(2)}) async-start(), calls=%async_computation.28 | async-start | bytes 884736 | tf_op jit(solution)/shard_map/reduce_scatter | solution.py:492
  866.5 589.1 %reduce-scatter.39.cloned.1.call-start = ((), (), s32[]{:S(2)}) async-start(), calls=%async_computation.29 | async-start | bytes 884736 | tf_op jit(solution)/shard_map/reduce_scatter | solution.py:498
  869.9 720.7 %reduce-scatter.47.cloned.1.call-start = ((), (), s32[]{:S(2)}) async-start(), calls=%async_computation.33 | async-start | bytes 540672
  872.6 853.5 %reduce-scatter.35.cloned.1.call-start = ((), (), s32[]{:S(2)}) async-start(), calls=%async_computation.27 | async-start | bytes 2162688 | tf_op jit(solution)/shard_map/reduce_scatter | solution.py:550
  876.2 196.7 %copy-start.109 = (f32[384]{0:T(512)S(1)}, f32[384]{0:T(512)}, u32[]{:S(2)}) copy-start(f32[384]{0:T(512)} %get-tuple-element.335) | copy-start | bytes 4612
  876.2 196.8 %copy-start.117 = (f32[384]{0:T(512)S(1)}, f32[384]{0:T(512)}, u32[]{:S(2)}) copy-start(f32[384]{0:T(512)} %get-tuple-element.281) | copy-start | bytes 4612
  876.2 198.0 %copy-start.119 = (f32[6]{0:T(128)S(1)}, f32[6]{0:T(128)}, u32[]{:S(2)}) copy-start(f32[6]{0:T(128)} %get-tuple-element.272) | copy-start | bytes 76
  876.2 581.0 %copy-start.11 = (bf16[256,1024]{1,0:T(8,128)(2,1)S(1)}, bf16[256,1024]{1,0:T(8,128)(2,1)}, u32[]{:S(2)}) copy-start(bf16[256,1024]{1,0:T(8,128)(2,1)} %reduce-scatter.27.cloned.1.call-done) | copy-start | bytes 1572868
  876.2 581.0 %copy-start.19 = (bf16[256,1024]{1,0:T(8,128)(2,1)S(1)}, bf16[256,1024]{1,0:T(8,128)(2,1)}, u32[]{:S(2)}) copy-start(bf16[256,1024]{1,0:T(8,128)(2,1)} %param.23) | copy-start | bytes 1572868
  876.3 581.0 %copy-start.21 = (bf16[256,1024]{1,0:T(8,128)(2,1)S(1)}, bf16[256,1024]{1,0:T(8,128)(2,1)}, u32[]{:S(2)}) copy-start(bf16[256,1024]{1,0:T(8,128)(2,1)} %reduce-scatter.31.cloned.1.call-done) | copy-start | bytes 1572868
  876.3 581.0 %copy-start.36 = (bf16[256,1024]{1,0:T(8,128)(2,1)S(1)}, bf16[256,1024]{1,0:T(8,128)(2,1)}, u32[]{:S(2)}) copy-start(bf16[256,1024]{1,0:T(8,128)(2,1)} %reduce-scatter.33.cloned.1.call-done) | copy-start | bytes 1572868
  876.3 581.0 %copy-start.97 = (f32[256]{0:T(256)S(1)}, f32[256]{0:T(256)}, u32[]{:S(2)}) copy-start(f32[256]{0:T(256)} %copy-done.96) | copy-start | bytes 3076
  876.3 581.0 %copy-start.102 = (f32[256]{0:T(256)S(1)}, f32[256]{0:T(256)}, u32[]{:S(2)}) copy-start(f32[256]{0:T(256)} %copy-done.101) | copy-start | bytes 3076
  876.3 581.0 %copy-start.104 = (f32[256]{0:T(256)S(1)}, f32[256]{0:T(256)}, u32[]{:S(2)}) copy-start(f32[256]{0:T(256)} %copy-done.103) | copy-start | bytes 3076
  876.3 581.0 %copy-start.110 = (f32[256]{0:T(256)S(1)}, f32[256]{0:T(256)}, u32[]{:S(2)}) copy-start(f32[256]{0:T(256)} %get-tuple-element.372) | copy-start | bytes 3076
  (89 other events, 313.4 us)
Sparse Core Ops, SparseCore 0:
  11.7 56.3 all-gather.12
  70.2 21.6 all-gather.10
  410.3 28.6 reduce-scatter.26
  590.8 31.4 reduce-scatter.28
  624.6 31.4 reduce-scatter.30
Sparse Core Ops, SparseCore 1:
  413.0 37.5 all-gather.18
  452.7 20.9 all-gather.14
  475.9 40.4 all-gather.16
  518.6 38.0 all-gather.20
  558.9 21.4 all-gather.22
  662.0 22.4 all-gather.24
  836.0 32.3 reduce-scatter.32
  871.6 63.5 reduce-scatter.54
  938.9 62.6 reduce-scatter.44
  1005.5 62.5 reduce-scatter.42
  1071.6 60.4 reduce-scatter.48
  1135.8 60.3 reduce-scatter.52
  1199.7 60.4 reduce-scatter.40
  1263.8 61.5 reduce-scatter.50
  1328.7 61.5 reduce-scatter.36
  1394.0 61.6 reduce-scatter.38
  1457.9 132.7 reduce-scatter.46
  1593.6 132.5 reduce-scatter.34
where the time goes:
time: 1740 us; the launch traced here: 1730 us
  waiting for transfers between devices  1020 us (59%)
  blocking collectives  354 us (20%)
  matrix products  208 us (12%)
  other arithmetic  81.7 us (5%)
  local copies, waits for them, and re-layouts  47.5 us (3%)
  between operations  18 us (1%)
    unnamed x28, waiting for transfers between devices  333 us
    reduce_scatter x1, waiting for transfers between devices, local(): lax.psum_scatter(product_tn(first_full, shared_grad), ('dp', 'tensor'), s...  134 us
    dot_general x3, matrix products, mamba_sequence(): mixing = jnp.einsum('hij,jhp->ihp', decay_mat, driven, precision=HIGH)  88.9 us
    reduce_scatter x4, waiting for transfers between devices, seq_reduce(): lax.psum_scatter(values.astype(jnp.bfloat16), 'tensor', scatter_dimension...  87.8 us
    unnamed x2, blocking collectives  78.3 us
    all_gather x4, waiting for transfers between devices, seq_gather(): return lax.all_gather(values, 'tensor', axis=0, tiled=True)  69.2 us
    reduce_scatter x1, waiting for transfers between devices, local(): lax.psum_scatter(gate_w_grad.astype(jnp.bfloat16), 'dp', scatter_dimensio...  64.9 us
    reduce_scatter x1, waiting for transfers between devices, local(): lax.psum_scatter(up_w_grad.astype(jnp.bfloat16), 'dp', scatter_dimension=...  64.6 us
  transfers between devices with their start and end apart: 23, of which 20 were waited for; matrix products, arithmetic and copies ran while one was open for 6% of the time, Pallas kernels for 0%

commit v1 on v0

v1 whole, which is shorter than its diff:
```python
import functools
import math

import jax
import jax.numpy as jnp
from jax import lax
from jax.experimental import pallas as pl
from jax.experimental.pallas import tpu as pltpu
from jax.sharding import PartitionSpec as P

D = 1024
MH = 24
HEAD_SIZE = 64
MAMBA_STATES = 128
CONV = 4
QUERY_HEADS = 8
KEY_VALUE_HEADS = 2
SEQUENCE_TOKENS = 1024
DSSM = 1536


EPS = 1e-05
ROPE_BASE = 100000000000.0
NEG_FILL = -1e30
HIGH = lax.Precision.HIGHEST


def rms_scale(values):
    return lax.rsqrt(jnp.mean(values * values, axis=-1, keepdims=True) + EPS)


def norm_back(values, row_scale, gain_row, grad_in):
    scaled_grad = grad_in * gain_row
    gain_grad = jnp.sum(grad_in * values * row_scale, axis=0)
    value_grad = row_scale * scaled_grad - values * (row_scale * row_scale * row_scale) * jnp.mean(
        scaled_grad * values, axis=-1, keepdims=True
    )
    return (value_grad, gain_grad)


def product(left, right):
    return jnp.dot(left, right, preferred_element_type=jnp.float32)


def product_tn(left, right):
    return lax.dot_general(
        left, right, (((0,), (0,)), ((), ())), preferred_element_type=jnp.float32
    )


def product_nt(left, right):
    return lax.dot_general(
        left, right, (((1,), (1,)), ((), ())), preferred_element_type=jnp.float32
    )


def split_dot(values, selector, dims):
    high = values.astype(jnp.bfloat16)
    low = (values - high.astype(jnp.float32)).astype(jnp.bfloat16)
    left = lax.dot_general(high, selector, dims, preferred_element_type=jnp.float32)
    return left + lax.dot_general(low, selector, dims, preferred_element_type=jnp.float32)


NN = (((1,), (0,)), ((), ()))
NT = (((1,), (1,)), ((), ()))
TN = (((0,), (0,)), ((), ()))


def mxu(left, right, dims):
    return lax.dot_general(
        left.astype(jnp.bfloat16),
        right.astype(jnp.bfloat16),
        dims,
        preferred_element_type=jnp.float32,
    )


def iota(shape, dim):
    return lax.broadcasted_iota(jnp.int32, shape, dim)


def head_groups(width):
    return [(low, min(low + 2 * HEAD_SIZE, width)) for low in range(0, width, 2 * HEAD_SIZE)]


def chunk_common(chunk, start, width, x_ref, bc_ref, raw_ref, doc_ref, pad_ref, w_ref, par_ref):
    rows = pl.ds(start, chunk)
    doc = doc_ref[rows, :]
    age = start + iota((chunk, 1), 0) - doc
    span = pad_ref[pl.ds(start, chunk + 8), :]
    conv = w_ref[CONV : CONV + 1, :] + w_ref[CONV - 1 : CONV, :] * span[8:, :]
    lagged = [span[8:, :]]
    for lag in range(1, CONV):
        moved = jnp.where(age >= lag, span[8 - lag : 8 - lag + chunk, :], 0.0)
        lagged.append(moved)
        conv = conv + w_ref[CONV - 1 - lag : CONV - lag, :] * moved
    sig = jax.nn.sigmoid(conv)
    act = conv * sig
    raw = raw_ref[rows, :] + par_ref[0:1, :]
    step = jnp.maximum(raw, 0.0) + jnp.log1p(jnp.exp(-jnp.abs(raw)))
    rate = step * par_ref[1:2, :]
    lower = (iota((chunk, chunk), 0) >= iota((chunk, chunk), 1)).astype(jnp.bfloat16)
    high = rate.astype(jnp.bfloat16)
    low = (rate - high.astype(jnp.float32)).astype(jnp.bfloat16)
    total = mxu(lower, high, NN) + mxu(lower, low, NN)
    lanes = par_ref.shape[1]
    spread = (iota((lanes, width), 0) == iota((lanes, width), 1) // HEAD_SIZE).astype(jnp.bfloat16)
    key_pos = start + iota((chunk, chunk), 1)
    allowed = (key_pos <= start + iota((chunk, chunk), 0)) & (key_pos >= doc)
    doc_last = doc[chunk - 1 : chunk, :]
    ends = total[chunk - 1 : chunk, :]
    live = jnp.where(doc < start, jnp.exp(total), 0.0)
    keep = jnp.where(start + iota((chunk, 1), 0) >= doc_last, jnp.exp(ends - total), 0.0)
    carry = jnp.where(doc_last < start, jnp.exp(ends), 0.0)
    wide = split_dot(jnp.concatenate([step, live, keep, jnp.broadcast_to(carry, (8, lanes))], axis=0), spread, NN)
    return dict(
        conv=conv, sig=sig, act=act, raw=raw, step=step, total=total, turned=total.T, spread=spread, allowed=allowed,
        carry=carry, age=age, lagged=lagged, lower=lower,
        step_w=wide[:chunk], live_w=wide[chunk : 2 * chunk], keep_w=wide[2 * chunk : 3 * chunk],
        carry_w=wide[3 * chunk : 3 * chunk + 1],
    )


def decay_of(part, head):
    gap = part["total"][:, head : head + 1] - part["turned"][head : head + 1, :]
    return jnp.where(part["allowed"], jnp.exp(gap), 0.0)


def only(values, low, high):
    lane = iota(values.shape, 1)
    return jnp.where((lane >= low) & (lane < high), values, jnp.zeros_like(values))


def mamba_forward_kernel(
    chunk, width, x_ref, bc_ref, raw_ref, z_ref, doc_ref, w_ref, par_ref, skip_ref, y_ref, square_ref, kept_ref, pad_ref, state_ref
):
    length = x_ref.shape[0]
    pad_ref[0:8, :] = jnp.zeros((8, pad_ref.shape[1]), jnp.float32)
    pad_ref[8:, :width] = x_ref[:, :width]
    pad_ref[8:, width:] = bc_ref[...]
    state_ref[...] = jnp.zeros_like(state_ref)

    def one_chunk(index, _):
        start = pl.multiple_of(index * chunk, chunk)
        rows = pl.ds(start, chunk)
        part = chunk_common(chunk, start, width, x_ref, bc_ref, raw_ref, doc_ref, pad_ref, w_ref, par_ref)
        inner = part["act"][:, :width]
        bm = part["act"][:, width : width + MAMBA_STATES].astype(jnp.bfloat16)
        cm = part["act"][:, width + MAMBA_STATES :].astype(jnp.bfloat16)
        driven = (inner * part["step_w"]).astype(jnp.bfloat16)
        pair = mxu(cm, bm, NT)
        pieces = []
        for low, high in head_groups(width):
            heads = range(low // HEAD_SIZE, high // HEAD_SIZE)
            mats = [(decay_of(part, head) * pair).astype(jnp.bfloat16) for head in heads]
            piece = driven[:, low:high]
            right = [
                only(piece, HEAD_SIZE * k, HEAD_SIZE * (k + 1)) if len(mats) > 1 else piece
                for k in range(len(mats))
            ]
            pieces.append(
                mxu(jnp.concatenate(mats, axis=1), jnp.concatenate(right, axis=0), NN)
            )
        state = state_ref[...]
        kept_ref[pl.ds(pl.multiple_of(index * MAMBA_STATES, MAMBA_STATES), MAMBA_STATES), :] = state
        y = jnp.concatenate(pieces, axis=1) + part["live_w"] * mxu(cm, state, NN)
        y = y + skip_ref[0:1, :] * inner
        state_ref[...] = state * part["carry_w"] + mxu(
            bm, driven.astype(jnp.float32) * part["keep_w"], TN
        )
        y_ref[rows, :] = y
        z = z_ref[rows, :width]
        gated = y * z * jax.nn.sigmoid(z)
        square_ref[:, rows] = split_dot_left(gated * gated)
        return 0

    lax.fori_loop(0, length // chunk, one_chunk, 0)


def split_dot_left(values):
    ones = jnp.ones((8, values.shape[1]), jnp.bfloat16)
    high = values.astype(jnp.bfloat16)
    low = (values - high.astype(jnp.float32)).astype(jnp.bfloat16)
    return mxu(ones, high, NT) + mxu(ones, low, NT)


def mamba_backward_kernel(
    chunk, width, x_ref, bc_ref, raw_ref, z_ref, doc_ref, w_ref, par_ref, skip_ref, gain_ref, y_ref, mixed_ref, rows_ref,
    dq_ref, dkv_ref, kept_ref, din_ref, dcommon_ref, dw_ref, dpar_ref, dskip_ref, pad_ref, state_ref, halo_ref
):
    length = x_ref.shape[0]
    count = length // chunk
    wide = x_ref.shape[1]
    if wide > width:
        din_ref[...] = jnp.zeros_like(din_ref)
    din_ref[:, 2 * wide : 2 * wide + 2 * HEAD_SIZE] = dq_ref[...]
    dcommon_ref[:, 2 * MAMBA_STATES :] = dkv_ref[...]
    pad_ref[0:8, :] = jnp.zeros((8, pad_ref.shape[1]), jnp.float32)
    pad_ref[8:, :width] = x_ref[:, :width]
    pad_ref[8:, width:] = bc_ref[...]
    state_ref[...] = jnp.zeros_like(state_ref)
    halo_ref[...] = jnp.zeros_like(halo_ref)

    @pl.when(pl.program_id(0) == 0)
    def _():
        dw_ref[...] = jnp.zeros_like(dw_ref)
        dpar_ref[...] = jnp.zeros_like(dpar_ref)
        dskip_ref[...] = jnp.zeros_like(dskip_ref)

    def one_chunk(step_index, _):
        index = count - 1 - step_index
        start = pl.multiple_of(index * chunk, chunk)
        rows = pl.ds(start, chunk)
        part = chunk_common(chunk, start, width, x_ref, bc_ref, raw_ref, doc_ref, pad_ref, w_ref, par_ref)
        inner = part["act"][:, :width]
        bm = part["act"][:, width : width + MAMBA_STATES].astype(jnp.bfloat16)
        cm = part["act"][:, width + MAMBA_STATES :].astype(jnp.bfloat16)
        driven = (inner * part["step_w"]).astype(jnp.bfloat16)
        driven_f = driven.astype(jnp.float32)
        y = y_ref[rows, :]
        z = z_ref[rows, :width]
        z_sig = jax.nn.sigmoid(z)
        silu_z = z * z_sig
        gated = y * silu_z
        scale = rows_ref[rows, 0:1]
        normed_grad = mixed_ref[rows, :width]
        dskip_ref[1:2, :] += jnp.sum(normed_grad * gated * scale, axis=0, keepdims=True)
        gated_grad = scale * (normed_grad * gain_ref[0:1, :]) - gated * rows_ref[rows, 1:2]
        dy = gated_grad * silu_z
        din_ref[rows, :width] = (gated_grad * y * z_sig * (1.0 + z * (1.0 - z_sig))).astype(jnp.bfloat16)
        dy_b = dy.astype(jnp.bfloat16)
        pair = mxu(cm, bm, NT)
        pair_grad = jnp.zeros((chunk, chunk), jnp.float32)
        pieces = []
        for low, high in head_groups(width):
            heads = list(range(low // HEAD_SIZE, high // HEAD_SIZE))
            piece = driven[:, low:high]
            grads = [
                only(dy_b[:, low:high], HEAD_SIZE * k, HEAD_SIZE * (k + 1)) if len(heads) > 1 else dy_b[:, low:high]
                for k in range(len(heads))
            ]
            mats = []
            for k, head in enumerate(heads):
                decay = decay_of(part, head)
                mats.append((decay * pair).astype(jnp.bfloat16))
                pair_grad = pair_grad + decay * mxu(grads[k], piece, NT)
            pieces.append(mxu(jnp.concatenate(mats, axis=0), jnp.concatenate(grads, axis=0), TN))
        within = jnp.concatenate(pieces, axis=1)
        state = kept_ref[pl.ds(pl.multiple_of(index * MAMBA_STATES, MAMBA_STATES), MAMBA_STATES), :]
        state_grad = state_ref[...]
        pair_grad = pair_grad.astype(jnp.bfloat16)
        dy_live = (dy * part["live_w"]).astype(jnp.bfloat16)
        driven_keep = (driven_f * part["keep_w"]).astype(jnp.bfloat16)
        later = part["keep_w"] * mxu(bm, state_grad, NN)
        c_grad = mxu(pair_grad, bm, NN) + mxu(dy_live, state, NT)
        b_grad = mxu(pair_grad, cm, TN) + mxu(driven_keep, state_grad, NT)
        state_ref[...] = state_grad * part["carry_w"] + mxu(cm, dy_live, TN)
        driven_grad = within + later
        later_part = driven_f * later
        mixed = y - skip_ref[0:1, :] * inner
        sums = split_dot(
            jnp.concatenate(
                [
                    dy_b.astype(jnp.float32) * mixed - driven_f * within - later_part,
                    driven_grad * inner,
                    jnp.broadcast_to(
                        jnp.sum(later_part, axis=0, keepdims=True)
                        + part["carry_w"] * jnp.sum(state_grad * state, axis=0, keepdims=True),
                        (8, width),
                    ),
                ],
                axis=0,
            ),
            part["spread"],
            NT,
        )
        high = sums[:chunk].astype(jnp.bfloat16)
        low = (sums[:chunk] - high.astype(jnp.float32)).astype(jnp.bfloat16)
        rate_grad = (
            mxu(part["lower"], high, TN) + mxu(part["lower"], low, TN) + sums[2 * chunk : 2 * chunk + 1]
        )
        step_grad = rate_grad * par_ref[1:2, :] + sums[chunk : 2 * chunk]
        raw_grad = step_grad * jax.nn.sigmoid(part["raw"])
        din_ref[rows, 2 * wide + 2 * HEAD_SIZE :] = raw_grad.astype(jnp.bfloat16)
        dpar_ref[0:1, :] += jnp.sum(raw_grad, axis=0, keepdims=True)
        dpar_ref[1:2, :] += par_ref[1:2, :] * jnp.sum(rate_grad * part["step"], axis=0, keepdims=True)
        dskip_ref[0:1, :] += jnp.sum(dy * inner, axis=0, keepdims=True)
        inner_grad = driven_grad * part["step_w"] + skip_ref[0:1, :] * dy
        sig, conv = (part["sig"], part["conv"])
        conv_grad = jnp.concatenate([inner_grad, b_grad, c_grad], axis=1) * (
            sig * (1.0 + conv * (1.0 - sig))
        )
        dw_ref[CONV : CONV + 1, :] += jnp.sum(conv_grad, axis=0, keepdims=True)
        v_grad = w_ref[CONV - 1 : CONV, :] * conv_grad
        long = jnp.concatenate([conv_grad, halo_ref[...]], axis=0)
        next_start = jnp.minimum(start + chunk, length - 8)
        ages = jnp.concatenate([part["age"], start + chunk + iota((8, 1), 0) - doc_ref[pl.ds(pl.multiple_of(next_start, 8), 8), :]], axis=0)
        dw_ref[CONV - 1 : CONV, :] += jnp.sum(conv_grad * part["lagged"][0], axis=0, keepdims=True)
        for lag in range(1, CONV):
            dw_ref[CONV - 1 - lag : CONV - lag, :] += jnp.sum(
                conv_grad * part["lagged"][lag], axis=0, keepdims=True
            )
            masked = jnp.where(ages >= lag, long, 0.0)
            v_grad = v_grad + w_ref[CONV - 1 - lag : CONV - lag, :] * masked[lag : lag + chunk, :]
        halo_ref[...] = conv_grad[:8, :]
        din_ref[rows, wide : wide + width] = v_grad[:, :width].astype(jnp.bfloat16)
        dcommon_ref[rows, : 2 * MAMBA_STATES] = v_grad[:, width:].astype(jnp.bfloat16)
        return 0

    lax.fori_loop(0, count, one_chunk, 0)


CHUNK = 128
VMEM_LIMIT = 60 * 1024 * 1024


def columns_of(width, place=0):
    return pl.BlockSpec((SEQUENCE_TOKENS, width), lambda i: (i, place))


def whole_spec(shape):
    return pl.BlockSpec(shape, lambda i: (0,) * len(shape))


def mamba_forward(in_act, common, doc, taps, params, skip_row, chunk=CHUNK):
    tokens = in_act.shape[0]
    width = skip_row.shape[1]
    lanes = params.shape[1]
    wide = (in_act.shape[1] - 2 * lanes) // 2
    seq = SEQUENCE_TOKENS
    count = tokens // seq
    kept = seq // chunk * MAMBA_STATES
    return pl.pallas_call(
        functools.partial(mamba_forward_kernel, chunk, width),
        grid=(count,),
        in_specs=[
            columns_of(wide, 1),
            columns_of(2 * MAMBA_STATES),
            columns_of(lanes, 2 * wide // lanes + 1),
            columns_of(wide),
            columns_of(1),
            whole_spec(taps.shape),
            whole_spec(params.shape),
            whole_spec(skip_row.shape),
        ],
        out_specs=[
            columns_of(width),
            pl.BlockSpec((8, seq), lambda i: (0, i)),
            pl.BlockSpec((kept, width), lambda i: (i, 0)),
        ],
        out_shape=[
            jax.ShapeDtypeStruct((tokens, width), jnp.float32),
            jax.ShapeDtypeStruct((8, tokens), jnp.float32),
            jax.ShapeDtypeStruct((count * kept, width), jnp.float32),
        ],
        scratch_shapes=[
            pltpu.VMEM((seq + 8, width + 2 * MAMBA_STATES), jnp.float32),
            pltpu.VMEM((MAMBA_STATES, width), jnp.float32),
        ],
        compiler_params=pltpu.CompilerParams(vmem_limit_bytes=VMEM_LIMIT),
        cost_estimate=pl.CostEstimate(
            flops=tokens * width * 20000, bytes_accessed=tokens * width * 20, transcendentals=0
        ),
    )(in_act, common, in_act, in_act, doc, taps, params, skip_row)


def mamba_backward(
    in_act, common, doc, taps, params, skip_row, y, mixed_grad, rows_of, gain_row, dq, dkv, kept_states, chunk=CHUNK
):
    tokens = in_act.shape[0]
    width = skip_row.shape[1]
    lanes = params.shape[1]
    wide = (in_act.shape[1] - 2 * lanes) // 2
    seq = SEQUENCE_TOKENS
    count = tokens // seq
    kept = seq // chunk * MAMBA_STATES
    conv_width = width + 2 * MAMBA_STATES
    return pl.pallas_call(
        functools.partial(mamba_backward_kernel, chunk, width),
        grid=(count,),
        in_specs=[
            columns_of(wide, 1),
            columns_of(2 * MAMBA_STATES),
            columns_of(lanes, 2 * wide // lanes + 1),
            columns_of(wide),
            columns_of(1),
            whole_spec(taps.shape),
            whole_spec(params.shape),
            whole_spec(skip_row.shape),
            whole_spec(gain_row.shape),
            columns_of(width),
            columns_of(mixed_grad.shape[1]),
            columns_of(rows_of.shape[1]),
            columns_of(dq.shape[1]),
            columns_of(dkv.shape[1]),
            pl.BlockSpec((kept, width), lambda i: (i, 0)),
        ],
        out_specs=[
            columns_of(in_act.shape[1]),
            columns_of(common.shape[1]),
            whole_spec((8, conv_width)),
            whole_spec((8, lanes)),
            whole_spec((8, width)),
        ],
        out_shape=[
            jax.ShapeDtypeStruct(in_act.shape, jnp.bfloat16),
            jax.ShapeDtypeStruct(common.shape, jnp.bfloat16),
            jax.ShapeDtypeStruct((8, conv_width), jnp.float32),
            jax.ShapeDtypeStruct((8, lanes), jnp.float32),
            jax.ShapeDtypeStruct((8, width), jnp.float32),
        ],
        scratch_shapes=[
            pltpu.VMEM((seq + 8, conv_width), jnp.float32),
            pltpu.VMEM((MAMBA_STATES, width), jnp.float32),
            pltpu.VMEM((8, conv_width), jnp.float32),
        ],
        compiler_params=pltpu.CompilerParams(vmem_limit_bytes=VMEM_LIMIT),
        cost_estimate=pl.CostEstimate(
            flops=tokens * width * 60000, bytes_accessed=tokens * width * 20, transcendentals=0
        ),
    )(
        in_act, common, in_act, in_act, doc, taps, params, skip_row, gain_row, y, mixed_grad, rows_of, dq, dkv, kept_states
    )


NEGATIVE = -1e30
QUERY_BLOCK = 256


def swap_halves(values):
    half = HEAD_SIZE // 2
    lane = iota(values.shape, 1)
    width = values.shape[1]
    return jnp.where(
        lane % HEAD_SIZE < half,
        pltpu.roll(values, width - half, 1),
        pltpu.roll(values, half, 1),
    )


def attention_mask(start, rows, keys, doc):
    position = start + iota((rows, 1), 0)
    key_pos = iota((rows, keys), 1)
    return (key_pos <= position) & (key_pos >= doc)


def both_heads(values):
    return jnp.concatenate(
        [only(values, 0, HEAD_SIZE), only(values, HEAD_SIZE, 2 * HEAD_SIZE)], axis=0
    )


def chosen(values, kv):
    lane = iota(values.shape, 1)
    turned = pltpu.roll(values, HEAD_SIZE, 1)
    return jnp.where((lane < HEAD_SIZE) == (kv == 0), values, turned)


def attention_forward_kernel(
    kv_ref, q_ref, key_ref, value_ref, cos_ref, sin_ref, doc_ref, out_ref, qr_ref, kr_ref, vr_ref, log_ref
):
    length = q_ref.shape[0]
    kv = kv_ref[0]
    cos, sin = (cos_ref[...], sin_ref[...])
    query = q_ref[...]
    qr_ref[...] = ((query * cos + swap_halves(query) * sin).astype(jnp.bfloat16).astype(jnp.float32) * HEAD_SIZE**-0.5).astype(jnp.bfloat16)
    key = key_ref[...]
    kr_ref[...] = chosen(key * cos + swap_halves(key) * sin, kv).astype(jnp.bfloat16)
    vr_ref[...] = chosen(value_ref[...], kv).astype(jnp.bfloat16)
    rows = QUERY_BLOCK
    for start in range(0, length, rows):
        keys = start + rows
        block = slice(start, start + rows)
        mask = attention_mask(start, rows, keys, doc_ref[block, :])
        scores = mxu(both_heads(qr_ref[block, :]), kr_ref[0:keys, :], NT)
        outs = []
        logs = []
        for head in range(2):
            part = jnp.where(mask, scores[head * rows : (head + 1) * rows], NEGATIVE)
            peak = jnp.max(part, axis=1, keepdims=True)
            weight = jnp.exp(part - peak)
            total = jnp.sum(weight, axis=1, keepdims=True)
            outs.append(mxu(weight * (1.0 / total), vr_ref[0:keys, :], NN))
            logs.append(peak + jnp.log(total))
        lane = iota((rows, 2 * HEAD_SIZE), 1)
        out_ref[block, :] = jnp.where(lane < HEAD_SIZE, outs[0], outs[1]).astype(jnp.bfloat16)
        log_ref[block, :] = jnp.where(lane < HEAD_SIZE, logs[0], logs[1])


def attention_backward_kernel(
    kv_ref, qr_ref, kr_ref, vr_ref, cos_ref, sin_ref, doc_ref, log_ref, grad_ref, dq_ref, dkv_ref, dk_ref, dv_ref
):
    length = qr_ref.shape[0]
    kv = kv_ref[0]
    rows = QUERY_BLOCK
    dk_ref[...] = jnp.zeros_like(dk_ref)
    dv_ref[...] = jnp.zeros_like(dv_ref)
    for start in range(0, length, rows):
        keys = start + rows
        block = slice(start, start + rows)
        mask = attention_mask(start, rows, keys, doc_ref[block, :])
        query = both_heads(qr_ref[block, :])
        grad = both_heads(grad_ref[block, :])
        logs = log_ref[block, :]
        scores = mxu(query, kr_ref[0:keys, :], NT)
        prob_grad = mxu(grad, vr_ref[0:keys, :], NT)
        probs = []
        score_grads = []
        for head in range(2):
            mine = slice(head * rows, (head + 1) * rows)
            log = logs[:, head * HEAD_SIZE : head * HEAD_SIZE + 1]
            weight = jnp.where(mask, jnp.exp(scores[mine] - log), 0.0)
            product_grad = weight * prob_grad[mine]
            total = jnp.sum(product_grad, axis=1, keepdims=True)
            probs.append(weight.astype(jnp.bfloat16))
            score_grads.append((product_grad - weight * total).astype(jnp.bfloat16))
        lane = iota((rows, 2 * HEAD_SIZE), 1)
        dq = mxu(jnp.concatenate(score_grads, axis=0), kr_ref[0:keys, :], NN)
        dq = jnp.where(lane < HEAD_SIZE, dq[:rows], dq[rows:]) * HEAD_SIZE**-0.5
        dq = dq * cos_ref[block, :] - swap_halves(dq) * sin_ref[block, :]
        dq_ref[block, :] = dq.astype(jnp.bfloat16)
        dk_ref[0:keys, :] += mxu(jnp.concatenate(score_grads, axis=0), query, TN)
        dv_ref[0:keys, :] += mxu(jnp.concatenate(probs, axis=0), grad, TN)
    lane = iota((length, 2 * HEAD_SIZE), 1)
    mine = (lane < HEAD_SIZE) == (kv == 0)
    dk = dk_ref[...]
    dk = dk + pltpu.roll(dk, HEAD_SIZE, 1)
    dk = dk * cos_ref[...] - swap_halves(dk) * sin_ref[...]
    dv = dv_ref[...]
    dv = dv + pltpu.roll(dv, HEAD_SIZE, 1)
    dkv_ref[:, : 2 * HEAD_SIZE] = jnp.where(mine, dk, 0.0).astype(jnp.bfloat16)
    dkv_ref[:, 2 * HEAD_SIZE :] = jnp.where(mine, dv, 0.0).astype(jnp.bfloat16)


def attention_call(kernel, kv, tokens, ins, places, outs, scratch, flops):
    seq = SEQUENCE_TOKENS
    return pl.pallas_call(
        kernel,
        grid_spec=pltpu.PrefetchScalarGridSpec(
            num_scalar_prefetch=1,
            grid=(tokens // seq,),
            in_specs=[
                pl.BlockSpec((seq, columns), functools.partial(lambda place, i, kv: (i, place), place))
                for columns, place in places
            ],
            out_specs=[pl.BlockSpec((seq, columns), lambda i, kv: (i, 0)) for columns, _ in outs],
            scratch_shapes=scratch,
        ),
        out_shape=[jax.ShapeDtypeStruct((tokens, columns), kind) for columns, kind in outs],
        compiler_params=pltpu.CompilerParams(vmem_limit_bytes=VMEM_LIMIT),
        cost_estimate=pl.CostEstimate(flops=flops * tokens, bytes_accessed=tokens * 4096, transcendentals=0),
    )(kv, *ins)


def attention_forward(kv, in_act, common, cos, sin, doc):
    two = 2 * HEAD_SIZE
    low, full = (jnp.bfloat16, jnp.float32)
    return attention_call(
        attention_forward_kernel,
        kv,
        in_act.shape[0],
        (in_act, common, common, cos, sin, doc),
        (
            (two, in_act.shape[1] // two - 2),
            (two, 2 * MAMBA_STATES // two),
            (two, 2 * MAMBA_STATES // two + 1),
            (two, 0),
            (two, 0),
            (1, 0),
        ),
        ((two, low), (two, low), (two, low), (two, low), (two, full)),
        [],
        4000000,
    )


def attention_backward(kv, qr, kr, vr, cos, sin, doc, log, grad):
    two = 2 * HEAD_SIZE
    seq = SEQUENCE_TOKENS
    ins = (qr, kr, vr, cos, sin, doc, log, grad)
    return attention_call(
        attention_backward_kernel,
        kv,
        qr.shape[0],
        ins,
        [(a.shape[1], 0) for a in ins],
        ((two, jnp.bfloat16), (2 * two, jnp.bfloat16)),
        [pltpu.VMEM((seq, two), jnp.float32), pltpu.VMEM((seq, two), jnp.float32)],
        9000000,
    )


def rope_rows(position):
    lane = jnp.arange(2 * HEAD_SIZE, dtype=jnp.int32)
    half = HEAD_SIZE // 2
    inverse = jnp.exp(
        (lane % half).astype(jnp.float32) * (-2.0 * math.log(ROPE_BASE) / HEAD_SIZE)
    )
    angles = position.astype(jnp.float32)[:, None] * inverse[None, :]
    sign = jnp.where(lane % HEAD_SIZE < half, -1.0, 1.0)
    return (jnp.cos(angles), jnp.sin(angles) * sign[None, :])
def grid_of(count):
    rows = 1
    while 8 * rows * rows <= count:
        rows *= 2
    return (count // rows, rows)


def ring_cycle(count):
    depth, rows = grid_of(count)
    order = []
    for level in range(depth):
        inner = list(range(1, rows))
        if level % 2:
            inner.reverse()
        order += [level * rows + row for row in inner]
    return order + [level * rows for level in reversed(range(depth))]


class Ring:
    def __init__(self, count):
        self.count = count
        self.order = ring_cycle(count)
        place = [0] * count
        for spot, device in enumerate(self.order):
            place[device] = spot
        self.spot = jnp.asarray(place, jnp.int32)[lax.axis_index("dp")]
        self.table = jnp.asarray(self.order + self.order, jnp.int32)

    def device_at(self, offset):
        return self.table[(self.spot + offset + self.count) % self.count]

    def send(self, block, step):
        count, order = (self.count, self.order)
        return lax.ppermute(
            block, "dp", [(order[k], order[(k + step) % count]) for k in range(count)]
        )


def ring_gather(ring, block):
    count = ring.count
    rows = block.shape[0]
    half = rows // 2
    out = jnp.zeros((count * rows,) + block.shape[1:], block.dtype)

    def put(out, piece, offset, extra=0):
        return lax.dynamic_update_slice_in_dim(
            out, piece, ring.device_at(offset) * rows + extra, 0
        )

    out = put(out, block, 0)
    ahead = behind = block
    for step in range(1, count // 2):
        ahead = ring.send(ahead, 1)
        behind = ring.send(behind, -1)
        out = put(out, ahead, -step)
        out = put(out, behind, step)
    out = put(out, ring.send(ahead[:half], 1), -(count // 2))
    return put(out, ring.send(behind[half:], -1), count // 2, half)


def ring_scatter(ring, values):
    count = ring.count
    rows = values.shape[0] // count
    half = rows // 2

    def piece(offset, start=0, size=rows):
        return lax.dynamic_slice_in_dim(
            values, ring.device_at(offset) * rows + start, size, 0
        ).astype(jnp.float32)

    far = count // 2
    ahead = ring.send(piece(far, 0, half).astype(jnp.bfloat16), 1).astype(jnp.float32)
    behind = ring.send(piece(far, half, rows - half).astype(jnp.bfloat16), -1).astype(jnp.float32)
    ahead = jnp.concatenate([ahead, jnp.zeros_like(behind)], axis=0)
    behind = jnp.concatenate([jnp.zeros_like(ahead[:half]), behind], axis=0)
    for offset in range(far - 1, 0, -1):
        ahead = ring.send((ahead + piece(offset)).astype(jnp.bfloat16), 1).astype(jnp.float32)
        behind = ring.send((behind + piece(-offset)).astype(jnp.bfloat16), -1).astype(jnp.float32)
    return ahead + behind + piece(0)


def core_swap(block):
    count = lax.axis_size("tensor")
    return lax.ppermute(block, "tensor", [(k, k ^ 1) for k in range(count)])


def chip_shift(block, step):
    count = lax.axis_size("tensor")
    return lax.ppermute(block, "tensor", [(k, (k + 2 * step) % count) for k in range(count)])


def tensor_stack(block):
    count = lax.axis_size("tensor")
    mine = lax.axis_index("tensor")
    out = jnp.zeros((count,) + block.shape, block.dtype)
    put = lax.dynamic_update_index_in_dim
    out = put(out, block, mine, 0)
    others = [(chip_shift(block, step), (mine + count - 2 * step) % count) for step in range(1, count // 2)]
    out = put(out, core_swap(block), mine ^ 1, 0)
    for other, source in others:
        out = put(out, other, source, 0)
        out = put(out, core_swap(other), source ^ 1, 0)
    return out


def seq_gather(values):
    return tensor_stack(values).reshape((-1,) + values.shape[1:])


def tensor_scatter(pick, dtype):
    count = lax.axis_size("tensor")
    mine = lax.axis_index("tensor")
    received = []
    for step in range(1, count // 2):
        target = (mine + 2 * step) % count
        from_mate = core_swap(pick(target ^ 1).astype(dtype)).astype(jnp.float32)
        merged = (pick(target).astype(jnp.float32) + from_mate).astype(dtype)
        received.append(chip_shift(merged, step).astype(jnp.float32))
    total = pick(mine).astype(jnp.float32) + core_swap(pick(mine ^ 1).astype(dtype)).astype(jnp.float32)
    for other in received:
        total = total + other
    return total


def seq_reduce(values):
    rows = values.shape[0] // lax.axis_size("tensor")
    lowered = values.astype(jnp.bfloat16)
    return tensor_scatter(
        lambda index: lax.dynamic_slice_in_dim(lowered, index * rows, rows, 0), jnp.bfloat16
    )


def width_total(values):
    return jnp.sum(tensor_stack(values), axis=0)


def dp_exchange(pieces):
    count = lax.axis_size("dp")
    mine = lax.axis_index("dp")
    out = jnp.zeros_like(pieces)
    for step in range(count):
        piece = lax.dynamic_index_in_dim(pieces, (mine + step) % count, 0, False)
        if step:
            piece = lax.ppermute(piece, "dp", [(k, (k + step) % count) for k in range(count)])
        out = lax.dynamic_update_index_in_dim(out, piece, (mine + count - step) % count, 0)
    return out


def dp_stack(block):
    count = lax.axis_size("dp")
    mine = lax.axis_index("dp")
    out = jnp.zeros((count,) + block.shape, block.dtype)
    for step in range(count):
        piece = block
        if step:
            piece = lax.ppermute(block, "dp", [(k, (k + step) % count) for k in range(count)])
        out = lax.dynamic_update_index_in_dim(out, piece, (mine + count - step) % count, 0)
    return out


def after(value, *others):
    return lax.optimization_barrier((value,) + others)[0]


def local(
    layer_input,
    out_grad,
    segment_ids,
    valid_mask,
    doc_start,
    norm_gains,
    conv_weight,
    conv_bias,
    mixer_gain,
    shared_proj,
    step_bias,
    decay_log,
    skip_gain,
    mamba_gate,
    mamba_input,
    mamba_step,
    query_proj,
    mamba_out,
    attention_out,
    swiglu_gate,
    swiglu_up,
    swiglu_down,
):
    tensor_position = lax.axis_index("tensor")
    dp_count = lax.axis_size("dp")
    tensor_count = lax.axis_size("tensor")
    ring = Ring(dp_count)
    local_width = mamba_gate.shape[1]
    query_width = query_proj.shape[1]
    head_local = mamba_step.shape[1]
    hidden_width = swiglu_gate.shape[1]
    slab = 2 * HEAD_SIZE
    wide = -(-local_width // slab) * slab
    in_width = 2 * wide + slab

    def padded(values, columns):
        return jnp.pad(values, ((0, 0), (0, columns - values.shape[1])))

    x_full = seq_gather(layer_input)
    small = jnp.concatenate(
        [norm_gains.reshape(-1), conv_weight.reshape(-1), conv_bias, mixer_gain]
    )
    small = jnp.pad(small, (0, shared_proj.shape[1] - small.shape[0]))
    common = dp_stack(jnp.concatenate([shared_proj, small[None]], axis=0))
    common = tensor_stack(common)
    common = jnp.swapaxes(common, 0, 1)
    shared_w = common[:, :, :-1].reshape(-1, shared_proj.shape[1])
    small_all = common[:, :, -1].reshape(dp_count * tensor_count, -1)
    w_in = ring_gather(
        ring,
        jnp.concatenate(
            [
                padded(mamba_gate, wide),
                padded(mamba_input, wide),
                padded(query_proj, slab),
                padded(mamba_step, slab),
            ],
            axis=1,
        ),
    )
    w_out = ring_gather(
        ring, after(jnp.concatenate([mamba_out.T, attention_out.T], axis=1), w_in)
    )
    w_ffn = lax.all_gather(
        after(jnp.concatenate([swiglu_gate, swiglu_up, swiglu_down.T], axis=1), w_in),
        "dp",
        axis=0,
        tiled=True,
    )
    ffn_gate_up_w = w_ffn[:, : 2 * hidden_width]
    ffn_down_w = w_ffn[:, 2 * hidden_width :]
    cuts = []
    spot = 0
    for piece in (norm_gains, conv_weight, conv_bias, mixer_gain):
        size = piece.size
        cuts.append(small_all[:, spot : spot + size])
        spot += size
    gains_all = jnp.swapaxes(cuts[0].reshape(-1, 2, norm_gains.shape[1]), 0, 1).reshape(2, -1)
    conv_all = jnp.swapaxes(cuts[1].reshape(-1, CONV, conv_weight.shape[1]), 0, 1).reshape(CONV, -1)
    shift_all = cuts[2].reshape(-1)
    mixer_gain_all = cuts[3].reshape(-1)
    tokens_f = layer_input.astype(jnp.float32)
    gains_f = gains_all.astype(jnp.float32)
    scale_one = rms_scale(tokens_f)
    x_wide = x_full.astype(jnp.float32)
    first_full = (x_wide * rms_scale(x_wide) * gains_f[0]).astype(jnp.bfloat16)
    tokens_per_group = first_full.shape[0]
    seq_count = tokens_per_group // SEQUENCE_TOKENS
    query_slice = query_width // HEAD_SIZE
    channel_start = tensor_position * local_width
    head_start = tensor_position * head_local
    in_act = product(first_full, w_in)
    common_input = product(first_full, shared_w)
    conv_f = conv_all.astype(jnp.float32)
    shift_f = shift_all.astype(jnp.float32)
    own_conv = jnp.concatenate(
        [lax.dynamic_slice_in_dim(conv_f, channel_start, local_width, 1), conv_f[:, DSSM:]], axis=1
    )
    own_shift = jnp.concatenate(
        [lax.dynamic_slice_in_dim(shift_f, channel_start, local_width, 0), shift_f[DSSM:]], axis=0
    )
    own_bias = lax.dynamic_slice_in_dim(step_bias, head_start, head_local, 0)
    own_decay = lax.dynamic_slice_in_dim(decay_log, head_start, head_local, 0)
    own_skip = lax.dynamic_slice_in_dim(skip_gain, head_start, head_local, 0)
    own_gain = lax.dynamic_slice_in_dim(
        mixer_gain_all.astype(jnp.float32), channel_start, local_width, 0
    )
    doc = doc_start[:, None]
    taps = jnp.concatenate(
        [own_conv, own_shift[None], jnp.zeros((3, own_conv.shape[1]), jnp.float32)], axis=0
    )
    params = jnp.pad(
        jnp.stack([own_bias, -jnp.exp(own_decay)], axis=0), ((0, 6), (0, slab - head_local))
    )
    skip_row = jnp.broadcast_to(jnp.repeat(own_skip, HEAD_SIZE)[None], (8, local_width))
    gain_row = jnp.broadcast_to(own_gain[None], (8, local_width))
    position = jnp.tile(jnp.arange(SEQUENCE_TOKENS, dtype=jnp.int32), seq_count) - doc_start
    cosine_table, sine_table = rope_rows(position)
    kv = (tensor_position * query_slice // (QUERY_HEADS // KEY_VALUE_HEADS)).astype(jnp.int32)[None]
    mamba_y, square_rows, kept_states = mamba_forward(in_act, common_input, doc, taps, params, skip_row)
    attended, query_rot, key_rot, value_low, log_total = attention_forward(
        kv, in_act, common_input, cosine_table, sine_table, doc
    )
    square_sum = width_total(square_rows[0])
    gate_scale = lax.rsqrt(square_sum / DSSM + EPS)[:, None]
    gate_z = in_act[:, :local_width]
    gated_y = mamba_y * jax.nn.silu(gate_z)
    normed_b = (gated_y * gate_scale * own_gain).astype(jnp.bfloat16)
    attended_flat = attended[:, :query_width]
    mixed_b = jnp.concatenate([normed_b, attended_flat], axis=1)
    mixer_sum = seq_reduce(product_nt(mixed_b, w_out))
    middle = tokens_f + mixer_sum
    scale_two = rms_scale(middle)
    second_b = (middle * scale_two * gains_f[1]).astype(jnp.bfloat16)
    ffn_in = seq_gather(second_b)
    ffn_act = product(ffn_in, ffn_gate_up_w)
    gate_act = ffn_act[:, :hidden_width]
    up_act = ffn_act[:, hidden_width:]
    hidden_b = (jax.nn.silu(gate_act) * up_act).astype(jnp.bfloat16)
    ffn_part = product_nt(hidden_b, ffn_down_w)
    ffn_out = seq_reduce(ffn_part)
    result = middle + ffn_out
    valid_f = valid_mask.astype(jnp.float32)
    out_cot = out_grad.astype(jnp.float32) * valid_f[:, None]
    cot_b = out_cot.astype(jnp.bfloat16)
    ffn_grad_in = seq_gather(after(cot_b, w_in))
    hidden_grad = product(ffn_grad_in, ffn_down_w)
    sigmoid_gate = jax.nn.sigmoid(gate_act)
    gate_up_grad = jnp.concatenate(
        [
            hidden_grad * up_act * sigmoid_gate * (1.0 + gate_act * (1.0 - sigmoid_gate)),
            hidden_grad * jax.nn.silu(gate_act),
        ],
        axis=1,
    ).astype(jnp.bfloat16)
    second_grad = seq_reduce(product_nt(gate_up_grad, ffn_gate_up_w))
    ffn_w_grad = jnp.concatenate(
        [product_tn(ffn_in, gate_up_grad), product_tn(ffn_grad_in, hidden_b)], axis=1
    ).astype(jnp.bfloat16)
    ffn_w_grad = lax.psum_scatter(
        after(ffn_w_grad, second_grad), "dp", scatter_dimension=0, tiled=True
    ).astype(jnp.float32)
    gate_w_grad = ffn_w_grad[:, :hidden_width]
    up_w_grad = ffn_w_grad[:, hidden_width : 2 * hidden_width]
    down_w_grad = ffn_w_grad[:, 2 * hidden_width :].T
    second_value_grad, gain_two_grad = norm_back(middle, scale_two, gains_f[1], second_grad)
    middle_grad = out_cot + second_value_grad
    mixer_grad_full = seq_gather(middle_grad.astype(jnp.bfloat16))
    out_w_grad = product_tn(mixer_grad_full, mixed_b).astype(jnp.bfloat16)
    mixed_grad = product(mixer_grad_full, w_out)
    normed_grad = mixed_grad[:, :local_width]
    attended_grad = padded(mixed_grad[:, local_width:].astype(jnp.bfloat16), slab)
    inner_sum = width_total(jnp.sum(normed_grad * own_gain * gated_y, axis=1))
    dq, dkv = attention_backward(
        kv, query_rot, key_rot, value_low, cosine_table, sine_table, doc, log_total, attended_grad
    )
    row_terms = jnp.concatenate(
        [gate_scale, gate_scale * gate_scale * gate_scale * (inner_sum / DSSM)[:, None]], axis=1
    )
    in_grad, shared_grad, taps_grad, params_grad, rows_grad = mamba_backward(
        in_act, common_input, doc, taps, params, skip_row, mamba_y, mixed_grad, row_terms, gain_row, dq, dkv, kept_states
    )
    conv_grad = taps_grad[:CONV]
    shift_grad = taps_grad[CONV]
    bias_grad = params_grad[0, :head_local]
    decay_grad = params_grad[1, :head_local]
    skip_grad = jnp.sum(rows_grad[0].reshape(head_local, HEAD_SIZE), axis=1)
    own_gain_grad = rows_grad[1]
    first_part = product_nt(in_grad, w_in) + product_nt(shared_grad, shared_w)
    gain_one_grad = jnp.sum(first_part * x_wide * rms_scale(x_wide), axis=0)
    first_grad = seq_reduce(first_part)
    first_value_grad, _ = norm_back(tokens_f, scale_one, gains_f[0], first_grad)
    input_grad = middle_grad + first_value_grad
    out_w_grad = ring_scatter(ring, out_w_grad)
    mamba_out_grad = out_w_grad[:, :local_width].T
    attend_out_grad = out_w_grad[:, local_width:].T
    in_w_grad = ring_scatter(ring, product_tn(first_full, in_grad).astype(jnp.bfloat16))
    gate_proj_grad = in_w_grad[:, :local_width]
    input_proj_grad = in_w_grad[:, wide : wide + local_width]
    query_proj_grad = in_w_grad[:, 2 * wide : 2 * wide + query_width]
    step_proj_grad = in_w_grad[:, in_width : in_width + head_local]
    shared_w_grad = product_tn(first_full, shared_grad).reshape(
        dp_count, tensor_count, -1, shared_proj.shape[1]
    ).astype(jnp.bfloat16)
    shared_w_grad = tensor_scatter(
        lambda index: lax.dynamic_index_in_dim(shared_w_grad, index, 1, False), jnp.bfloat16
    )
    shared_proj_grad = jnp.sum(
        dp_exchange(shared_w_grad.astype(jnp.bfloat16)).astype(jnp.float32), axis=0
    )
    zero_row = jnp.zeros((DSSM,), jnp.float32)
    conv_rows = jnp.concatenate([conv_grad, shift_grad[None]], axis=0)
    conv_rows = jnp.concatenate(
        [
            lax.dynamic_update_slice_in_dim(
                jnp.zeros((CONV + 1, DSSM), jnp.float32), conv_rows[:, :local_width], channel_start, 1
            ),
            conv_rows[:, local_width:],
        ],
        axis=1,
    )
    gain_row = lax.dynamic_update_slice_in_dim(zero_row, own_gain_grad, channel_start, 0)
    gains_rows = jnp.stack([gain_one_grad, gain_two_grad], axis=0)
    device_count = dp_count * tensor_count

    def by_device(rows_in):
        return jnp.swapaxes(rows_in.reshape(rows_in.shape[0], device_count, -1), 0, 1).reshape(
            device_count, -1
        )

    scattered = jnp.concatenate(
        [by_device(gains_rows), by_device(conv_rows), by_device(gain_row[None])], axis=1
    ).reshape(dp_count, tensor_count, -1)
    scattered = tensor_scatter(
        lambda index: lax.dynamic_index_in_dim(scattered, index, 1, False), jnp.float32
    )
    bias_full = lax.dynamic_update_slice_in_dim(
        jnp.zeros((MH,), jnp.float32), bias_grad, head_start, 0
    )
    decay_full = lax.dynamic_update_slice_in_dim(
        jnp.zeros((MH,), jnp.float32), decay_grad, head_start, 0
    )
    skip_full = lax.dynamic_update_slice_in_dim(
        jnp.zeros((MH,), jnp.float32), skip_grad, head_start, 0
    )
    tracked = (tokens_f, mixer_sum, middle, ffn_out, result)
    stat_terms = jnp.stack(
        [jnp.sum(valid_f * jnp.sum(tracked_arr * tracked_arr, axis=1)) for tracked_arr in tracked]
    )
    everywhere = width_total(
        jnp.concatenate([stat_terms, jnp.sum(valid_f)[None], bias_full, decay_full, skip_full])
    )
    last = dp_exchange(
        jnp.concatenate(
            [
                scattered,
                jnp.broadcast_to(everywhere[None], (dp_count, everywhere.shape[0])),
            ],
            axis=1,
        )
    )
    last = jnp.sum(last, axis=0)
    gain_cols, conv_cols, mix_cols = (norm_gains.shape[1], conv_weight.shape[1], mixer_gain.shape[0])
    gains_grad = last[: 2 * gain_cols].reshape(2, gain_cols)
    spot = 2 * gain_cols
    conv_full_grad = last[spot : spot + CONV * conv_cols].reshape(CONV, conv_cols)
    spot += CONV * conv_cols
    shift_full_grad = last[spot : spot + conv_cols]
    spot += conv_cols
    gain_full_grad = last[spot : spot + mix_cols]
    spot += mix_cols
    stat_totals, count_all = (last[spot : spot + 5], last[spot + 5])
    bias_total = last[spot + 6 : spot + 6 + MH]
    decay_total = last[spot + 6 + MH : spot + 6 + 2 * MH]
    skip_total = last[spot + 6 + 2 * MH :]
    residual_rms = jnp.sqrt(stat_totals / (count_all * D))
    return (
        result.astype(jnp.bfloat16),
        input_grad,
        gains_grad,
        conv_full_grad,
        shift_full_grad,
        gain_full_grad,
        shared_proj_grad,
        bias_total,
        decay_total,
        skip_total,
        gate_proj_grad,
        input_proj_grad,
        step_proj_grad,
        query_proj_grad,
        mamba_out_grad,
        attend_out_grad,
        gate_w_grad,
        up_w_grad,
        down_w_grad,
        residual_rms,
    )


def solution(mesh):
    in_specs = (
        P(("dp", "tensor"), None),
        P(("dp", "tensor"), None),
        P("dp"),
        P(("dp", "tensor")),
        P("dp"),
        P(None, ("dp", "tensor")),
        P(None, ("dp", "tensor")),
        P(("dp", "tensor")),
        P(("dp", "tensor")),
        P(("dp", "tensor"), None),
        P(),
        P(),
        P(),
        P("dp", "tensor"),
        P("dp", "tensor"),
        P("dp", "tensor"),
        P("dp", "tensor"),
        P("tensor", "dp"),
        P("tensor", "dp"),
        P("dp", "tensor"),
        P("dp", "tensor"),
        P("tensor", "dp"),
    )
    out_specs = (
        P(("dp", "tensor"), None),
        P(("dp", "tensor"), None),
        P(None, ("dp", "tensor")),
        P(None, ("dp", "tensor")),
        P(("dp", "tensor")),
        P(("dp", "tensor")),
        P(("dp", "tensor"), None),
        P(),
        P(),
        P(),
        P("dp", "tensor"),
        P("dp", "tensor"),
        P("dp", "tensor"),
        P("dp", "tensor"),
        P("tensor", "dp"),
        P("tensor", "dp"),
        P("dp", "tensor"),
        P("dp", "tensor"),
        P("tensor", "dp"),
        P(),
    )
    return jax.shard_map(local, mesh=mesh, in_specs=in_specs, out_specs=out_specs, check_vma=False)
```

time: 1740 us -> 510 us (0.29)
  waiting for transfers between devices: 1020 us -> 129 us
  blocking collectives: 354 us -> 0 us
  matrix products: 208 us -> 44.3 us
  starting transfers between devices: 1.56 us -> 84.4 us
  local copies, waits for them, and re-layouts: 47.5 us -> 112 us
  Pallas kernels: 0 us -> 51.3 us
  other arithmetic: 81.7 us -> 52.6 us
    reduce_scatter x10 -> x0, waiting for transfers between devices: 541 us -> none  [the longest x1 134 us: local(): lax.psum_scatter(product_tn(first_full, shared_grad), ('dp', 'tensor'), s...]
    unnamed x28 -> x3, waiting for transfers between devices: 333 us -> 0.04 us
    all_gather x8 -> x0, blocking collectives: 264 us -> none  [the longest x1 43.2 us: local(): lax.all_gather(norm_gains, ('dp', 'tensor'), axis=1, tiled=True)]
    all_gather x8 -> x1, waiting for transfers between devices: 149 us -> 0.01 us  [local(): lax.all_gather(after(jnp.concatenate([swiglu_gate, swiglu_up, swiglu_down...]
    ppermute x0 -> x95, waiting for transfers between devices: none -> 129 us  [the longest x14 66 us: chip_shift(): lax.ppermute(block, 'tensor', [(k, (k + 2 * step) % count) for k in range...]
    dot_general x17 -> x0, matrix products: 122 us -> none  [the longest x3 88.9 us: mamba_sequence(): mixing = jnp.einsum('hij,jhp->ihp', decay_mat, driven, precision=HIGH)]
    ppermute x0 -> x95, starting transfers between devices: none -> 84.4 us  [the longest x32 38.3 us: send(): lax.ppermute(block, 'dp', [(order[k], order[(k + step) % count]) for k in...]
    unnamed x2 -> x0, blocking collectives: 78.3 us -> none
  transfers between devices with their start and end apart: 23 -> 97, of which waited for: 20 -> 33; matrix products, arithmetic and copies ran while one was open for 6% -> 34% of each run, Pallas kernels for 0% -> 10%
where the time goes in v1:
time: 510 us; the launch traced here: 502 us
  waiting for transfers between devices  129 us (25%)
  local copies, waits for them, and re-layouts  112 us (22%)
  starting transfers between devices  84.4 us (17%)
  other arithmetic  52.6 us (10%)
  Pallas kernels  51.3 us (10%)
  matrix products  44.3 us (9%)
  between operations  28.9 us (6%)
    ppermute x14, waiting for transfers between devices, chip_shift(): lax.ppermute(block, 'tensor', [(k, (k + 2 * step) % count) for k in range...  66 us
    ppermute x32, starting transfers between devices, send(): lax.ppermute(block, 'dp', [(order[k], order[(k + step) % count]) for k in...  38.3 us
    ppermute x32, waiting for transfers between devices, send(): lax.ppermute(block, 'dp', [(order[k], order[(k + step) % count]) for k in...  32.7 us
    ppermute x14, waiting for transfers between devices, dp_exchange(): lax.ppermute(piece, 'dp', [(k, (k + step) % count) for k in range(count)])  25.8 us
    pallas_call x1, Pallas kernels, mamba_backward(): pl.pallas_call(functools.partial(mamba_backward_kernel, chunk, width), gr...  22.4 us
    unnamed x154, local copies, waits for them, and re-layouts  22.2 us
    dot_general x5, matrix products, product(): return jnp.dot(left, right, preferred_element_type=jnp.float32)  18.4 us
    ppermute x14, starting transfers between devices, dp_exchange(): lax.ppermute(piece, 'dp', [(k, (k + step) % count) for k in range(count)])  17.2 us
  transfers between devices with their start and end apart: 97, of which 33 were waited for; matrix products, arithmetic and copies ran while one was open for 34% of the time, Pallas kernels for 10%

profile of v1, /device:TPU:0, one launch (start us, length us, event | category | flops | bytes accessed | tf_op | source)
XLA Modules:
  0.0 502.3 jit_solution(7427108118128630866)
XLA Ops:
  19.0 3.0 collective-permute-start.13
  22.3 2.0 collective-permute-start.3
  25.9 2.5 collective-permute-start.5
  29.3 3.1 fusion.24
  43.6 2.6 collective-permute-start.7
  51.0 2.1 collective-permute-done.9
  60.9 2.9 collective-permute-done.11
  63.8 1.7 collective-permute-done.15
  69.0 5.6 %collective-permute-done.1 = bf16[256,1024]{1,0:T(8,128)(2,1)} collective-permute-done((bf16[256,1024]{1,0:T(8,128)(2,1)S(1)}, bf16[256,1024]{1,0:T(8,128)(2,1)}, u32[]{:S(2)}, u32[]{:S(2)}) %collective-permute-start.1) | collective-permute-done | bytes 524320 | tf_op jit(solution)/shard_map/ppermute | solution.py:690
  121.3 4.4 fusion.52.x_ref.raw_ref.z_ref.q_ref
  125.7 2.6 fusion.53.bc_ref.key_ref.value_ref
  128.9 13.2 %shard_map.374 = (f32[1024,384]{1,0:T(8,128)}, f32[8,1024]{1,0:T(8,128)}, f32[1024,384]{1,0:T(8,128)}) custom-call(f32[1024,1024]{1,0:T(8,128)} %fusion.52.x_ref.raw_ref.z_ref.q_ref, f32[1024,512]{1,0:T(8,128)} %fusion.53.bc_ref.key_ref.value_ref, f32[1024,1024]{1,0:T(8,128)} %fusion.52.x_ref.raw_ref.z_ref.q_ref, ...), custom_call_target="tpu_custom_call" | custom-call | flops 7864320000 | bytes 7864320 | tf_op jit(solution)/shard_map/pallas_call | solution.py:333
  146.4 7.5 %shard_map.375 = (bf16[1024,128]{1,0:T(8,128)(2,1)}, bf16[1024,128]{1,0:T(8,128)(2,1)}, bf16[1024,128]{1,0:T(8,128)(2,1)}, bf16[1024,128]{1,0:T(8,128)(2,1)}, f32[1024,128]{1,0:T(8,128)}) custom-call(s32[1]{0:T(128)} %bitcast.50.kv_ref, f32[1024,1024]{1,0:T(8,128)} %fusion.52.x_ref.raw_ref.z_ref.q_ref, f32[1024,512]{1,0:T(8,128)} %fusion.53.bc_ref.key_ref.value_ref, ...), custom_call_target="tpu_custom_call" | custom-call | flops 4096000000 | bytes 4194304 | tf_op jit(solution)/shard_map/pallas_call | solution.py:537
  154.3 3.4 multiply_convert_fusion.3
  159.8 7.0 %collective-permute-done.28 = bf16[128,512]{0,1:T(8,128)(2,1)S(1)} collective-permute-done((bf16[128,512]{0,1:T(8,128)(2,1)S(1)}, bf16[128,512]{0,1:T(8,128)(2,1)S(1)}, u32[]{:S(2)}, u32[]{:S(2)}) %collective-permute-start.28) | collective-permute-done | bytes 131104 | tf_op jit(solution)/shard_map/ppermute | solution.py:635
  169.2 8.5 %collective-permute-done.30 = bf16[64,512]{0,1:T(8,128)(2,1)S(1)} collective-permute-done((bf16[64,512]{0,1:T(8,128)(2,1)S(1)}, bf16[64,512]{0,1:T(8,128)(2,1)S(1)}, u32[]{:S(2)}, u32[]{:S(2)}) %collective-permute-start.30) | collective-permute-done | bytes 65568 | tf_op jit(solution)/shard_map/ppermute | solution.py:635
  180.3 2.5 convolution_convert_fusion.4
  190.1 11.4 %collective-permute-done.42 = bf16[256,1024]{1,0:T(8,128)(2,1)} collective-permute-done((bf16[256,1024]{1,0:T(8,128)(2,1)}, bf16[256,1024]{1,0:T(8,128)(2,1)}, u32[]{:S(2)}, u32[]{:S(2)}) %collective-permute-start.42) | collective-permute-done | bytes 524320 | tf_op jit(solution)/shard_map/ppermute | solution.py:690
  201.5 10.6 %collective-permute-done.34 = bf16[256,1024]{1,0:T(8,128)(2,1)} collective-permute-done((bf16[256,1024]{1,0:T(8,128)(2,1)S(1)}, bf16[256,1024]{1,0:T(8,128)(2,1)}, u32[]{:S(2)}, u32[]{:S(2)}) %collective-permute-start.34) | collective-permute-done | bytes 524320 | tf_op jit(solution)/shard_map/ppermute | solution.py:690
  212.1 2.5 multiply_reduce_fusion.5
  219.0 1.9 bitcast_dynamic-update-slice_fusion.7
  221.8 1.9 bitcast_dynamic-update-slice_fusion.5
  223.6 6.8 %collective-permute-done.36 = bf16[256,1024]{1,0:T(8,128)(2,1)S(1)} collective-permute-done((bf16[256,1024]{1,0:T(8,128)(2,1)S(1)}, bf16[256,1024]{1,0:T(8,128)(2,1)S(1)}, u32[]{:S(2)}, u32[]{:S(2)}) %collective-permute-start.36) | collective-permute-done | bytes 524320 | tf_op jit(solution)/shard_map/ppermute | solution.py:690
  233.8 4.7 fusion.9
  238.5 3.7 multiply_convert_fusion.1
  242.2 2.4 convolution_convert_fusion.2
  253.1 4.1 copy.161
  257.2 7.9 %collective-permute-done.46 = bf16[256,1024]{1,0:T(8,128)(2,1)} collective-permute-done((bf16[256,1024]{1,0:T(8,128)(2,1)}, bf16[256,1024]{1,0:T(8,128)(2,1)}, u32[]{:S(2)}, u32[]{:S(2)}) %collective-permute-start.46) | collective-permute-done | bytes 524320 | tf_op jit(solution)/shard_map/ppermute | solution.py:690
  265.1 10.8 %collective-permute-done.40 = bf16[256,1024]{1,0:T(8,128)(2,1)} collective-permute-done((bf16[256,1024]{1,0:T(8,128)(2,1)}, bf16[256,1024]{1,0:T(8,128)(2,1)}, u32[]{:S(2)}, u32[]{:S(2)}) %collective-permute-start.40) | collective-permute-done | bytes 524320 | tf_op jit(solution)/shard_map/ppermute | solution.py:690
  276.0 4.0 multiply_reduce_fusion
  284.6 3.9 convolution_convert_fusion
  288.6 2.8 convolution_convert_fusion.5
  291.4 6.3 %collective-permute-done.48 = bf16[256,1024]{1,0:T(8,128)(2,1)S(1)} collective-permute-done((bf16[256,1024]{1,0:T(8,128)(2,1)}, bf16[256,1024]{1,0:T(8,128)(2,1)S(1)}, u32[]{:S(2)}, u32[]{:S(2)}) %collective-permute-start.48) | collective-permute-done | bytes 524320 | tf_op jit(solution)/shard_map/ppermute | solution.py:690
  297.7 1.9 pad_maximum_fusion
  299.7 4.7 copy.172
  306.2 1.9 bitcast_dynamic-update-slice_fusion
  308.1 3.0 fusion.54.mixed_ref
  311.9 2.5 fusion.12
  319.1 3.9 collective-permute-start.91
  322.9 8.2 %shard_map.376 = (bf16[1024,128]{1,0:T(8,128)(2,1)}, bf16[1024,256]{1,0:T(8,128)(2,1)}) custom-call(s32[1]{0:T(128)} %bitcast.50.kv_ref, bf16[1024,128]{1,0:T(8,128)(2,1)} %get-tuple-element.45.qr_ref, bf16[1024,128]{1,0:T(8,128)(2,1)} %get-tuple-element.46.kr_ref, bf16[1024,128]{1,0:T(8,128)(2,1)} %get-tuple-element.47.vr_ref, ...), custom_call_target="tpu_custom_call" | custom-call | flops 9216000000 | bytes 4194304 | tf_op jit(solution)/shard_map/pallas_call | solution.py:537
  333.4 22.4 %shard_map.377 = (bf16[1024,1024]{1,0:T(8,128)(2,1)}, bf16[1024,512]{1,0:T(8,128)(2,1)}, f32[8,640]{1,0:T(8,128)}, f32[8,128]{1,0:T(8,128)}, f32[8,384]{1,0:T(8,128)}) custom-call(f32[1024,1024]{1,0:T(8,128)} %fusion.52.x_ref.raw_ref.z_ref.q_ref, f32[1024,512]{1,0:T(8,128)} %fusion.53.bc_ref.key_ref.value_ref, ...), custom_call_target="tpu_custom_call" | custom-call | flops 23592960000 | bytes 7864320 | tf_op jit(solution)/shard_map/pallas_call | solution.py:378
  355.8 2.7 fusion.55
  358.5 3.8 convolution_convert_fusion.1
  362.3 2.7 fusion.6
  373.7 2.6 convolution_convert_fusion.7
  386.6 2.0 collective-permute-start.92
  390.2 2.0 collective-permute-start.84
  395.4 6.3 %collective-permute-done.89 = bf16[128,512]{1,0:T(8,128)(2,1)S(1)} collective-permute-done((bf16[128,512]{1,0:T(8,128)(2,1)S(1)}, bf16[128,512]{1,0:T(8,128)(2,1)S(1)}, u32[]{:S(2)}, u32[]{:S(2)}) %collective-permute-start.89) | collective-permute-done | bytes 131104 | tf_op jit(solution)/shard_map/ppermute | solution.py:635
  406.5 2.2 collective-permute-done.90
  417.4 1.8 collective-permute-start.72
  421.6 2.4 collective-permute-done.72
  424.4 5.3 %collective-permute-done.73 = bf16[32,512]{1,0:T(8,128)(2,1)S(1)} collective-permute-done((bf16[32,512]{1,0:T(8,128)(2,1)S(1)}, bf16[32,512]{1,0:T(8,128)(2,1)S(1)}, u32[]{:S(2)}, u32[]{:S(2)}) %collective-permute-start.73) | collective-permute-done | bytes 32800 | tf_op jit(solution)/shard_map/ppermute | solution.py:745
  429.8 5.7 %collective-permute-done.74 = bf16[32,512]{1,0:T(8,128)(2,1)S(1)} collective-permute-done((bf16[32,512]{1,0:T(8,128)(2,1)S(1)}, bf16[32,512]{1,0:T(8,128)(2,1)S(1)}, u32[]{:S(2)}, u32[]{:S(2)}) %collective-permute-start.74) | collective-permute-done | bytes 32800 | tf_op jit(solution)/shard_map/ppermute | solution.py:745
  435.5 4.8 collective-permute-done.75
  440.3 4.8 collective-permute-done.76
  446.6 2.7 collective-permute-done.77
  449.4 2.3 collective-permute-start.78
  453.1 2.0 collective-permute-start.86
  455.8 3.7 collective-permute-done.82
  462.8 4.0 concatenate.95
  472.1 2.0 collective-permute-start.63
  475.3 4.0 collective-permute-start.65
  479.3 2.6 collective-permute-start.67
  483.2 2.4 fusion.16
  (539 shorter events, 189.7 us)
Async XLA Ops:
  7.3 226.5 %all-gather.2.cloned.1.call-start = ((), (), s32[]{:S(2)}) async-start(), calls=%async_computation.1 | async-start | bytes 3538944 | tf_op jit(solution)/shard_map/all_gather | solution.py:830
  19.0 35.9 %collective-permute-start.13 = (bf16[128,1024]{1,0:T(8,128)(2,1)}, bf16[128,1024]{1,0:T(8,128)(2,1)}, u32[]{:S(2)}, u32[]{:S(2)}) collective-permute-start(bf16[128,1024]{1,0:T(8,128)(2,1)} %get-tuple-element.209), channel_id=1, source_target_pairs={{4,12},{12,20},{20,28},{28,24},{24,16},{16,8},{8,0},{0,4},{5,13},{... | collective-permute-start | bytes 786440 | tf_op jit(solution)/shard_map/ppermute | solution.py:635
  21.9 35.3 %collective-permute-start.14 = (bf16[128,1024]{1,0:T(8,128)(2,1)}, bf16[128,1024]{1,0:T(8,128)(2,1)}, u32[]{:S(2)}, u32[]{:S(2)}) collective-permute-start(bf16[128,1024]{1,0:T(8,128)(2,1)} %get-tuple-element.209), channel_id=1, source_target_pairs={{4,0},{12,4},{20,12},{28,20},{24,28},{16,24},{8,16},{0,8},{5,1},{1... | collective-permute-start | bytes 786440 | tf_op jit(solution)/shard_map/ppermute | solution.py:635
  22.3 19.3 %collective-permute-start.3 = (bf16[33,512]{1,0:T(8,128)(2,1)S(1)}, bf16[33,512]{1,0:T(8,128)(2,1)}, u32[]{:S(2)}, u32[]{:S(2)}) collective-permute-start(bf16[33,512]{1,0:T(8,128)(2,1)S(1)} %constant_dynamic-update-slice_fusion.17), channel_id=1, source_target_pairs={{0,4},{4,8},{8,12},{12,16},{16,20},{20,24},{24,28},{28,0},{1,5},{5... | collective-permute-start | bytes 101384 | tf_op jit(solution)/shard_map/ppermute | solution.py:757
  24.3 19.3 %collective-permute-start.4 = (bf16[33,512]{1,0:T(8,128)(2,1)S(1)}, bf16[33,512]{1,0:T(8,128)(2,1)}, u32[]{:S(2)}, u32[]{:S(2)}) collective-permute-start(bf16[33,512]{1,0:T(8,128)(2,1)S(1)} %constant_dynamic-update-slice_fusion.17), channel_id=1, source_target_pairs={{0,8},{4,12},{8,16},{12,20},{16,24},{20,28},{24,0},{28,4},{1,9},{5... | collective-permute-start | bytes 101384 | tf_op jit(solution)/shard_map/ppermute | solution.py:757
  25.9 21.2 %collective-permute-start.5 = (bf16[33,512]{1,0:T(8,128)(2,1)S(1)}, bf16[33,512]{1,0:T(8,128)(2,1)}, u32[]{:S(2)}, u32[]{:S(2)}) collective-permute-start(bf16[33,512]{1,0:T(8,128)(2,1)S(1)} %constant_dynamic-update-slice_fusion.17), channel_id=1, source_target_pairs={{0,12},{4,16},{8,20},{12,24},{16,28},{20,0},{24,4},{28,8},{1,13},{... | collective-permute-start | bytes 101384 | tf_op jit(solution)/shard_map/ppermute | solution.py:757
  41.6 7.6 %collective-permute-start.6 = (bf16[33,512]{1,0:T(8,128)(2,1)S(1)}, bf16[33,512]{1,0:T(8,128)(2,1)S(1)}, u32[]{:S(2)}, u32[]{:S(2)}) collective-permute-start(bf16[33,512]{1,0:T(8,128)(2,1)S(1)} %constant_dynamic-update-slice_fusion.17), channel_id=1, source_target_pairs={{0,16},{4,20},{8,24},{12,28},{16,0},{20,4},{24,8},{28,12},{1,17},{... | collective-permute-start | bytes 101384 | tf_op jit(solution)/shard_map/ppermute | solution.py:757
  50.6 25.8 %collective-permute-start = (bf16[256,1024]{1,0:T(8,128)(2,1)S(1)}, bf16[256,1024]{1,0:T(8,128)(2,1)S(1)}, u32[]{:S(2)}, u32[]{:S(2)}) collective-permute-start(bf16[256,1024]{1,0:T(8,128)(2,1)S(1)} %copy-done.2), channel_id=1, source_target_pairs={{0,1},{1,0},{2,3},{3,2},{4,5},{5,4},{6,7},{7,6},{8,9},{9,8},{10,11... | collective-permute-start | bytes 1572872 | tf_op jit(solution)/shard_map/ppermute | solution.py:685
  53.2 7.2 %collective-permute-start.10 = (bf16[8,33,512]{2,1,0:T(8,128)(2,1)S(1)}, bf16[8,33,512]{2,1,0:T(8,128)(2,1)S(1)}, u32[]{:S(2)}, u32[]{:S(2)}) collective-permute-start(bf16[8,33,512]{2,1,0:T(8,128)(2,1)S(1)} %bitcast_dynamic-update-slice_fusion.20), channel_id=1, source_target_pairs={{0,1},{1,0},{2,3},{3,2},{4,5},{5,4},{6,7},{7,6},{8,9},{9,8},{10,11... | collective-permute-start | bytes 811016 | tf_op jit(solution)/shard_map/ppermute | solution.py:685
  53.2 10.6 %collective-permute-start.11 = (bf16[8,33,512]{2,1,0:T(8,128)(2,1)S(1)}, bf16[8,33,512]{2,1,0:T(8,128)(2,1)S(1)}, u32[]{:S(2)}, u32[]{:S(2)}) collective-permute-start(bf16[8,33,512]{2,1,0:T(8,128)(2,1)S(1)} %bitcast_dynamic-update-slice_fusion.20), channel_id=1, source_target_pairs={{0,2},{1,3},{2,0},{3,1},{4,6},{5,7},{6,4},{7,5},{8,10},{9,11},{10,... | collective-permute-start | bytes 811016 | tf_op jit(solution)/shard_map/ppermute | solution.py:690
  54.9 19.7 %collective-permute-start.1 = (bf16[256,1024]{1,0:T(8,128)(2,1)S(1)}, bf16[256,1024]{1,0:T(8,128)(2,1)}, u32[]{:S(2)}, u32[]{:S(2)}) collective-permute-start(bf16[256,1024]{1,0:T(8,128)(2,1)S(1)} %copy-done.2), channel_id=1, source_target_pairs={{0,2},{1,3},{2,0},{3,1},{4,6},{5,7},{6,4},{7,5},{8,10},{9,11},{10,... | collective-permute-start | bytes 1572872 | tf_op jit(solution)/shard_map/ppermute | solution.py:690
  57.2 8.4 %collective-permute-start.15 = (bf16[128,1024]{1,0:T(8,128)(2,1)}, bf16[128,1024]{1,0:T(8,128)(2,1)}, u32[]{:S(2)}, u32[]{:S(2)}) collective-permute-start(bf16[128,1024]{1,0:T(8,128)(2,1)} %collective-permute-done.13), channel_id=1, source_target_pairs={{4,12},{12,20},{20,28},{28,24},{24,16},{16,8},{8,0},{0,4},{5,13},{... | collective-permute-start | bytes 786440 | tf_op jit(solution)/shard_map/ppermute | solution.py:635
  60.4 8.1 %collective-permute-start.16 = (bf16[128,1024]{1,0:T(8,128)(2,1)}, bf16[128,1024]{1,0:T(8,128)(2,1)}, u32[]{:S(2)}, u32[]{:S(2)}) collective-permute-start(bf16[128,1024]{1,0:T(8,128)(2,1)} %collective-permute-done.14), channel_id=1, source_target_pairs={{4,0},{12,4},{20,12},{28,20},{24,28},{16,24},{8,16},{0,8},{5,1},{1... | collective-permute-start | bytes 786440 | tf_op jit(solution)/shard_map/ppermute | solution.py:635
  63.8 15.4 %collective-permute-start.12 = (bf16[8,33,512]{2,1,0:T(8,128)(2,1)S(1)}, bf16[8,33,512]{2,1,0:T(8,128)(2,1)S(1)}, u32[]{:S(2)}, u32[]{:S(2)}) collective-permute-start(bf16[8,33,512]{2,1,0:T(8,128)(2,1)S(1)} %collective-permute-done.11), channel_id=1, source_target_pairs={{0,1},{1,0},{2,3},{3,2},{4,5},{5,4},{6,7},{7,6},{8,9},{9,8},{10,11... | collective-permute-start | bytes 811016 | tf_op jit(solution)/shard_map/ppermute | solution.py:685
  65.6 33.2 %collective-permute-start.17 = (bf16[128,1024]{1,0:T(8,128)(2,1)}, bf16[128,1024]{1,0:T(8,128)(2,1)}, u32[]{:S(2)}, u32[]{:S(2)}) collective-permute-start(bf16[128,1024]{1,0:T(8,128)(2,1)} %collective-permute-done.15), channel_id=1, source_target_pairs={{4,12},{12,20},{20,28},{28,24},{24,16},{16,8},{8,0},{0,4},{5,13},{... | collective-permute-start | bytes 786440 | tf_op jit(solution)/shard_map/ppermute | solution.py:635
  68.5 32.7 %collective-permute-start.18 = (bf16[128,1024]{1,0:T(8,128)(2,1)}, bf16[128,1024]{1,0:T(8,128)(2,1)}, u32[]{:S(2)}, u32[]{:S(2)}) collective-permute-start(bf16[128,1024]{1,0:T(8,128)(2,1)} %collective-permute-done.16), channel_id=1, source_target_pairs={{4,0},{12,4},{20,12},{28,20},{24,28},{16,24},{8,16},{0,8},{5,1},{1... | collective-permute-start | bytes 786440 | tf_op jit(solution)/shard_map/ppermute | solution.py:635
  74.6 42.9 %collective-permute-start.2 = (bf16[256,1024]{1,0:T(8,128)(2,1)}, bf16[256,1024]{1,0:T(8,128)(2,1)}, u32[]{:S(2)}, u32[]{:S(2)}) collective-permute-start(bf16[256,1024]{1,0:T(8,128)(2,1)} %collective-permute-done.1), channel_id=1, source_target_pairs={{0,1},{1,0},{2,3},{3,2},{4,5},{5,4},{6,7},{7,6},{8,9},{9,8},{10,11... | collective-permute-start | bytes 1572872 | tf_op jit(solution)/shard_map/ppermute | solution.py:685
  114.0 377.2 %reduce-scatter.4.cloned.1.call-start = ((), (), s32[]{:S(2)}) async-start(), calls=%async_computation.2 | async-start | bytes 3538944
  114.3 43.4 %collective-permute-start.26 = (bf16[128,512]{0,1:T(8,128)(2,1)}, bf16[128,512]{0,1:T(8,128)(2,1)S(1)}, u32[]{:S(2)}, u32[]{:S(2)}) collective-permute-start(bf16[128,512]{0,1:T(8,128)(2,1)} %collective-permute-done.24), channel_id=1, source_target_pairs={{4,12},{12,20},{20,28},{28,24},{24,16},{16,8},{8,0},{0,4},{5,13},{... | collective-permute-start | bytes 393224 | tf_op jit(solution)/shard_map/ppermute | solution.py:635
  114.9 43.3 %collective-permute-start.27 = (bf16[128,512]{0,1:T(8,128)(2,1)}, bf16[128,512]{0,1:T(8,128)(2,1)S(1)}, u32[]{:S(2)}, u32[]{:S(2)}) collective-permute-start(bf16[128,512]{0,1:T(8,128)(2,1)} %collective-permute-done.25), channel_id=1, source_target_pairs={{4,0},{12,4},{20,12},{28,20},{24,28},{16,24},{8,16},{0,8},{5,1},{1... | collective-permute-start | bytes 393224 | tf_op jit(solution)/shard_map/ppermute | solution.py:635
  145.2 8.8 %collective-permute-start.21 = (f32[1024]{0:T(1024)S(1)}, f32[1024]{0:T(1024)S(1)}, u32[]{:S(2)}, u32[]{:S(2)}) collective-permute-start(f32[1024]{0:T(1024)S(1)} %bitcast.263), channel_id=1, source_target_pairs={{0,1},{1,0},{2,3},{3,2},{4,5},{5,4},{6,7},{7,6},{8,9},{9,8},{10,11... | collective-permute-start | bytes 12296 | tf_op jit(solution)/shard_map/ppermute | solution.py:685
  146.4 7.8 %collective-permute-start.23 = (f32[1024]{0:T(1024)S(1)}, f32[1024]{0:T(1024)S(1)}, u32[]{:S(2)}, u32[]{:S(2)}) collective-permute-start(f32[1024]{0:T(1024)S(1)} %collective-permute-done.22), channel_id=1, source_target_pairs={{0,1},{1,0},{2,3},{3,2},{4,5},{5,4},{6,7},{7,6},{8,9},{9,8},{10,11... | collective-permute-start | bytes 12296 | tf_op jit(solution)/shard_map/ppermute | solution.py:685
  157.7 9.1 %collective-permute-start.28 = (bf16[128,512]{0,1:T(8,128)(2,1)S(1)}, bf16[128,512]{0,1:T(8,128)(2,1)S(1)}, u32[]{:S(2)}, u32[]{:S(2)}) collective-permute-start(bf16[128,512]{0,1:T(8,128)(2,1)S(1)} %collective-permute-done.26), channel_id=1, source_target_pairs={{4,12},{12,20},{20,28},{28,24},{24,16},{16,8},{8,0},{0,4},{5,13},{... | collective-permute-start | bytes 393224 | tf_op jit(solution)/shard_map/ppermute | solution.py:635
  158.2 9.0 %collective-permute-start.29 = (bf16[128,512]{0,1:T(8,128)(2,1)S(1)}, bf16[128,512]{0,1:T(8,128)(2,1)S(1)}, u32[]{:S(2)}, u32[]{:S(2)}) collective-permute-start(bf16[128,512]{0,1:T(8,128)(2,1)S(1)} %collective-permute-done.27), channel_id=1, source_target_pairs={{4,0},{12,4},{20,12},{28,20},{24,28},{16,24},{8,16},{0,8},{5,1},{1... | collective-permute-start | bytes 393224 | tf_op jit(solution)/shard_map/ppermute | solution.py:635
  166.8 10.9 %collective-permute-start.30 = (bf16[64,512]{0,1:T(8,128)(2,1)S(1)}, bf16[64,512]{0,1:T(8,128)(2,1)S(1)}, u32[]{:S(2)}, u32[]{:S(2)}) collective-permute-start(bf16[64,512]{0,1:T(8,128)(2,1)S(1)} %bitcast.252), channel_id=1, source_target_pairs={{4,12},{12,20},{20,28},{28,24},{24,16},{16,8},{8,0},{0,4},{5,13},{... | collective-permute-start | bytes 196616 | tf_op jit(solution)/shard_map/ppermute | solution.py:635
  167.3 10.8 %collective-permute-start.31 = (bf16[64,512]{0,1:T(8,128)(2,1)S(1)}, bf16[64,512]{0,1:T(8,128)(2,1)S(1)}, u32[]{:S(2)}, u32[]{:S(2)}) collective-permute-start(bf16[64,512]{0,1:T(8,128)(2,1)S(1)} %slice.207), channel_id=1, source_target_pairs={{4,0},{12,4},{20,12},{28,20},{24,28},{16,24},{8,16},{0,8},{5,1},{1... | collective-permute-start | bytes 196616 | tf_op jit(solution)/shard_map/ppermute | solution.py:635
  186.4 15.1 %collective-permute-start.42 = (bf16[256,1024]{1,0:T(8,128)(2,1)}, bf16[256,1024]{1,0:T(8,128)(2,1)}, u32[]{:S(2)}, u32[]{:S(2)}) collective-permute-start(bf16[256,1024]{1,0:T(8,128)(2,1)} %fusion.19), channel_id=1, source_target_pairs={{0,2},{1,3},{2,0},{3,1},{4,6},{5,7},{6,4},{7,5},{8,10},{9,11},{10,... | collective-permute-start | bytes 1572872 | tf_op jit(solution)/shard_map/ppermute | solution.py:690
  186.4 15.1 %collective-permute-start.32 = (bf16[256,1024]{1,0:T(8,128)(2,1)}, bf16[256,1024]{1,0:T(8,128)(2,1)}, u32[]{:S(2)}, u32[]{:S(2)}) collective-permute-start(bf16[256,1024]{1,0:T(8,128)(2,1)} %get-tuple-element.185), channel_id=1, source_target_pairs={{0,1},{1,0},{2,3},{3,2},{4,5},{5,4},{6,7},{7,6},{8,9},{9,8},{10,11... | collective-permute-start | bytes 1572872 | tf_op jit(solution)/shard_map/ppermute | solution.py:685
  188.6 23.5 %collective-permute-start.34 = (bf16[256,1024]{1,0:T(8,128)(2,1)S(1)}, bf16[256,1024]{1,0:T(8,128)(2,1)}, u32[]{:S(2)}, u32[]{:S(2)}) collective-permute-start(bf16[256,1024]{1,0:T(8,128)(2,1)S(1)} %add_convert_fusion.3), channel_id=1, source_target_pairs={{0,2},{1,3},{2,0},{3,1},{4,6},{5,7},{6,4},{7,5},{8,10},{9,11},{10,... | collective-permute-start | bytes 1572872 | tf_op jit(solution)/shard_map/ppermute | solution.py:690
  189.8 31.1 %collective-permute-start.41 = (bf16[256,1024]{1,0:T(8,128)(2,1)}, bf16[256,1024]{1,0:T(8,128)(2,1)S(1)}, u32[]{:S(2)}, u32[]{:S(2)}) collective-permute-start(bf16[256,1024]{1,0:T(8,128)(2,1)} %fusion.19), channel_id=1, source_target_pairs={{0,1},{1,0},{2,3},{3,2},{4,5},{5,4},{6,7},{7,6},{8,9},{9,8},{10,11... | collective-permute-start | bytes 1572872 | tf_op jit(solution)/shard_map/ppermute | solution.py:685
  201.5 28.9 %collective-permute-start.43 = (bf16[256,1024]{1,0:T(8,128)(2,1)}, bf16[256,1024]{1,0:T(8,128)(2,1)S(1)}, u32[]{:S(2)}, u32[]{:S(2)}) collective-permute-start(bf16[256,1024]{1,0:T(8,128)(2,1)} %collective-permute-done.42), channel_id=1, source_target_pairs={{0,1},{1,0},{2,3},{3,2},{4,5},{5,4},{6,7},{7,6},{8,9},{9,8},{10,11... | collective-permute-start | bytes 1572872 | tf_op jit(solution)/shard_map/ppermute | solution.py:685
  217.2 13.3 %collective-permute-start.36 = (bf16[256,1024]{1,0:T(8,128)(2,1)S(1)}, bf16[256,1024]{1,0:T(8,128)(2,1)S(1)}, u32[]{:S(2)}, u32[]{:S(2)}) collective-permute-start(bf16[256,1024]{1,0:T(8,128)(2,1)S(1)} %get-tuple-element.161), channel_id=1, source_target_pairs={{0,2},{1,3},{2,0},{3,1},{4,6},{5,7},{6,4},{7,5},{8,10},{9,11},{10,... | collective-permute-start | bytes 1572872 | tf_op jit(solution)/shard_map/ppermute | solution.py:690
  220.9 10.4 %collective-permute-start.35 = (bf16[256,1024]{1,0:T(8,128)(2,1)S(1)}, bf16[256,1024]{1,0:T(8,128)(2,1)S(1)}, u32[]{:S(2)}, u32[]{:S(2)}) collective-permute-start(bf16[256,1024]{1,0:T(8,128)(2,1)S(1)} %get-tuple-element.161), channel_id=1, source_target_pairs={{0,1},{1,0},{2,3},{3,2},{4,5},{5,4},{6,7},{7,6},{8,9},{9,8},{10,11... | collective-permute-start | bytes 1572872 | tf_op jit(solution)/shard_map/ppermute | solution.py:685
  248.6 8.6 %collective-permute-start.44 = (bf16[256,1024]{1,0:T(8,128)(2,1)}, bf16[256,1024]{1,0:T(8,128)(2,1)}, u32[]{:S(2)}, u32[]{:S(2)}) collective-permute-start(bf16[256,1024]{1,0:T(8,128)(2,1)} %get-tuple-element.181), channel_id=1, source_target_pairs={{0,1},{1,0},{2,3},{3,2},{4,5},{5,4},{6,7},{7,6},{8,9},{9,8},{10,11... | collective-permute-start | bytes 1572872 | tf_op jit(solution)/shard_map/ppermute | solution.py:685
  249.1 8.1 %collective-permute-start.38 = (bf16[256,1024]{1,0:T(8,128)(2,1)}, bf16[256,1024]{1,0:T(8,128)(2,1)}, u32[]{:S(2)}, u32[]{:S(2)}) collective-permute-start(bf16[256,1024]{1,0:T(8,128)(2,1)} %get-tuple-element.183), channel_id=1, source_target_pairs={{0,1},{1,0},{2,3},{3,2},{4,5},{5,4},{6,7},{7,6},{8,9},{9,8},{10,11... | collective-permute-start | bytes 1572872 | tf_op jit(solution)/shard_map/ppermute | solution.py:685
  250.1 15.0 %collective-permute-start.46 = (bf16[256,1024]{1,0:T(8,128)(2,1)}, bf16[256,1024]{1,0:T(8,128)(2,1)}, u32[]{:S(2)}, u32[]{:S(2)}) collective-permute-start(bf16[256,1024]{1,0:T(8,128)(2,1)} %add_convert_fusion.1), channel_id=1, source_target_pairs={{0,2},{1,3},{2,0},{3,1},{4,6},{5,7},{6,4},{7,5},{8,10},{9,11},{10,... | collective-permute-start | bytes 1572872 | tf_op jit(solution)/shard_map/ppermute | solution.py:690
  252.2 23.8 %collective-permute-start.40 = (bf16[256,1024]{1,0:T(8,128)(2,1)}, bf16[256,1024]{1,0:T(8,128)(2,1)}, u32[]{:S(2)}, u32[]{:S(2)}) collective-permute-start(bf16[256,1024]{1,0:T(8,128)(2,1)} %add_convert_fusion.2), channel_id=1, source_target_pairs={{0,2},{1,3},{2,0},{3,1},{4,6},{5,7},{6,4},{7,5},{8,10},{9,11},{10,... | collective-permute-start | bytes 1572872 | tf_op jit(solution)/shard_map/ppermute | solution.py:690
  283.9 13.8 %collective-permute-start.48 = (bf16[256,1024]{1,0:T(8,128)(2,1)}, bf16[256,1024]{1,0:T(8,128)(2,1)S(1)}, u32[]{:S(2)}, u32[]{:S(2)}) collective-permute-start(bf16[256,1024]{1,0:T(8,128)(2,1)} %get-tuple-element.157), channel_id=1, source_target_pairs={{0,2},{1,3},{2,0},{3,1},{4,6},{5,7},{6,4},{7,5},{8,10},{9,11},{10,... | collective-permute-start | bytes 1572872 | tf_op jit(solution)/shard_map/ppermute | solution.py:690
  288.5 16.0 %collective-permute-start.47 = (bf16[256,1024]{1,0:T(8,128)(2,1)}, bf16[256,1024]{1,0:T(8,128)(2,1)S(1)}, u32[]{:S(2)}, u32[]{:S(2)}) collective-permute-start(bf16[256,1024]{1,0:T(8,128)(2,1)} %get-tuple-element.157), channel_id=1, source_target_pairs={{0,1},{1,0},{2,3},{3,2},{4,5},{5,4},{6,7},{7,6},{8,9},{9,8},{10,11... | collective-permute-start | bytes 1572872 | tf_op jit(solution)/shard_map/ppermute | solution.py:685
  297.7 8.5 %collective-permute-start.49 = (bf16[256,1024]{1,0:T(8,128)(2,1)S(1)}, bf16[256,1024]{1,0:T(8,128)(2,1)}, u32[]{:S(2)}, u32[]{:S(2)}) collective-permute-start(bf16[256,1024]{1,0:T(8,128)(2,1)S(1)} %collective-permute-done.48), channel_id=1, source_target_pairs={{0,1},{1,0},{2,3},{3,2},{4,5},{5,4},{6,7},{7,6},{8,9},{9,8},{10,11... | collective-permute-start | bytes 1572872 | tf_op jit(solution)/shard_map/ppermute | solution.py:685
  314.4 16.8 %collective-permute-start.50 = (f32[1024]{0:T(1024)S(1)}, f32[1024]{0:T(1024)S(1)}, u32[]{:S(2)}, u32[]{:S(2)}) collective-permute-start(f32[1024]{0:T(1024)S(1)} %fusion.12), channel_id=1, source_target_pairs={{0,1},{1,0},{2,3},{3,2},{4,5},{5,4},{6,7},{7,6},{8,9},{9,8},{10,11... | collective-permute-start | bytes 12296 | tf_op jit(solution)/shard_map/ppermute | solution.py:685
  315.0 8.0 %collective-permute-start.51 = (f32[1024]{0:T(1024)S(1)}, f32[1024]{0:T(1024)S(1)}, u32[]{:S(2)}, u32[]{:S(2)}) collective-permute-start(f32[1024]{0:T(1024)S(1)} %fusion.12), channel_id=1, source_target_pairs={{0,2},{1,3},{2,0},{3,1},{4,6},{5,7},{6,4},{7,5},{8,10},{9,11},{10,... | collective-permute-start | bytes 12296 | tf_op jit(solution)/shard_map/ppermute | solution.py:690
  318.3 63.8 %collective-permute-start.87 = (bf16[64,512]{1,0:T(8,128)(2,1)}, bf16[64,512]{1,0:T(8,128)(2,1)}, u32[]{:S(2)}, u32[]{:S(2)}) collective-permute-start(bf16[64,512]{1,0:T(8,128)(2,1)} %get-tuple-element.193), channel_id=1, source_target_pairs={{4,12},{12,20},{20,28},{28,24},{24,16},{16,8},{8,0},{0,4},{5,13},{... | collective-permute-start | bytes 196616 | tf_op jit(solution)/shard_map/ppermute | solution.py:635
  319.1 63.9 %collective-permute-start.91 = (bf16[64,512]{1,0:T(8,128)(2,1)}, bf16[64,512]{1,0:T(8,128)(2,1)}, u32[]{:S(2)}, u32[]{:S(2)}) collective-permute-start(bf16[64,512]{1,0:T(8,128)(2,1)} %get-tuple-element.194), channel_id=1, source_target_pairs={{4,0},{12,4},{20,12},{28,20},{24,28},{16,24},{8,16},{0,8},{5,1},{1... | collective-permute-start | bytes 196616 | tf_op jit(solution)/shard_map/ppermute | solution.py:635
  322.9 8.5 %collective-permute-start.52 = (f32[1024]{0:T(1024)S(1)}, f32[1024]{0:T(1024)S(1)}, u32[]{:S(2)}, u32[]{:S(2)}) collective-permute-start(f32[1024]{0:T(1024)S(1)} %collective-permute-done.51), channel_id=1, source_target_pairs={{0,1},{1,0},{2,3},{3,2},{4,5},{5,4},{6,7},{7,6},{8,9},{9,8},{10,11... | collective-permute-start | bytes 12296 | tf_op jit(solution)/shard_map/ppermute | solution.py:685
  367.3 51.9 %collective-permute-start.54 = (bf16[256,1024]{1,0:T(8,128)(2,1)}, bf16[256,1024]{1,0:T(8,128)(2,1)}, u32[]{:S(2)}, u32[]{:S(2)}) collective-permute-start(bf16[256,1024]{1,0:T(8,128)(2,1)} %get-tuple-element.180), channel_id=1, source_target_pairs={{0,1},{1,0},{2,3},{3,2},{4,5},{5,4},{6,7},{7,6},{8,9},{9,8},{10,11... | collective-permute-start | bytes 1572872 | tf_op jit(solution)/shard_map/ppermute | solution.py:685
  372.6 7.5 %collective-permute-start.57 = (f32[8,392]{1,0:T(8,128)}, f32[8,392]{1,0:T(8,128)}, u32[]{:S(2)}, u32[]{:S(2)}) collective-permute-start(f32[8,392]{1,0:T(8,128)} %bitcast.238), channel_id=1, source_target_pairs={{0,1},{1,0},{2,3},{3,2},{4,5},{5,4},{6,7},{7,6},{8,9},{9,8},{10,11... | collective-permute-start | bytes 37640 | tf_op jit(solution)/shard_map/ppermute | solution.py:685
  373.2 11.2 %collective-permute-start.56 = (f32[8,392]{1,0:T(8,128)}, f32[8,392]{1,0:T(8,128)}, u32[]{:S(2)}, u32[]{:S(2)}) collective-permute-start(f32[8,392]{1,0:T(8,128)} %bitcast.239), channel_id=1, source_target_pairs={{0,1},{1,0},{2,3},{3,2},{4,5},{5,4},{6,7},{7,6},{8,9},{9,8},{10,11... | collective-permute-start | bytes 37640 | tf_op jit(solution)/shard_map/ppermute | solution.py:685
  380.1 9.9 %collective-permute-start.79 = (bf16[64,1024]{1,0:T(8,128)(2,1)}, bf16[64,1024]{1,0:T(8,128)(2,1)S(1)}, u32[]{:S(2)}, u32[]{:S(2)}) collective-permute-start(bf16[64,1024]{1,0:T(8,128)(2,1)} %get-tuple-element.177), channel_id=1, source_target_pairs={{4,12},{12,20},{20,28},{28,24},{24,16},{16,8},{8,0},{0,4},{5,13},{... | collective-permute-start | bytes 393224 | tf_op jit(solution)/shard_map/ppermute | solution.py:635
  382.1 7.9 %collective-permute-start.83 = (bf16[64,1024]{1,0:T(8,128)(2,1)S(1)}, bf16[64,1024]{1,0:T(8,128)(2,1)S(1)}, u32[]{:S(2)}, u32[]{:S(2)}) collective-permute-start(bf16[64,1024]{1,0:T(8,128)(2,1)S(1)} %get-tuple-element.178), channel_id=1, source_target_pairs={{4,0},{12,4},{20,12},{28,20},{24,28},{16,24},{8,16},{0,8},{5,1},{1... | collective-permute-start | bytes 393224 | tf_op jit(solution)/shard_map/ppermute | solution.py:635
  390.1 13.1 %collective-permute-start.80 = (bf16[128,1024]{1,0:T(8,128)(2,1)S(1)}, bf16[128,1024]{1,0:T(8,128)(2,1)S(1)}, u32[]{:S(2)}, u32[]{:S(2)}) collective-permute-start(bf16[128,1024]{1,0:T(8,128)(2,1)S(1)} %get-tuple-element.175), channel_id=1, source_target_pairs={{4,12},{12,20},{20,28},{28,24},{24,16},{16,8},{8,0},{0,4},{5,13},{... | collective-permute-start | bytes 786440 | tf_op jit(solution)/shard_map/ppermute | solution.py:635
  390.2 13.9 %collective-permute-start.84 = (bf16[128,1024]{1,0:T(8,128)(2,1)S(1)}, bf16[128,1024]{1,0:T(8,128)(2,1)S(1)}, u32[]{:S(2)}, u32[]{:S(2)}) collective-permute-start(bf16[128,1024]{1,0:T(8,128)(2,1)S(1)} %get-tuple-element.176), channel_id=1, source_target_pairs={{4,0},{12,4},{20,12},{28,20},{24,28},{16,24},{8,16},{0,8},{5,1},{1... | collective-permute-start | bytes 786440 | tf_op jit(solution)/shard_map/ppermute | solution.py:635
  392.3 9.4 %collective-permute-start.89 = (bf16[128,512]{1,0:T(8,128)(2,1)S(1)}, bf16[128,512]{1,0:T(8,128)(2,1)S(1)}, u32[]{:S(2)}, u32[]{:S(2)}) collective-permute-start(bf16[128,512]{1,0:T(8,128)(2,1)S(1)} %get-tuple-element.189), channel_id=1, source_target_pairs={{4,12},{12,20},{20,28},{28,24},{24,16},{16,8},{8,0},{0,4},{5,13},{... | collective-permute-start | bytes 393224 | tf_op jit(solution)/shard_map/ppermute | solution.py:635
  393.1 8.7 %collective-permute-start.93 = (bf16[128,512]{1,0:T(8,128)(2,1)S(1)}, bf16[128,512]{1,0:T(8,128)(2,1)S(1)}, u32[]{:S(2)}, u32[]{:S(2)}) collective-permute-start(bf16[128,512]{1,0:T(8,128)(2,1)S(1)} %get-tuple-element.190), channel_id=1, source_target_pairs={{4,0},{12,4},{20,12},{28,20},{24,28},{16,24},{8,16},{0,8},{5,1},{1... | collective-permute-start | bytes 393224 | tf_op jit(solution)/shard_map/ppermute | solution.py:635
  401.7 58.9 %collective-permute-start.53 = (bf16[256,1024]{1,0:T(8,128)(2,1)}, bf16[256,1024]{1,0:T(8,128)(2,1)S(1)}, u32[]{:S(2)}, u32[]{:S(2)}) collective-permute-start(bf16[256,1024]{1,0:T(8,128)(2,1)} %get-tuple-element.179), channel_id=1, source_target_pairs={{0,1},{1,0},{2,3},{3,2},{4,5},{5,4},{6,7},{7,6},{8,9},{9,8},{10,11... | collective-permute-start | bytes 1572872 | tf_op jit(solution)/shard_map/ppermute | solution.py:685
  401.7 12.4 %collective-permute-start.69 = (bf16[8,32,512]{2,1,0:T(8,128)(2,1)S(1)}, bf16[8,32,512]{2,1,0:T(8,128)(2,1)}, u32[]{:S(2)}, u32[]{:S(2)}) collective-permute-start(bf16[8,32,512]{2,1,0:T(8,128)(2,1)S(1)} %get-tuple-element.195), channel_id=1, source_target_pairs={{0,1},{1,0},{2,3},{3,2},{4,5},{5,4},{6,7},{7,6},{8,9},{9,8},{10,11... | collective-permute-start | bytes 786440 | tf_op jit(solution)/shard_map/ppermute | solution.py:685
  408.7 7.4 %collective-permute-start.71 = (bf16[8,32,512]{2,1,0:T(8,128)(2,1)S(1)}, bf16[8,32,512]{2,1,0:T(8,128)(2,1)S(1)}, u32[]{:S(2)}, u32[]{:S(2)}) collective-permute-start(bf16[8,32,512]{2,1,0:T(8,128)(2,1)S(1)} %fusion.25), channel_id=1, source_target_pairs={{0,2},{1,3},{2,0},{3,1},{4,6},{5,7},{6,4},{7,5},{8,10},{9,11},{10,... | collective-permute-start | bytes 786440 | tf_op jit(solution)/shard_map/ppermute | solution.py:690
  409.9 41.8 %collective-permute-start.81 = (bf16[128,1024]{1,0:T(8,128)(2,1)}, bf16[128,1024]{1,0:T(8,128)(2,1)S(1)}, u32[]{:S(2)}, u32[]{:S(2)}) collective-permute-start(bf16[128,1024]{1,0:T(8,128)(2,1)} %get-tuple-element.173), channel_id=1, source_target_pairs={{4,12},{12,20},{20,28},{28,24},{24,16},{16,8},{8,0},{0,4},{5,13},{... | collective-permute-start | bytes 786440 | tf_op jit(solution)/shard_map/ppermute | solution.py:635
  414.2 37.5 %collective-permute-start.85 = (bf16[128,1024]{1,0:T(8,128)(2,1)}, bf16[128,1024]{1,0:T(8,128)(2,1)S(1)}, u32[]{:S(2)}, u32[]{:S(2)}) collective-permute-start(bf16[128,1024]{1,0:T(8,128)(2,1)} %get-tuple-element.174), channel_id=1, source_target_pairs={{4,0},{12,4},{20,12},{28,20},{24,28},{16,24},{8,16},{0,8},{5,1},{1... | collective-permute-start | bytes 786440 | tf_op jit(solution)/shard_map/ppermute | solution.py:635
  420.6 40.0 %collective-permute-start.55 = (bf16[256,1024]{1,0:T(8,128)(2,1)S(1)}, bf16[256,1024]{1,0:T(8,128)(2,1)S(1)}, u32[]{:S(2)}, u32[]{:S(2)}) collective-permute-start(bf16[256,1024]{1,0:T(8,128)(2,1)S(1)} %add_convert_fusion), channel_id=1, source_target_pairs={{0,2},{1,3},{2,0},{3,1},{4,6},{5,7},{6,4},{7,5},{8,10},{9,11},{10,... | collective-permute-start | bytes 1572872 | tf_op jit(solution)/shard_map/ppermute | solution.py:690
  472.0 7.3 %collective-permute-start.62 = (f32[470]{0:T(512)S(1)}, f32[470]{0:T(512)S(1)}, u32[]{:S(2)}, u32[]{:S(2)}) collective-permute-start(f32[470]{0:T(512)S(1)} %bitcast.278), channel_id=1, source_target_pairs={{0,4},{4,8},{8,12},{12,16},{16,20},{20,24},{24,28},{28,0},{1,5},{5... | collective-permute-start | bytes 5648 | tf_op jit(solution)/shard_map/ppermute | solution.py:745
  472.1 9.9 %collective-permute-start.63 = (f32[470]{0:T(512)S(1)}, f32[470]{0:T(512)S(1)}, u32[]{:S(2)}, u32[]{:S(2)}) collective-permute-start(f32[470]{0:T(512)S(1)} %bitcast.277), channel_id=1, source_target_pairs={{0,8},{4,12},{8,16},{12,20},{16,24},{20,28},{24,0},{28,4},{1,9},{5... | collective-permute-start | bytes 5648 | tf_op jit(solution)/shard_map/ppermute | solution.py:745
  474.1 11.8 %collective-permute-start.64 = (f32[470]{0:T(512)S(1)}, f32[470]{0:T(512)S(1)}, u32[]{:S(2)}, u32[]{:S(2)}) collective-permute-start(f32[470]{0:T(512)S(1)} %bitcast.276), channel_id=1, source_target_pairs={{0,12},{4,16},{8,20},{12,24},{16,28},{20,0},{24,4},{28,8},{1,13},{... | collective-permute-start | bytes 5648 | tf_op jit(solution)/shard_map/ppermute | solution.py:745
  475.3 10.7 %collective-permute-start.65 = (f32[470]{0:T(512)S(1)}, f32[470]{0:T(512)S(1)}, u32[]{:S(2)}, u32[]{:S(2)}) collective-permute-start(f32[470]{0:T(512)S(1)} %bitcast.275), channel_id=1, source_target_pairs={{0,16},{4,20},{8,24},{12,28},{16,0},{20,4},{24,8},{28,12},{1,17},{... | collective-permute-start | bytes 5648 | tf_op jit(solution)/shard_map/ppermute | solution.py:745
  (103 other events, 738.0 us)
Sparse Core Ops, SparseCore 0:
  114.2 66.8 all-gather.1
  304.6 76.8 reduce-scatter.3

commit v2 on v1

v2 whole, which is shorter than its diff:
```python
import functools
import math

import jax
import jax.numpy as jnp
from jax import lax
from jax.experimental import pallas as pl
from jax.experimental.pallas import tpu as pltpu
from jax.sharding import PartitionSpec as P

D = 1024
MH = 24
HEAD_SIZE = 64
MAMBA_STATES = 128
CONV = 4
QUERY_HEADS = 8
KEY_VALUE_HEADS = 2
SEQUENCE_TOKENS = 1024
DSSM = 1536


EPS = 1e-05
ROPE_BASE = 100000000000.0
NEG_FILL = -1e30
HIGH = lax.Precision.HIGHEST


def rms_scale(values):
    return lax.rsqrt(jnp.mean(values * values, axis=-1, keepdims=True) + EPS)


def norm_back(values, row_scale, gain_row, grad_in):
    scaled_grad = grad_in * gain_row
    gain_grad = jnp.sum(grad_in * values * row_scale, axis=0)
    value_grad = row_scale * scaled_grad - values * (row_scale * row_scale * row_scale) * jnp.mean(
        scaled_grad * values, axis=-1, keepdims=True
    )
    return (value_grad, gain_grad)


def product(left, right):
    return jnp.dot(left, right, preferred_element_type=jnp.float32)


def product_tn(left, right):
    return lax.dot_general(
        left, right, (((0,), (0,)), ((), ())), preferred_element_type=jnp.float32
    )


def product_nt(left, right):
    return lax.dot_general(
        left, right, (((1,), (1,)), ((), ())), preferred_element_type=jnp.float32
    )


def split_dot(values, selector, dims):
    high = values.astype(jnp.bfloat16)
    low = (values - high.astype(jnp.float32)).astype(jnp.bfloat16)
    left = lax.dot_general(high, selector, dims, preferred_element_type=jnp.float32)
    return left + lax.dot_general(low, selector, dims, preferred_element_type=jnp.float32)


NN = (((1,), (0,)), ((), ()))
NT = (((1,), (1,)), ((), ()))
TN = (((0,), (0,)), ((), ()))


def mxu(left, right, dims):
    return lax.dot_general(
        left.astype(jnp.bfloat16),
        right.astype(jnp.bfloat16),
        dims,
        preferred_element_type=jnp.float32,
    )


def iota(shape, dim):
    return lax.broadcasted_iota(jnp.int32, shape, dim)


def head_groups(width):
    return [(low, min(low + 2 * HEAD_SIZE, width)) for low in range(0, width, 2 * HEAD_SIZE)]


def chunk_common(chunk, start, rows, width, raw_ref, doc_ref, pad_ref, w_ref, par_ref):
    doc = doc_ref[pl.ds(start, chunk), :]
    age = start + iota((chunk, 1), 0) - doc
    span = pad_ref[pl.ds(start, chunk + 8), :]
    conv = w_ref[CONV : CONV + 1, :] + w_ref[CONV - 1 : CONV, :] * span[8:, :]
    lagged = [span[8:, :]]
    for lag in range(1, CONV):
        moved = jnp.where(age >= lag, span[8 - lag : 8 - lag + chunk, :], 0.0)
        lagged.append(moved)
        conv = conv + w_ref[CONV - 1 - lag : CONV - lag, :] * moved
    sig = jax.nn.sigmoid(conv)
    act = conv * sig
    raw = raw_ref[rows, :] + par_ref[0:1, :]
    step = jnp.maximum(raw, 0.0) + jnp.log1p(jnp.exp(-jnp.abs(raw)))
    rate = step * par_ref[1:2, :]
    lower = (iota((chunk, chunk), 0) >= iota((chunk, chunk), 1)).astype(jnp.bfloat16)
    high = rate.astype(jnp.bfloat16)
    low = (rate - high.astype(jnp.float32)).astype(jnp.bfloat16)
    total = mxu(lower, high, NN) + mxu(lower, low, NN)
    lanes = par_ref.shape[1]
    spread = (iota((lanes, width), 0) == iota((lanes, width), 1) // HEAD_SIZE).astype(jnp.bfloat16)
    key_pos = start + iota((chunk, chunk), 1)
    allowed = (key_pos <= start + iota((chunk, chunk), 0)) & (key_pos >= doc)
    doc_last = doc[chunk - 1 : chunk, :]
    ends = total[chunk - 1 : chunk, :]
    live = jnp.where(doc < start, jnp.exp(total), 0.0)
    keep = jnp.where(start + iota((chunk, 1), 0) >= doc_last, jnp.exp(ends - total), 0.0)
    carry = jnp.where(doc_last < start, jnp.exp(ends), 0.0)
    wide = split_dot(jnp.concatenate([step, live, keep, jnp.broadcast_to(carry, (8, lanes))], axis=0), spread, NN)
    return dict(
        conv=conv, sig=sig, act=act, raw=raw, step=step, total=total, turned=total.T, spread=spread, allowed=allowed,
        carry=carry, age=age, lagged=lagged, lower=lower,
        step_w=wide[:chunk], live_w=wide[chunk : 2 * chunk], keep_w=wide[2 * chunk : 3 * chunk],
        carry_w=wide[3 * chunk : 3 * chunk + 1],
    )


def decay_of(part, head):
    gap = part["total"][:, head : head + 1] - part["turned"][head : head + 1, :]
    return jnp.where(part["allowed"], jnp.exp(gap), 0.0)


def only(values, low, high):
    lane = iota(values.shape, 1)
    return jnp.where((lane >= low) & (lane < high), values, jnp.zeros_like(values))


def place_of(order_ref, block_rows, length, start):
    token = pl.program_id(0) * length + start
    return pl.multiple_of(
        order_ref[token // block_rows] * block_rows + token % block_rows, 128
    )


def fill_conv_input(order_ref, block_rows, width, x_ref, bc_ref, pad_ref):
    length = pad_ref.shape[0] - 8
    pad_ref[0:8, :] = jnp.zeros((8, pad_ref.shape[1]), jnp.float32)
    for start in range(0, length, block_rows):
        rows = pl.ds(place_of(order_ref, block_rows, length, start), block_rows)
        pad_ref[8 + start : 8 + start + block_rows, :width] = x_ref[rows, :width]
        pad_ref[8 + start : 8 + start + block_rows, width:] = bc_ref[rows, :]


def mamba_forward_kernel(
    chunk, width, block_rows, order_ref, x_ref, bc_ref, raw_ref, z_ref, doc_ref, w_ref, par_ref, skip_ref, y_ref, square_ref, kept_ref, pad_ref, state_ref
):
    length = pad_ref.shape[0] - 8
    fill_conv_input(order_ref, block_rows, width, x_ref, bc_ref, pad_ref)
    state_ref[...] = jnp.zeros_like(state_ref)

    def one_chunk(index, _):
        start = pl.multiple_of(index * chunk, chunk)
        rows = pl.ds(place_of(order_ref, block_rows, length, start), chunk)
        part = chunk_common(chunk, start, rows, width, raw_ref, doc_ref, pad_ref, w_ref, par_ref)
        inner = part["act"][:, :width]
        bm = part["act"][:, width : width + MAMBA_STATES].astype(jnp.bfloat16)
        cm = part["act"][:, width + MAMBA_STATES :].astype(jnp.bfloat16)
        driven = (inner * part["step_w"]).astype(jnp.bfloat16)
        pair = mxu(cm, bm, NT)
        pieces = []
        for low, high in head_groups(width):
            heads = range(low // HEAD_SIZE, high // HEAD_SIZE)
            mats = [(decay_of(part, head) * pair).astype(jnp.bfloat16) for head in heads]
            piece = driven[:, low:high]
            right = [
                only(piece, HEAD_SIZE * k, HEAD_SIZE * (k + 1)) if len(mats) > 1 else piece
                for k in range(len(mats))
            ]
            pieces.append(
                mxu(jnp.concatenate(mats, axis=1), jnp.concatenate(right, axis=0), NN)
            )
        state = state_ref[...]
        kept_ref[pl.ds(pl.multiple_of(index * MAMBA_STATES, MAMBA_STATES), MAMBA_STATES), :] = state
        y = jnp.concatenate(pieces, axis=1) + part["live_w"] * mxu(cm, state, NN)
        y = y + skip_ref[0:1, :] * inner
        state_ref[...] = state * part["carry_w"] + mxu(
            bm, driven.astype(jnp.float32) * part["keep_w"], TN
        )
        y_ref[rows, :] = y
        z = z_ref[rows, :width]
        gated = y * z * jax.nn.sigmoid(z)
        square_ref[:, rows] = split_dot_left(gated * gated)
        return 0

    lax.fori_loop(0, length // chunk, one_chunk, 0)


def split_dot_left(values):
    ones = jnp.ones((8, values.shape[1]), jnp.bfloat16)
    high = values.astype(jnp.bfloat16)
    low = (values - high.astype(jnp.float32)).astype(jnp.bfloat16)
    return mxu(ones, high, NT) + mxu(ones, low, NT)


def mamba_backward_kernel(
    chunk, width, block_rows, order_ref, x_ref, bc_ref, raw_ref, doc_ref, w_ref, par_ref, skip_ref, y_ref, dy_ref,
    dkv_ref, kept_ref, din_ref, dw_ref, dpar_ref, pad_ref, state_ref, halo_ref, dskip_ref
):
    length = pad_ref.shape[0] - 8
    count = length // chunk
    wide = x_ref.shape[1]
    common_at = wide + 2 * HEAD_SIZE

    @pl.when(pl.program_id(0) == 0)
    def _():
        if wide > width:
            din_ref[...] = jnp.zeros_like(din_ref)
        din_ref[:, common_at + 2 * MAMBA_STATES :] = dkv_ref[...]

    fill_conv_input(order_ref, block_rows, width, x_ref, bc_ref, pad_ref)
    state_ref[...] = jnp.zeros_like(state_ref)
    halo_ref[...] = jnp.zeros_like(halo_ref)

    @pl.when(pl.program_id(0) == 0)
    def _():
        dw_ref[...] = jnp.zeros_like(dw_ref)
        dpar_ref[...] = jnp.zeros_like(dpar_ref)
        dskip_ref[...] = jnp.zeros_like(dskip_ref)

    def one_chunk(step_index, _):
        index = count - 1 - step_index
        start = pl.multiple_of(index * chunk, chunk)
        rows = pl.ds(place_of(order_ref, block_rows, length, start), chunk)
        part = chunk_common(chunk, start, rows, width, raw_ref, doc_ref, pad_ref, w_ref, par_ref)
        inner = part["act"][:, :width]
        bm = part["act"][:, width : width + MAMBA_STATES].astype(jnp.bfloat16)
        cm = part["act"][:, width + MAMBA_STATES :].astype(jnp.bfloat16)
        driven = (inner * part["step_w"]).astype(jnp.bfloat16)
        driven_f = driven.astype(jnp.float32)
        y = y_ref[rows, :]
        dy = dy_ref[rows, :]
        dy_b = dy.astype(jnp.bfloat16)
        pair = mxu(cm, bm, NT)
        pair_grad = jnp.zeros((chunk, chunk), jnp.float32)
        pieces = []
        for low, high in head_groups(width):
            heads = list(range(low // HEAD_SIZE, high // HEAD_SIZE))
            piece = driven[:, low:high]
            grads = [
                only(dy_b[:, low:high], HEAD_SIZE * k, HEAD_SIZE * (k + 1)) if len(heads) > 1 else dy_b[:, low:high]
                for k in range(len(heads))
            ]
            mats = []
            for k, head in enumerate(heads):
                decay = decay_of(part, head)
                mats.append((decay * pair).astype(jnp.bfloat16))
                pair_grad = pair_grad + decay * mxu(grads[k], piece, NT)
            pieces.append(mxu(jnp.concatenate(mats, axis=0), jnp.concatenate(grads, axis=0), TN))
        within = jnp.concatenate(pieces, axis=1)
        state = kept_ref[pl.ds(pl.multiple_of(index * MAMBA_STATES, MAMBA_STATES), MAMBA_STATES), :]
        state_grad = state_ref[...]
        pair_grad = pair_grad.astype(jnp.bfloat16)
        dy_live = (dy * part["live_w"]).astype(jnp.bfloat16)
        driven_keep = (driven_f * part["keep_w"]).astype(jnp.bfloat16)
        later = part["keep_w"] * mxu(bm, state_grad, NN)
        c_grad = mxu(pair_grad, bm, NN) + mxu(dy_live, state, NT)
        b_grad = mxu(pair_grad, cm, TN) + mxu(driven_keep, state_grad, NT)
        state_ref[...] = state_grad * part["carry_w"] + mxu(cm, dy_live, TN)
        driven_grad = within + later
        later_part = driven_f * later
        mixed = y - skip_ref[0:1, :] * inner
        sums = split_dot(
            jnp.concatenate(
                [
                    dy_b.astype(jnp.float32) * mixed - driven_f * within - later_part,
                    driven_grad * inner,
                    jnp.broadcast_to(
                        jnp.sum(later_part, axis=0, keepdims=True)
                        + part["carry_w"] * jnp.sum(state_grad * state, axis=0, keepdims=True),
                        (8, width),
                    ),
                ],
                axis=0,
            ),
            part["spread"],
            NT,
        )
        high = sums[:chunk].astype(jnp.bfloat16)
        low = (sums[:chunk] - high.astype(jnp.float32)).astype(jnp.bfloat16)
        rate_grad = (
            mxu(part["lower"], high, TN) + mxu(part["lower"], low, TN) + sums[2 * chunk : 2 * chunk + 1]
        )
        step_grad = rate_grad * par_ref[1:2, :] + sums[chunk : 2 * chunk]
        raw_grad = step_grad * jax.nn.sigmoid(part["raw"])
        din_ref[rows, wide:common_at] = raw_grad.astype(jnp.bfloat16)
        dpar_ref[0:1, :] += jnp.sum(raw_grad, axis=0, keepdims=True)
        dpar_ref[1:2, :] += par_ref[1:2, :] * jnp.sum(rate_grad * part["step"], axis=0, keepdims=True)
        dskip_ref[0:1, :] += jnp.sum(dy * inner, axis=0, keepdims=True)
        inner_grad = driven_grad * part["step_w"] + skip_ref[0:1, :] * dy
        sig, conv = (part["sig"], part["conv"])
        conv_grad = jnp.concatenate([inner_grad, b_grad, c_grad], axis=1) * (
            sig * (1.0 + conv * (1.0 - sig))
        )
        dw_ref[CONV : CONV + 1, :] += jnp.sum(conv_grad, axis=0, keepdims=True)
        v_grad = w_ref[CONV - 1 : CONV, :] * conv_grad
        long = jnp.concatenate([conv_grad, halo_ref[...]], axis=0)
        next_start = jnp.minimum(start + chunk, length - 8)
        ages = jnp.concatenate([part["age"], start + chunk + iota((8, 1), 0) - doc_ref[pl.ds(pl.multiple_of(next_start, 8), 8), :]], axis=0)
        dw_ref[CONV - 1 : CONV, :] += jnp.sum(conv_grad * part["lagged"][0], axis=0, keepdims=True)
        for lag in range(1, CONV):
            dw_ref[CONV - 1 - lag : CONV - lag, :] += jnp.sum(
                conv_grad * part["lagged"][lag], axis=0, keepdims=True
            )
            masked = jnp.where(ages >= lag, long, 0.0)
            v_grad = v_grad + w_ref[CONV - 1 - lag : CONV - lag, :] * masked[lag : lag + chunk, :]
        halo_ref[...] = conv_grad[:8, :]
        din_ref[rows, :width] = v_grad[:, :width].astype(jnp.bfloat16)
        din_ref[rows, common_at : common_at + 2 * MAMBA_STATES] = v_grad[:, width:].astype(jnp.bfloat16)
        return 0

    lax.fori_loop(0, count, one_chunk, 0)

    @pl.when(pl.program_id(0) == pl.num_programs(0) - 1)
    def _():
        lanes = dpar_ref.shape[1]
        spread = (iota((lanes, width), 0) == iota((lanes, width), 1) // HEAD_SIZE).astype(jnp.bfloat16)
        dpar_ref[2:3, :] = split_dot(dskip_ref[...], spread, NT)[0:1]


CHUNK = 128
VMEM_LIMIT = 60 * 1024 * 1024


def tokens_spec(tokens, width, place=0):
    return pl.BlockSpec((tokens, width), lambda i, *_: (0, place))


def whole_spec(shape):
    return pl.BlockSpec(shape, lambda i, *_: (0,) * len(shape))


def mamba_forward(order, block_rows, early, late, common, doc, taps, params, skip_row, chunk=CHUNK):
    tokens = late.shape[0]
    width = skip_row.shape[1]
    lanes = params.shape[1]
    wide = late.shape[1] - lanes
    seq = SEQUENCE_TOKENS
    count = tokens // seq
    kept = seq // chunk * MAMBA_STATES
    return pl.pallas_call(
        functools.partial(mamba_forward_kernel, chunk, width, block_rows),
        grid_spec=pltpu.PrefetchScalarGridSpec(
        num_scalar_prefetch=1,
        grid=(count,),
        in_specs=[
            tokens_spec(tokens, wide),
            tokens_spec(tokens, 2 * MAMBA_STATES),
            tokens_spec(tokens, lanes, wide // lanes),
            tokens_spec(tokens, wide),
            pl.BlockSpec((seq, 1), lambda i, *_: (i, 0)),
            whole_spec(taps.shape),
            whole_spec(params.shape),
            whole_spec(skip_row.shape),
        ],
        out_specs=[
            tokens_spec(tokens, width),
            whole_spec((8, tokens)),
            pl.BlockSpec((kept, width), lambda i, *_: (i, 0)),
        ],
        scratch_shapes=[
            pltpu.VMEM((seq + 8, width + 2 * MAMBA_STATES), jnp.float32),
            pltpu.VMEM((MAMBA_STATES, width), jnp.float32),
        ],
        ),
        out_shape=[
            jax.ShapeDtypeStruct((tokens, width), jnp.float32),
            jax.ShapeDtypeStruct((8, tokens), jnp.float32),
            jax.ShapeDtypeStruct((count * kept, width), jnp.float32),
        ],
        compiler_params=pltpu.CompilerParams(vmem_limit_bytes=VMEM_LIMIT),
        cost_estimate=pl.CostEstimate(
            flops=tokens * width * 20000, bytes_accessed=tokens * width * 20, transcendentals=0
        ),
    )(order, late, common, late, early, doc, taps, params, skip_row)


def mamba_backward(
    order, block_rows, late, common, doc, taps, params, skip_row, y, dy, dkv, kept_states, chunk=CHUNK
):
    tokens = late.shape[0]
    width = skip_row.shape[1]
    lanes = params.shape[1]
    wide = late.shape[1] - lanes
    seq = SEQUENCE_TOKENS
    count = tokens // seq
    kept = seq // chunk * MAMBA_STATES
    conv_width = width + 2 * MAMBA_STATES
    return pl.pallas_call(
        functools.partial(mamba_backward_kernel, chunk, width, block_rows),
        grid_spec=pltpu.PrefetchScalarGridSpec(
        num_scalar_prefetch=1,
        grid=(count,),
        in_specs=[
            tokens_spec(tokens, wide),
            tokens_spec(tokens, 2 * MAMBA_STATES),
            tokens_spec(tokens, lanes, wide // lanes),
            pl.BlockSpec((seq, 1), lambda i, *_: (i, 0)),
            whole_spec(taps.shape),
            whole_spec(params.shape),
            whole_spec(skip_row.shape),
            tokens_spec(tokens, width),
            tokens_spec(tokens, width),
            tokens_spec(tokens, dkv.shape[1]),
            pl.BlockSpec((kept, width), lambda i, *_: (i, 0)),
        ],
        out_specs=[
            tokens_spec(tokens, late.shape[1] + common.shape[1]),
            whole_spec((8, conv_width)),
            whole_spec((8, lanes)),
        ],
        scratch_shapes=[
            pltpu.VMEM((seq + 8, conv_width), jnp.float32),
            pltpu.VMEM((MAMBA_STATES, width), jnp.float32),
            pltpu.VMEM((8, conv_width), jnp.float32),
            pltpu.VMEM((8, width), jnp.float32),
        ],
        ),
        out_shape=[
            jax.ShapeDtypeStruct((tokens, late.shape[1] + common.shape[1]), jnp.bfloat16),
            jax.ShapeDtypeStruct((8, conv_width), jnp.float32),
            jax.ShapeDtypeStruct((8, lanes), jnp.float32),
        ],
        compiler_params=pltpu.CompilerParams(vmem_limit_bytes=VMEM_LIMIT),
        cost_estimate=pl.CostEstimate(
            flops=tokens * width * 60000, bytes_accessed=tokens * width * 20, transcendentals=0
        ),
    )(
        order, late, common, late, doc, taps, params, skip_row, y, dy, dkv, kept_states
    )


NEGATIVE = -1e30
QUERY_BLOCK = 256


def swap_halves(values):
    half = HEAD_SIZE // 2
    lane = iota(values.shape, 1)
    width = values.shape[1]
    return jnp.where(
        lane % HEAD_SIZE < half,
        pltpu.roll(values, width - half, 1),
        pltpu.roll(values, half, 1),
    )


def attention_mask(start, rows, keys, doc):
    position = start + iota((rows, 1), 0)
    key_pos = iota((rows, keys), 1)
    return (key_pos <= position) & (key_pos >= doc)


def both_heads(values):
    return jnp.concatenate(
        [only(values, 0, HEAD_SIZE), only(values, HEAD_SIZE, 2 * HEAD_SIZE)], axis=0
    )


def chosen(values, kv):
    lane = iota(values.shape, 1)
    turned = pltpu.roll(values, HEAD_SIZE, 1)
    return jnp.where((lane < HEAD_SIZE) == (kv == 0), values, turned)


def attention_forward_kernel(
    block_rows, kv_ref, order_ref, q_ref, key_ref, value_ref, cos_ref, sin_ref, doc_ref, out_ref, qr_ref, kr_ref, vr_ref, log_ref
):
    length = qr_ref.shape[0]
    kv = kv_ref[0]
    rows = block_rows
    for start in range(0, length, rows):
        block = slice(start, start + rows)
        place = pl.ds(place_of(order_ref, block_rows, length, start), rows)
        cos, sin = (cos_ref[block, :], sin_ref[block, :])
        query, key = (q_ref[place, :], key_ref[place, :])
        turned = (query * cos + swap_halves(query) * sin).astype(jnp.bfloat16)
        qr_ref[block, :] = (turned.astype(jnp.float32) * HEAD_SIZE**-0.5).astype(jnp.bfloat16)
        kr_ref[block, :] = chosen(key * cos + swap_halves(key) * sin, kv).astype(jnp.bfloat16)
        vr_ref[block, :] = chosen(value_ref[place, :], kv).astype(jnp.bfloat16)
        keys = start + rows
        mask = attention_mask(start, rows, keys, doc_ref[block, :])
        scores = mxu(both_heads(qr_ref[block, :]), kr_ref[0:keys, :], NT)
        outs = []
        logs = []
        for head in range(2):
            part = jnp.where(mask, scores[head * rows : (head + 1) * rows], NEGATIVE)
            peak = jnp.max(part, axis=1, keepdims=True)
            weight = jnp.exp(part - peak)
            total = jnp.sum(weight, axis=1, keepdims=True)
            outs.append(mxu(weight * (1.0 / total), vr_ref[0:keys, :], NN))
            logs.append(peak + jnp.log(total))
        lane = iota((rows, 2 * HEAD_SIZE), 1)
        out_ref[place, :] = jnp.where(lane < HEAD_SIZE, outs[0], outs[1]).astype(jnp.bfloat16)
        log_ref[block, :] = jnp.where(lane < HEAD_SIZE, logs[0], logs[1])


def attention_backward_kernel(
    block_rows, kv_ref, order_ref, qr_ref, kr_ref, vr_ref, cos_ref, sin_ref, doc_ref, log_ref, grad_ref, dq_ref, dkv_ref, dk_ref, dv_ref
):
    length = qr_ref.shape[0]
    kv = kv_ref[0]
    rows = block_rows
    lane = iota((rows, 2 * HEAD_SIZE), 1)
    mine = (lane < HEAD_SIZE) == (kv == 0)
    dk_ref[...] = jnp.zeros_like(dk_ref)
    dv_ref[...] = jnp.zeros_like(dv_ref)
    for start in reversed(range(0, length, rows)):
        keys = start + rows
        block = slice(start, start + rows)
        place = pl.ds(place_of(order_ref, block_rows, length, start), rows)
        mask = attention_mask(start, rows, keys, doc_ref[block, :])
        query = both_heads(qr_ref[block, :])
        grad = both_heads(grad_ref[place, :].astype(jnp.bfloat16))
        logs = log_ref[block, :]
        scores = mxu(query, kr_ref[0:keys, :], NT)
        prob_grad = mxu(grad, vr_ref[0:keys, :], NT)
        probs = []
        score_grads = []
        for head in range(2):
            part = slice(head * rows, (head + 1) * rows)
            log = logs[:, head * HEAD_SIZE : head * HEAD_SIZE + 1]
            weight = jnp.where(mask, jnp.exp(scores[part] - log), 0.0)
            product_grad = weight * prob_grad[part]
            total = jnp.sum(product_grad, axis=1, keepdims=True)
            probs.append(weight.astype(jnp.bfloat16))
            score_grads.append((product_grad - weight * total).astype(jnp.bfloat16))
        cos, sin = (cos_ref[block, :], sin_ref[block, :])
        dq = mxu(jnp.concatenate(score_grads, axis=0), kr_ref[0:keys, :], NN)
        dq = jnp.where(lane < HEAD_SIZE, dq[:rows], dq[rows:]) * HEAD_SIZE**-0.5
        dq = dq * cos - swap_halves(dq) * sin
        dq_ref[place, :] = dq.astype(jnp.bfloat16)
        dk_ref[0:keys, :] += mxu(jnp.concatenate(score_grads, axis=0), query, TN)
        dv_ref[0:keys, :] += mxu(jnp.concatenate(probs, axis=0), grad, TN)
        dk = dk_ref[block, :]
        dk = dk + pltpu.roll(dk, HEAD_SIZE, 1)
        dk = dk * cos - swap_halves(dk) * sin
        dv = dv_ref[block, :]
        dv = dv + pltpu.roll(dv, HEAD_SIZE, 1)
        dkv_ref[place, : 2 * HEAD_SIZE] = jnp.where(mine, dk, 0.0).astype(jnp.bfloat16)
        dkv_ref[place, 2 * HEAD_SIZE :] = jnp.where(mine, dv, 0.0).astype(jnp.bfloat16)


def attention_call(kernel, kv, order, block_rows, tokens, ins, outs, scratch, flops):
    seq = SEQUENCE_TOKENS

    def spec(columns, place):
        if place is None:
            return pl.BlockSpec((seq, columns), lambda i, *_: (i, 0))
        return tokens_spec(tokens, columns, place)

    return pl.pallas_call(
        functools.partial(kernel, block_rows),
        grid_spec=pltpu.PrefetchScalarGridSpec(
            num_scalar_prefetch=2,
            grid=(tokens // seq,),
            in_specs=[spec(columns, place) for _, columns, place in ins],
            out_specs=[spec(columns, place) for _, columns, place in outs],
            scratch_shapes=scratch,
        ),
        out_shape=[jax.ShapeDtypeStruct((tokens, columns), kind) for kind, columns, _ in outs],
        compiler_params=pltpu.CompilerParams(vmem_limit_bytes=VMEM_LIMIT),
        cost_estimate=pl.CostEstimate(
            flops=flops * tokens, bytes_accessed=tokens * 4096, transcendentals=0
        ),
    )(kv, order, *[value for value, _, _ in ins])


def attention_forward(kv, order, block_rows, early, common, cos, sin, doc):
    two = 2 * HEAD_SIZE
    low, full = (jnp.bfloat16, jnp.float32)
    query_at = early.shape[1] // two - 1
    key_at = 2 * MAMBA_STATES // two
    return attention_call(
        attention_forward_kernel,
        kv,
        order,
        block_rows,
        early.shape[0],
        (
            (early, two, query_at),
            (common, two, key_at),
            (common, two, key_at + 1),
            (cos, two, None),
            (sin, two, None),
            (doc, 1, None),
        ),
        ((low, two, 0), (low, two, None), (low, two, None), (low, two, None), (full, two, None)),
        [],
        4000000,
    )


def attention_backward(kv, order, block_rows, qr, kr, vr, cos, sin, doc, log, grad, grad_at):
    two = 2 * HEAD_SIZE
    seq = SEQUENCE_TOKENS
    return attention_call(
        attention_backward_kernel,
        kv,
        order,
        block_rows,
        qr.shape[0],
        (
            (qr, two, None),
            (kr, two, None),
            (vr, two, None),
            (cos, two, None),
            (sin, two, None),
            (doc, 1, None),
            (log, two, None),
            (grad, two, grad_at),
        ),
        ((jnp.bfloat16, two, 0), (jnp.bfloat16, 2 * two, 0)),
        [pltpu.VMEM((seq, two), jnp.float32), pltpu.VMEM((seq, two), jnp.float32)],
        9000000,
    )


def weight_grad_kernel(count, with_back, *refs):
    lefts, rights = (refs[:count], refs[count : 2 * count])
    rest = refs[2 * count :]
    out_ref = rest[-3] if with_back else rest[-1]
    spot = 0
    for left, right in zip(lefts, rights):
        grad = mxu(left[...], right[...], TN)
        columns = right.shape[1]
        out_ref[:, spot : spot + columns] = grad.astype(jnp.bfloat16)
        spot += columns
    if with_back:
        w_ref = rest[0]
        part = mxu(rights[-1][...], w_ref[...], NT)
        if len(rest) > 4:
            part = part + rest[1][...].astype(jnp.float32)
        rest[-2][...] = part.astype(rest[-2].dtype)
        rest[-1][...] = jnp.sum(grad * w_ref[...].astype(jnp.float32), axis=1, keepdims=True)


def weight_grads(pairs, back=None, base=None, kind=jnp.bfloat16):
    tokens, rows = pairs[0][0].shape
    total = sum(right.shape[1] for _, right in pairs)
    block = min(rows, 512)
    ins = [left for left, _ in pairs] + [right for _, right in pairs]
    specs = [pl.BlockSpec((tokens, block), lambda i: (0, i)) for _ in pairs]
    specs += [pl.BlockSpec((tokens, right.shape[1]), lambda i: (0, 0)) for _, right in pairs]
    outs = [jax.ShapeDtypeStruct((rows, total), jnp.bfloat16)]
    out_specs = [pl.BlockSpec((block, total), lambda i: (i, 0))]
    flops = 2 * tokens * rows * total
    if back is not None:
        weight, place = back
        ins.append(weight)
        specs.append(pl.BlockSpec((block, pairs[-1][1].shape[1]), lambda i: (i, place)))
        if base is not None:
            ins.append(base)
            specs.append(pl.BlockSpec((tokens, block), lambda i: (0, i)))
        outs += [
            jax.ShapeDtypeStruct((tokens, rows), kind),
            jax.ShapeDtypeStruct((rows, 1), jnp.float32),
        ]
        out_specs += [
            pl.BlockSpec((tokens, block), lambda i: (0, i)),
            pl.BlockSpec((block, 1), lambda i: (i, 0)),
        ]
        flops += 2 * tokens * rows * pairs[-1][1].shape[1]
    result = pl.pallas_call(
        functools.partial(weight_grad_kernel, len(pairs), back is not None),
        grid=(rows // block,),
        in_specs=specs,
        out_specs=out_specs,
        out_shape=outs,
        compiler_params=pltpu.CompilerParams(vmem_limit_bytes=VMEM_LIMIT),
        cost_estimate=pl.CostEstimate(
            flops=flops, bytes_accessed=4 * tokens * rows + 2 * rows * total, transcendentals=0
        ),
    )(*ins)
    return result if back is not None else result[0]


def feed_forward_kernel(hidden_width, x_ref, cot_ref, w_ref, grad_ref, hidden_ref, back_ref, out_ref):
    wide = 2 * hidden_width
    acts = mxu(x_ref[...], w_ref[:, :wide], NN)
    hidden_grad = mxu(cot_ref[...], w_ref[:, wide:], NN)
    gate, up = (acts[:, :hidden_width], acts[:, hidden_width:])
    sig = jax.nn.sigmoid(gate)
    silu = gate * sig
    grads = jnp.concatenate(
        [hidden_grad * up * (sig * (1.0 + gate * (1.0 - sig))), hidden_grad * silu], axis=1
    ).astype(jnp.bfloat16)
    grad_ref[...] = grads
    back_ref[...] = mxu(grads, w_ref[:, :wide], NT).astype(jnp.bfloat16)
    hidden = (silu * up).astype(jnp.bfloat16)
    hidden_ref[...] = hidden
    out_ref[...] = mxu(hidden, w_ref[:, wide:], NT).astype(jnp.bfloat16)


def feed_forward(x, cot, weights, rows):
    tokens, width = x.shape
    hidden_width = weights.shape[1] // 3
    by_rows = lambda columns: pl.BlockSpec((rows, columns), lambda i: (i, 0))
    sizes = (2 * hidden_width, hidden_width, width, width)
    return pl.pallas_call(
        functools.partial(feed_forward_kernel, hidden_width),
        grid=(tokens // rows,),
        in_specs=[by_rows(width), by_rows(width), pl.BlockSpec(weights.shape, lambda i: (0, 0))],
        out_specs=[by_rows(columns) for columns in sizes],
        out_shape=[jax.ShapeDtypeStruct((tokens, columns), jnp.bfloat16) for columns in sizes],
        compiler_params=pltpu.CompilerParams(vmem_limit_bytes=VMEM_LIMIT),
        cost_estimate=pl.CostEstimate(
            flops=12 * tokens * width * hidden_width,
            bytes_accessed=14 * tokens * width,
            transcendentals=0,
        ),
    )(x, cot, weights)


def finish_kernel(valid_ref, x_ref, mixer_ref, middle_ref, ffn_ref, out_ref, stat_ref):
    valid = valid_ref[...]
    middle, ffn = (middle_ref[...], ffn_ref[...])
    result = middle + ffn
    out_ref[...] = result.astype(jnp.bfloat16)
    tracked = (x_ref[...].astype(jnp.float32), mixer_ref[...], middle, ffn, result)
    stat_ref[...] = jnp.zeros_like(stat_ref)
    for k, values in enumerate(tracked):
        stat_ref[k : k + 1, 0:1] = jnp.sum(
            valid * jnp.sum(values * values, axis=1, keepdims=True), axis=0, keepdims=True
        )
    stat_ref[len(tracked) : len(tracked) + 1, 0:1] = jnp.sum(valid, axis=0, keepdims=True)


def finish(valid, x, mixer_sum, middle, ffn_out):
    return pl.pallas_call(
        finish_kernel,
        out_shape=[
            jax.ShapeDtypeStruct(x.shape, jnp.bfloat16),
            jax.ShapeDtypeStruct((8, 128), jnp.float32),
        ],
        compiler_params=pltpu.CompilerParams(vmem_limit_bytes=VMEM_LIMIT),
        cost_estimate=pl.CostEstimate(flops=16 * x.size, bytes_accessed=16 * x.size, transcendentals=0),
    )(valid, x, mixer_sum, middle, ffn_out)


def passengers(stages, *values):
    for _ in range(stages):
        yield []
    return (yield list(values))


def rope_rows(position):
    lane = jnp.arange(2 * HEAD_SIZE, dtype=jnp.int32)
    half = HEAD_SIZE // 2
    inverse = jnp.exp(
        (lane % half).astype(jnp.float32) * (-2.0 * math.log(ROPE_BASE) / HEAD_SIZE)
    )
    angles = position.astype(jnp.float32)[:, None] * inverse[None, :]
    sign = jnp.where(lane % HEAD_SIZE < half, -1.0, 1.0)
    return (jnp.cos(angles), jnp.sin(angles) * sign[None, :])
def grid_of(count):
    rows = 1
    while 8 * rows * rows <= count:
        rows *= 2
    return (count // rows, rows)


def ring_cycle(count):
    depth, rows = grid_of(count)
    order = []
    for level in range(depth):
        inner = list(range(1, rows))
        if level % 2:
            inner.reverse()
        order += [level * rows + row for row in inner]
    return order + [level * rows for level in reversed(range(depth))]


class Ring:
    def __init__(self, count):
        self.count = count
        self.order = ring_cycle(count)
        self.depth, self.rows = grid_of(count)
        inner = self.rows - 1
        mine = lax.axis_index("dp")
        level, row = (mine // self.rows, mine % self.rows)
        step = jnp.where(level % 2 == 0, row - 1, inner - row)
        self.spot = jnp.where(
            row > 0, level * inner + step, self.depth * inner + self.depth - 1 - level
        )

    def device_at(self, offset):
        inner = self.rows - 1
        spot = (self.spot + offset + self.count) % self.count
        level, step = (spot // inner, spot % inner)
        row = jnp.where(level % 2 == 0, step + 1, inner - step)
        back = self.count - 1 - spot
        return jnp.where(spot < self.depth * inner, level * self.rows + row, back * self.rows)

    def send(self, block, step):
        count, order = (self.count, self.order)
        return lax.ppermute(
            block, "dp", [(order[k], order[(k + step) % count]) for k in range(count)]
        )


def together(*values):
    return lax.optimization_barrier(values)


def lockstep(*chains):
    results = [None] * len(chains)
    waiting = {k: None for k in range(len(chains))}
    while waiting:
        sent = {}
        for k in list(waiting):
            try:
                sent[k] = chains[k].send(waiting[k])
            except StopIteration as stop:
                results[k] = stop.value
                del waiting[k]
        flat = [value for k in sent for value in sent[k]]
        if len(flat) > 1:
            flat = list(together(*flat))
        for k in sent:
            waiting[k] = flat[: len(sent[k])]
            flat = flat[len(sent[k]) :]
    return results


def after_stages(count, chain):
    for _ in range(count):
        yield []
    return (yield from chain)


def ring_gather(ring, block):
    count = ring.count
    rows = block.shape[0]
    half = rows // 2
    out = jnp.zeros((count * rows,) + block.shape[1:], block.dtype)

    def put(out, piece, offset, extra=0):
        return lax.dynamic_update_slice_in_dim(
            out, piece, ring.device_at(offset) * rows + extra, 0
        )

    out = put(out, block, 0)
    ahead = behind = block
    for step in range(1, count // 2):
        ahead, behind = yield [ring.send(ahead, 1), ring.send(behind, -1)]
        out = put(out, ahead, -step)
        out = put(out, behind, step)
    ahead, behind = yield [ring.send(ahead[:half], 1), ring.send(behind[half:], -1)]
    return put(put(out, ahead, -(count // 2)), behind, count // 2, half)


def ring_scatter(ring, *parts):
    count = ring.count
    rows = parts[0].shape[0] // count
    half = rows // 2

    def piece(offset, start=0, size=rows):
        first = ring.device_at(offset) * rows + start
        return jnp.concatenate(
            [lax.dynamic_slice_in_dim(part, first, size, 0).astype(jnp.float32) for part in parts],
            axis=1,
        )

    far = count // 2
    ahead = piece(far, 0, half).astype(jnp.bfloat16)
    behind = piece(far, half, rows - half).astype(jnp.bfloat16)
    for offset in range(far - 1, -1, -1):
        ahead, behind = yield [ring.send(ahead, 1), ring.send(behind, -1)]
        ahead, behind = (ahead.astype(jnp.float32), behind.astype(jnp.float32))
        if offset == far - 1:
            ahead, behind = (
                jnp.concatenate([ahead, jnp.zeros_like(behind)], axis=0),
                jnp.concatenate([jnp.zeros_like(ahead), behind], axis=0),
            )
        if offset:
            ahead = (ahead + piece(offset)).astype(jnp.bfloat16)
            behind = (behind + piece(-offset)).astype(jnp.bfloat16)
    return ahead + behind + piece(0)


def core_swap(block):
    count = lax.axis_size("tensor")
    return lax.ppermute(block, "tensor", [(k, k ^ 1) for k in range(count)])


def chip_shift(block, step):
    count = lax.axis_size("tensor")
    return lax.ppermute(block, "tensor", [(k, (k + 2 * step) % count) for k in range(count)])


def tensor_parts(block):
    chips = lax.axis_size("tensor") // 2
    mate, *others = yield [core_swap(block)] + [chip_shift(block, k) for k in range(1, chips)]
    mates = yield [core_swap(other) for other in others]
    parts = [block, mate]
    for other, beside in zip(others, mates):
        parts += [other, beside]
    return parts


def in_order(parts):
    chips = len(parts) // 2
    mine = lax.axis_index("tensor")
    flipped = mine % 2 == 1
    pairs = []
    for chip in range(chips):
        first, second = (parts[2 * chip], parts[2 * chip + 1])
        pairs.append((jnp.where(flipped, second, first), jnp.where(flipped, first, second)))
    out = []
    for chip in range(chips):
        back = (mine // 2 + chips - chip) % chips
        for core in range(2):
            value = pairs[0][core]
            for step in range(1, chips):
                value = jnp.where(back == step, pairs[step][core], value)
            out.append(value)
    return out


def seq_gather(values):
    parts = yield from tensor_parts(values)
    return jnp.concatenate(parts, axis=0)


def tensor_scatter(pick):
    chips = lax.axis_size("tensor") // 2
    places = [2 * (chips - step) for step in range(1, chips)]
    mate, *others = yield [core_swap(pick(place + 1)) for place in [0] + places]
    merged = [
        (pick(place).astype(jnp.float32) + other.astype(jnp.float32)).astype(jnp.bfloat16)
        for place, other in zip(places, others)
    ]
    received = yield [chip_shift(value, k + 1) for k, value in enumerate(merged)]
    total = pick(0).astype(jnp.float32) + mate.astype(jnp.float32)
    for other in received:
        total = total + other.astype(jnp.float32)
    return total


def seq_reduce(lowered):
    rows = lowered.shape[0] // lax.axis_size("tensor")
    return tensor_scatter(lambda place: lowered[place * rows : (place + 1) * rows])


def width_total(values):
    chips = lax.axis_size("tensor") // 2
    blocks = values.reshape(chips, 2, -1)
    blocks = blocks + core_swap(blocks)[:, ::-1]
    total = blocks
    for step in range(1, chips):
        total = total + jnp.roll(chip_shift(blocks, step), step, axis=0)
    return total.reshape(values.shape)


def exchange(blocks, axes):
    return lax.all_to_all(blocks, axes, 0, 0, tiled=False)


def dp_scatter(values):
    blocks = values.astype(jnp.bfloat16).reshape((lax.axis_size("dp"), -1) + values.shape[1:])
    return jnp.sum(exchange(blocks, "dp").astype(jnp.float32), axis=0)


def run(chain):
    return lockstep(chain)[0]


def local(
    layer_input,
    out_grad,
    segment_ids,
    valid_mask,
    doc_start,
    norm_gains,
    conv_weight,
    conv_bias,
    mixer_gain,
    shared_proj,
    step_bias,
    decay_log,
    skip_gain,
    mamba_gate,
    mamba_input,
    mamba_step,
    query_proj,
    mamba_out,
    attention_out,
    swiglu_gate,
    swiglu_up,
    swiglu_down,
):
    tensor_position = lax.axis_index("tensor")
    dp_count = lax.axis_size("dp")
    tensor_count = lax.axis_size("tensor")
    device = lax.axis_index("dp") * tensor_count + tensor_position
    ring = Ring(dp_count)
    local_width = mamba_gate.shape[1]
    query_width = query_proj.shape[1]
    head_local = mamba_step.shape[1]
    hidden_width = swiglu_gate.shape[1]
    query_slice = query_width // HEAD_SIZE
    slab = 2 * HEAD_SIZE
    wide = -(-local_width // slab) * slab
    early_width = wide + slab
    block_rows = layer_input.shape[0]
    tokens_per_group = block_rows * tensor_count
    seq_count = tokens_per_group // SEQUENCE_TOKENS
    channel_start = tensor_position * local_width
    head_start = tensor_position * head_local
    channels = conv_weight.shape[1] * dp_count * tensor_count

    def padded(values, columns):
        return jnp.pad(values, ((0, 0), (0, columns - values.shape[1])))

    def placed(rows_in, columns, start):
        whole = jnp.zeros((rows_in.shape[0], columns), rows_in.dtype)
        return lax.dynamic_update_slice_in_dim(whole, rows_in, start, 1)

    device_count = dp_count * tensor_count
    small = jnp.concatenate(
        [norm_gains.reshape(-1), conv_weight.reshape(-1), conv_bias, mixer_gain]
    )
    small_width = -(-small.shape[0] // 128) * 128
    small = jnp.pad(small, (0, small_width - small.shape[0]))
    small_all = exchange(
        jnp.broadcast_to(small[None], (device_count, small_width)), ("dp", "tensor")
    )
    shared_own = lax.all_gather(shared_proj, "tensor", axis=0, tiled=True)
    valid_f = valid_mask.astype(jnp.float32)
    out_cot = out_grad.astype(jnp.float32) * valid_f[:, None]
    layer_input, shared_own = together(layer_input, shared_own)
    x_full, w_in, ffn_grad_in, waited = lockstep(
        seq_gather(layer_input),
        ring_gather(
            ring,
            jnp.concatenate(
                [
                    padded(mamba_gate, wide),
                    padded(query_proj, slab),
                    mamba_out.T,
                    attention_out.T,
                    padded(mamba_input, wide),
                    padded(mamba_step, slab),
                    shared_own,
                ],
                axis=1,
            ),
        ),
        after_stages(2, seq_gather(out_cot.astype(jnp.bfloat16))),
        passengers(1, doc_start, swiglu_gate, swiglu_up, swiglu_down),
    )
    doc_start, swiglu_gate, swiglu_up, swiglu_down = waited
    ffn_block, w_in = together(
        jnp.concatenate([swiglu_gate, swiglu_up, swiglu_down.T], axis=1), w_in
    )
    shared_at = w_in.shape[1] - shared_proj.shape[1]
    late_at = early_width + local_width + query_width
    w_early, w_out, w_late, shared_w = (
        w_in[:, :early_width],
        w_in[:, early_width:late_at],
        w_in[:, late_at:shared_at],
        w_in[:, shared_at:],
    )
    w_ffn = lax.all_gather(ffn_block, "dp", axis=0, tiled=True)
    cuts = []
    spot = 0
    for piece in (norm_gains, conv_weight, conv_bias[None], mixer_gain[None]):
        taken = small_all[:, spot : spot + piece.size].astype(jnp.float32)
        cuts.append(jnp.swapaxes(taken.reshape((-1,) + piece.shape), 0, 1).reshape(piece.shape[0], -1))
        spot += piece.size
    gains_f = cuts[0]
    conv_f = jnp.concatenate(cuts[1:3], axis=0)
    mixer_gain_f = cuts[3][0]
    tokens_f = layer_input.astype(jnp.float32)
    scale_one = rms_scale(tokens_f)
    x_wide = x_full.astype(jnp.float32)
    first_full = (x_wide * rms_scale(x_wide) * gains_f[0]).astype(jnp.bfloat16)
    taps = jnp.concatenate(
        [lax.dynamic_slice_in_dim(conv_f, channel_start, local_width, 1), conv_f[:, DSSM:]], axis=1
    )
    taps = jnp.pad(taps, ((0, 3), (0, 0)))
    own_gain = lax.dynamic_slice_in_dim(mixer_gain_f, channel_start, local_width, 0)
    own_bias = lax.dynamic_slice_in_dim(step_bias, head_start, head_local, 0)
    own_decay = lax.dynamic_slice_in_dim(decay_log, head_start, head_local, 0)
    own_skip = lax.dynamic_slice_in_dim(skip_gain, head_start, head_local, 0)
    params = jnp.pad(
        jnp.stack([own_bias, -jnp.exp(own_decay)], axis=0), ((0, 6), (0, slab - head_local))
    )
    skip_row = jnp.broadcast_to(jnp.repeat(own_skip, HEAD_SIZE)[None], (8, local_width))
    doc = doc_start[:, None]
    position = jnp.tile(jnp.arange(SEQUENCE_TOKENS, dtype=jnp.int32), seq_count) - doc_start
    cosine_table, sine_table = rope_rows(position)
    kv = (tensor_position * query_slice // (QUERY_HEADS // KEY_VALUE_HEADS)).astype(jnp.int32)[None]
    device_ids = jnp.arange(tensor_count, dtype=jnp.int32)
    chip_count = tensor_count // 2
    block_order = (tensor_position // 2 + chip_count - device_ids // 2) % chip_count * 2 + (
        tensor_position + device_ids
    ) % 2

    late_act = product(first_full, w_late)
    common_act = product(first_full, shared_w)
    early_act = product(first_full, w_early)
    mamba_y, square_rows, kept_states = mamba_forward(
        block_order, block_rows, early_act, late_act, common_act, doc, taps, params, skip_row
    )
    attended, query_rot, key_rot, value_low, log_total = attention_forward(
        kv, block_order, block_rows, early_act, common_act, cosine_table, sine_table, doc
    )
    square_sum = width_total(square_rows[0])
    gate_scale = lax.rsqrt(square_sum / DSSM + EPS)[:, None]
    gate_z = early_act[:, :local_width]
    sigmoid_z = jax.nn.sigmoid(gate_z)
    silu_z = gate_z * sigmoid_z
    gated_y = mamba_y * silu_z
    normed_b = (gated_y * gate_scale * own_gain).astype(jnp.bfloat16)
    mixed_b = jnp.concatenate([normed_b, attended[:, :query_width]], axis=1)
    mixer_sum = run(seq_reduce(product_nt(mixed_b, w_out).astype(jnp.bfloat16)))

    middle = tokens_f + mixer_sum
    scale_two = rms_scale(middle)
    second_b = (middle * scale_two * gains_f[1]).astype(jnp.bfloat16)
    ffn_in = run(seq_gather(second_b))
    gate_up_grad, hidden_b, second_part, ffn_part = feed_forward(
        ffn_in, ffn_grad_in, w_ffn, block_rows
    )
    ffn_in, ffn_grad_in, second_part = together(ffn_in, ffn_grad_in, second_part)
    second_grad = run(seq_reduce(second_part))
    ffn_w_grad = weight_grads(((ffn_in, gate_up_grad), (ffn_grad_in, hidden_b)))
    second_value_grad, gain_two_grad = norm_back(middle, scale_two, gains_f[1], second_grad)
    middle_grad = out_cot + second_value_grad
    middle_grad, ffn_w_grad = together(middle_grad, ffn_w_grad)
    ffn_w_grad = lax.psum_scatter(ffn_w_grad, "dp", scatter_dimension=0, tiled=True).astype(
        jnp.float32
    )
    gate_w_grad = ffn_w_grad[:, :hidden_width]
    up_w_grad = ffn_w_grad[:, hidden_width : 2 * hidden_width]
    down_w_grad = ffn_w_grad[:, 2 * hidden_width :].T

    mixer_grad_full = run(seq_gather(middle_grad.astype(jnp.bfloat16)))
    ffn_part, mixer_grad_full = together(ffn_part, mixer_grad_full)
    mixed_grad = product(mixer_grad_full, w_out)
    normed_grad = mixed_grad[:, :local_width]
    scaled_normed = normed_grad * own_gain
    inner_sum = width_total(jnp.sum(scaled_normed * gated_y, axis=1))
    attended_grad, attended_at = (mixed_grad, local_width // slab)
    if local_width % slab or query_width != slab:
        attended_grad, attended_at = (padded(mixed_grad[:, local_width:], slab), 0)
    out_total = dp_scatter(weight_grads(((mixer_grad_full, mixed_b),)))
    dq, dkv = attention_backward(
        kv,
        block_order,
        block_rows,
        query_rot,
        key_rot,
        value_low,
        cosine_table,
        sine_table,
        doc,
        log_total,
        attended_grad,
        attended_at,
    )
    own_gain_grad = jnp.sum(normed_grad * gated_y * gate_scale, axis=0)
    gated_grad = (
        gate_scale * scaled_normed
        - gated_y * (gate_scale * gate_scale * gate_scale) * (inner_sum / DSSM)[:, None]
    )
    mamba_y_grad = gated_grad * silu_z
    gate_z_grad = (gated_grad * mamba_y * sigmoid_z * (1.0 + gate_z * (1.0 - sigmoid_z))).astype(
        jnp.bfloat16
    )
    early_grad = jnp.concatenate([padded(gate_z_grad, wide), dq], axis=1)
    early_w_grad, first_early, gain_one_early = weight_grads(
        ((first_full, early_grad),), (w_in, 0), kind=jnp.float32
    )
    early_w_grad, out_total = together(early_w_grad, out_total)
    early_total = dp_scatter(early_w_grad)
    ffn_out = run(seq_reduce(ffn_part))
    result_b, stat_terms = finish(valid_f[:, None], layer_input, mixer_sum, middle, ffn_out)
    mamba_y_grad, first_early = together(mamba_y_grad, first_early)
    late_grad, taps_grad, params_grad = mamba_backward(
        block_order,
        block_rows,
        late_act,
        common_act,
        doc,
        taps,
        params,
        skip_row,
        mamba_y,
        mamba_y_grad,
        dkv,
        kept_states,
    )

    back = (w_in, late_at // late_grad.shape[1])
    if late_at % late_grad.shape[1]:
        back = (w_in[:, late_at:], 0)
    late_w_grad, first_part, gain_one_late = weight_grads(
        ((first_full, late_grad),), back, first_early
    )
    gain_one_grad = (gain_one_early + gain_one_late)[:, 0] / gains_f[0]
    def by_device(rows_in):
        return jnp.swapaxes(rows_in.reshape(rows_in.shape[0], device_count, -1), 0, 1).reshape(
            device_count, -1
        )

    heads = jnp.concatenate(
        [placed(params_grad[:3, :head_local], MH, head_start).reshape(-1), stat_terms[:6, 0]]
    )
    sums = jnp.concatenate(
        [
            by_device(jnp.stack([gain_one_grad, gain_two_grad], axis=0)),
            by_device(
                jnp.concatenate(
                    [
                        placed(taps_grad[: CONV + 1, :local_width], DSSM, channel_start),
                        taps_grad[: CONV + 1, local_width:],
                    ],
                    axis=1,
                )
            ),
            by_device(placed(own_gain_grad[None], DSSM, channel_start)),
            jnp.broadcast_to(heads[None], (device_count, heads.shape[0])),
        ],
        axis=1,
    )
    sums = padded(sums, -(-sums.shape[1] // 128) * 128)
    sums, early_total = together(sums, early_total)

    def exchanged(blocks):
        (got,) = yield [exchange(blocks, ("dp", "tensor"))]
        return jnp.sum(got, axis=0)

    late_total, first_grad, sums = lockstep(
        ring_scatter(ring, late_w_grad),
        seq_reduce(first_part),
        after_stages(1, exchanged(sums)),
    )
    shared_total = late_total[:, early_width:].astype(jnp.bfloat16)
    shared_rows = shared_proj.shape[0]
    places = [
        ((tensor_position // 2 + chip_count - place // 2) % chip_count) * 2
        + (tensor_position + place) % 2
        for place in range(tensor_count)
    ]
    shared_proj_grad = run(
        tensor_scatter(
            lambda place: lax.dynamic_slice_in_dim(
                shared_total, places[place] * shared_rows, shared_rows, 0
            )
        )
    )
    mamba_out_grad = out_total[:, :local_width].T
    attend_out_grad = out_total[:, local_width:].T
    gate_proj_grad = early_total[:, :local_width]
    query_proj_grad = early_total[:, wide : wide + query_width]
    input_proj_grad = late_total[:, :local_width]
    step_proj_grad = late_total[:, wide : wide + head_local]
    first_value_grad, _ = norm_back(tokens_f, scale_one, gains_f[0], first_grad)
    input_grad = middle_grad + first_value_grad

    gain_cols, conv_cols, mix_cols = (
        norm_gains.shape[1],
        conv_weight.shape[1],
        mixer_gain.shape[0],
    )
    gains_grad = sums[: 2 * gain_cols].reshape(2, gain_cols)
    spot = 2 * gain_cols
    conv_grads = sums[spot : spot + (CONV + 1) * conv_cols].reshape(CONV + 1, conv_cols)
    spot += (CONV + 1) * conv_cols
    gain_full_grad = sums[spot : spot + mix_cols]
    spot += mix_cols
    heads_total = sums[spot : spot + 3 * MH].reshape(3, MH)
    spot += 3 * MH
    residual_rms = jnp.sqrt(sums[spot : spot + 5] / (sums[spot + 5] * D))
    return (
        result_b,
        input_grad,
        gains_grad,
        conv_grads[:CONV],
        conv_grads[CONV],
        gain_full_grad,
        shared_proj_grad,
        heads_total[0],
        heads_total[1],
        heads_total[2],
        gate_proj_grad,
        input_proj_grad,
        step_proj_grad,
        query_proj_grad,
        mamba_out_grad,
        attend_out_grad,
        gate_w_grad,
        up_w_grad,
        down_w_grad,
        residual_rms,
    )


def solution(mesh):
    in_specs = (
        P(("dp", "tensor"), None),
        P(("dp", "tensor"), None),
        P("dp"),
        P(("dp", "tensor")),
        P("dp"),
        P(None, ("dp", "tensor")),
        P(None, ("dp", "tensor")),
        P(("dp", "tensor")),
        P(("dp", "tensor")),
        P(("dp", "tensor"), None),
        P(),
        P(),
        P(),
        P("dp", "tensor"),
        P("dp", "tensor"),
        P("dp", "tensor"),
        P("dp", "tensor"),
        P("tensor", "dp"),
        P("tensor", "dp"),
        P("dp", "tensor"),
        P("dp", "tensor"),
        P("tensor", "dp"),
    )
    out_specs = (
        P(("dp", "tensor"), None),
        P(("dp", "tensor"), None),
        P(None, ("dp", "tensor")),
        P(None, ("dp", "tensor")),
        P(("dp", "tensor")),
        P(("dp", "tensor")),
        P(("dp", "tensor"), None),
        P(),
        P(),
        P(),
        P("dp", "tensor"),
        P("dp", "tensor"),
        P("dp", "tensor"),
        P("dp", "tensor"),
        P("tensor", "dp"),
        P("tensor", "dp"),
        P("dp", "tensor"),
        P("dp", "tensor"),
        P("tensor", "dp"),
        P(),
    )
    return jax.shard_map(local, mesh=mesh, in_specs=in_specs, out_specs=out_specs, check_vma=False)
```

time: 510 us -> 400 us (0.78)
  local copies, waits for them, and re-layouts: 112 us -> 48.8 us
  Pallas kernels: 51.3 us -> 104 us
  waiting for transfers between devices: 129 us -> 86.2 us
  starting transfers between devices: 84.4 us -> 53 us
  matrix products: 44.3 us -> 18.7 us
  between operations: 28.9 us -> 16.2 us
  other arithmetic: 52.6 us -> 60.3 us
  blocking collectives: 0 us -> 6.82 us
    pallas_call x4 -> x10, Pallas kernels: 51.3 us -> 104 us  [the longest x4 36.9 us: weight_grads(): pl.pallas_call(functools.partial(weight_grad_kernel, len(pairs), back is...]
    ppermute x21 -> x0, starting transfers between devices: 29.9 us -> none  [the longest x14 17.2 us: dp_exchange(): lax.ppermute(piece, 'dp', [(k, (k + step) % count) for k in range(count)])]
    ppermute x21 -> x0, waiting for transfers between devices: 28.3 us -> none  [the longest x14 25.8 us: dp_exchange(): lax.ppermute(piece, 'dp', [(k, (k + step) % count) for k in range(count)])]
    ppermute x32 -> x16, starting transfers between devices: 38.3 us -> 17.6 us  [send(): lax.ppermute(block, 'dp', [(order[k], order[(k + step) % count]) for k in...]
    ppermute x14 -> x11, waiting for transfers between devices: 66 us -> 45.4 us  [chip_shift(): lax.ppermute(block, 'tensor', [(k, (k + 2 * step) % count) for k in range...]
    dynamic_update_slice x58 -> x3, local copies, waits for them, and re-layouts: 19.8 us -> 0.08 us  [placed(): return lax.dynamic_update_slice_in_dim(whole, rows_in, start, 1)]
    all_to_all x0 -> x4, starting transfers between devices: none -> 19.6 us  [exchange(): return lax.all_to_all(blocks, axes, 0, 0, tiled=False)]
    dot_general x5 -> x0, matrix products: 14.4 us -> none  [product_tn(): lax.dot_general(left, right, (((0,), (0,)), ((), ())), preferred_element_...]
  transfers between devices with their start and end apart: 97 -> 53, of which waited for: 33 -> 25; matrix products, arithmetic and copies ran while one was open for 34% -> 26% of each run, Pallas kernels for 10% -> 24%
where the time goes in v2:
time: 400 us; the launch traced here: 394 us
  Pallas kernels  104 us (26%)
  waiting for transfers between devices  86.2 us (22%)
  other arithmetic  60.3 us (15%)
  starting transfers between devices  53 us (13%)
  local copies, waits for them, and re-layouts  48.8 us (12%)
  matrix products  18.7 us (5%)
  between operations  16.2 us (4%)
  blocking collectives  6.82 us (2%)
    ppermute x11, waiting for transfers between devices, chip_shift(): lax.ppermute(block, 'tensor', [(k, (k + 2 * step) % count) for k in range...  45.4 us
    pallas_call x4, Pallas kernels, weight_grads(): pl.pallas_call(functools.partial(weight_grad_kernel, len(pairs), back is...  36.9 us
    ppermute x16, waiting for transfers between devices, send(): lax.ppermute(block, 'dp', [(order[k], order[(k + step) % count]) for k in...  24.1 us
    pallas_call x1, Pallas kernels, mamba_backward(): pl.pallas_call(functools.partial(mamba_backward_kernel, chunk, width, blo...  21.2 us
    all_to_all x4, starting transfers between devices, exchange(): return lax.all_to_all(blocks, axes, 0, 0, tiled=False)  19.6 us
    ppermute x16, starting transfers between devices, send(): lax.ppermute(block, 'dp', [(order[k], order[(k + step) % count]) for k in...  17.6 us
    pallas_call x2, Pallas kernels, attention_call(): pl.pallas_call(functools.partial(kernel, block_rows), grid_spec=pltpu.Pre...  17.3 us
    dot_general x4, matrix products, product(): return jnp.dot(left, right, preferred_element_type=jnp.float32)  15.9 us
  transfers between devices with their start and end apart: 53, of which 25 were waited for; matrix products, arithmetic and copies ran while one was open for 26% of the time, Pallas kernels for 24%

profile of v2, /device:TPU:0, one launch (start us, length us, event | category | flops | bytes accessed | tf_op | source)
XLA Modules:
  0.0 393.6 jit_solution(8842755905716719652)
XLA Ops:
  7.2 6.8 %all_gather.6 = bf16[128,512]{1,0:T(8,128)(2,1)S(1)} all-gather(bf16[32,512]{1,0:T(8,128)(2,1)} %param.30), channel_id=1, replica_groups=mesh['dp'=8,'tensor'=4] {'tensor'}, dimensions={0}, use_global_device_ids=true | all-gather | bytes 163840 | tf_op jit(solution)/shard_map/all_gather | solution.py:1033
  14.4 1.9 collective-permute-start.1
  28.1 6.2 %all-to-all-start = ((bf16[32,2,256]{2,1,0:T(2,128)(2,1)}), bf16[32,2,256]{2,1,0:T(2,128)(2,1)S(1)}, u32[]{:S(2)}, u32[]{:S(2)}) async-start(bf16[32,2,256]{2,1,0:T(2,128)(2,1)} %reshape.262), calls=%async_computation | async-start | bytes 65536 | tf_op jit(solution)/shard_map/all_to_all | solution.py:961
  35.0 2.5 broadcast_in_dim.36
  39.6 2.0 all-to-all-done
  46.8 1.9 constant_dynamic-update-slice_fusion.11
  48.7 8.5 %collective-permute-done.5 = bf16[128,2048]{1,0:T(8,128)(2,1)} collective-permute-done((bf16[128,2048]{1,0:T(8,128)(2,1)S(1)}, bf16[128,2048]{1,0:T(8,128)(2,1)}, u32[]{:S(2)}, u32[]{:S(2)}) %collective-permute-start.5) | collective-permute-done | bytes 524320 | tf_op jit(solution)/shard_map/ppermute | solution.py:801
  57.6 1.6 collective-permute-start.7
  59.8 1.9 constant_dynamic-update-slice_fusion.10
  61.7 1.9 constant_dynamic-update-slice_fusion.9
  64.9 5.3 %fusion.2.refs_0_ = bf16[1024,1024]{1,0:T(8,128)(2,1)} fusion(f32[1024]{0:T(1024)S(1)} %mul.434, f32[1024]{0:T(1024)S(1)} %add_rsqrt_fusion, bf16[256,1024]{1,0:T(8,128)(2,1)S(1)} %collective-permute-done.4, bf16[256,1024]{1,0:T(8,128)(2,1)S(1)} %collective-permute-done.1, bf16[256,1024]{1,0:T(8,128)(2,1)S(1)} %collective-permute-done, ...), kind=kLoop, calls=%fused_computation.4 | loop fusion | flops 11534336 | bytes 4202496 | tf_op jit(solution)/shard_map/convert_element_type | solution.py:1082
  73.1 1.6 collective-permute-start.11
  77.1 1.9 constant_dynamic-update-slice_fusion.7
  79.0 2.9 collective-permute-done.11
  81.9 2.3 collective-permute-done.12
  85.7 3.8 fusion.13.x_ref.raw_ref
  89.5 3.8 fusion.11.bc_ref.key_ref.value_ref
  93.3 3.8 fusion.9.z_ref.q_ref
  98.0 13.8 %shard_map.356 = (f32[1024,384]{1,0:T(8,128)}, f32[8,1024]{1,0:T(8,128)}, f32[1024,384]{1,0:T(8,128)}) custom-call(s32[4]{0:T(128)} %fusion.35.order_ref, f32[1024,512]{1,0:T(8,128)} %fusion.13.x_ref.raw_ref, f32[1024,512]{1,0:T(8,128)} %fusion.11.bc_ref.key_ref.value_ref, f32[1024,512]{1,0:T(8,128)} %fusion.13.x_ref.raw_ref, ...), custom_call_target="tpu_custom_call" | custom-call | flops 7864320000 | bytes 7864320 | tf_op jit(solution)/shard_map/pallas_call | solution.py:345
  112.8 3.1 fusion.20
  117.5 8.2 %shard_map.357 = (bf16[1024,128]{1,0:T(8,128)(2,1)}, bf16[1024,128]{1,0:T(8,128)(2,1)}, bf16[1024,128]{1,0:T(8,128)(2,1)}, bf16[1024,128]{1,0:T(8,128)(2,1)}, f32[1024,128]{1,0:T(8,128)}) custom-call(s32[1]{0:T(128)} %bitcast.9.kv_ref, s32[4]{0:T(128)} %fusion.35.order_ref, f32[1024,512]{1,0:T(8,128)} %fusion.9.z_ref.q_ref, ...), custom_call_target="tpu_custom_call" | custom-call | flops 4096000000 | bytes 4194304 | tf_op jit(solution)/shard_map/pallas_call | solution.py:556
  125.8 2.1 multiply_convert_fusion.1
  127.8 2.8 convolution_convert_fusion
  134.3 13.6 %collective-permute-done.18 = bf16[256,1024]{1,0:T(8,128)(2,1)} collective-permute-done((bf16[256,1024]{1,0:T(8,128)(2,1)S(1)}, bf16[256,1024]{1,0:T(8,128)(2,1)}, u32[]{:S(2)}, u32[]{:S(2)}) %collective-permute-start.18) | collective-permute-done | bytes 524320 | tf_op jit(solution)/shard_map/ppermute | solution.py:893
  147.9 2.6 multiply_reduce_fusion.4
  152.7 12.4 %collective-permute-done.20 = bf16[256,1024]{1,0:T(8,128)(2,1)S(1)} collective-permute-done((bf16[256,1024]{1,0:T(8,128)(2,1)S(1)}, bf16[256,1024]{1,0:T(8,128)(2,1)S(1)}, u32[]{:S(2)}, u32[]{:S(2)}) %collective-permute-start.20) | collective-permute-done | bytes 524320 | tf_op jit(solution)/shard_map/ppermute | solution.py:893
  165.1 2.7 pad_maximum_fusion.2.cot_ref.refs_1_
  169.3 11.0 %shard_map.358 = (bf16[1024,1024]{1,0:T(8,128)(2,1)}, bf16[1024,512]{1,0:T(8,128)(2,1)}, bf16[1024,1024]{1,0:T(8,128)(2,1)}, bf16[1024,1024]{1,0:T(8,128)(2,1)}) custom-call(bf16[1024,1024]{1,0:T(8,128)(2,1)} %pad_maximum_fusion.1.x_ref.refs_0_, bf16[1024,1024]{1,0:T(8,128)(2,1)} %pad_maximum_fusion.2.cot_ref.refs_1_, ...), custom_call_target="tpu_custom_call" | custom-call | flops 6442450944 | bytes 14680064 | tf_op jit(solution)/shard_map/pallas_call | solution.py:704
  184.4 2.0 add_convert_fusion.2
  187.0 17.7 %shard_map.359 = bf16[1024,1536]{1,0:T(8,128)(2,1)} custom-call(bf16[1024,1024]{1,0:T(8,128)(2,1)} %pad_maximum_fusion.1.x_ref.refs_0_, bf16[1024,1024]{1,0:T(8,128)(2,1)} %pad_maximum_fusion.2.cot_ref.refs_1_, bf16[1024,1024]{1,0:T(8,128)(2,1)} %get-tuple-element.140.refs_2_, bf16[1024,512]{1,0:T(8,128)(2,1)} %get-tuple-element.141.refs_3_), custom_call_target="tpu_custom_call" | custom-call | flops 3221225472 | bytes 7340032 | tf_op jit(solution)/shard_map/pallas_call | solution.py:668
  204.6 1.9 multiply_reduce_fusion.2
  206.6 1.7 subtract_add_fusion
  211.4 12.5 %collective-permute-done.26 = bf16[256,1024]{1,0:T(8,128)(2,1)} collective-permute-done((bf16[256,1024]{1,0:T(8,128)(2,1)S(1)}, bf16[256,1024]{1,0:T(8,128)(2,1)}, u32[]{:S(2)}, u32[]{:S(2)}) %collective-permute-start.26) | collective-permute-done | bytes 524320 | tf_op jit(solution)/shard_map/ppermute | solution.py:893
  226.2 1.7 pad_maximum_fusion.3.refs_0_
  227.9 4.5 %fusion.16.grad_ref = f32[1024,512]{1,0:T(8,128)} fusion(bf16[1024,1024]{1,0:T(8,128)(2,1)S(1)} %pad_maximum_fusion.3.refs_0_, bf16[1024,2048]{1,0:T(8,128)(2,1)} %constant_dynamic-update-slice_fusion.5.refs_2_), kind=kOutput, calls=%fused_computation.52 | convolution fusion | flops 1073741824 | bytes 5242880 | tf_op jit(solution)/shard_map/dot_general | solution.py:42
  232.4 3.9 shard_map.365
  236.3 4.2 %all-to-all-start.1 = ((bf16[8,128,512]{2,1,0:T(8,128)(2,1)}), bf16[8,128,512]{2,1,0:T(8,128)(2,1)}, u32[]{:S(2)}, u32[]{:S(2)}) async-start(bf16[8,128,512]{2,1,0:T(8,128)(2,1)} %bitcast.46), calls=%async_computation.1 | async-start | bytes 2097152 | tf_op jit(solution)/shard_map/all_to_all | solution.py:961
  240.5 1.9 multiply_reduce_fusion
  242.8 2.4 fusion.45
  245.6 9.1 %shard_map.361 = (bf16[1024,128]{1,0:T(8,128)(2,1)}, bf16[1024,256]{1,0:T(8,128)(2,1)}) custom-call(s32[1]{0:T(128)} %bitcast.9.kv_ref, s32[4]{0:T(128)} %fusion.35.order_ref, bf16[1024,128]{1,0:T(8,128)(2,1)} %get-tuple-element.150.qr_ref, bf16[1024,128]{1,0:T(8,128)(2,1)} %get-tuple-element.151.kr_ref, bf16[1024,128]{1,0:T(8,128)(2,1)} %get-tuple-element.152.vr_ref, ...), custom_call_target="tpu_custom_call" | custom-call | flops 9216000000 | bytes 4194304 | tf_op jit(solution)/shard_map/pallas_call | solution.py:556
  254.8 1.7 collective-permute-start.32
  256.6 1.9 collective-permute-done.32
  258.5 3.4 multiply_convert_fusion
  263.0 6.0 %shard_map.362 = (bf16[1024,512]{1,0:T(8,128)(2,1)}, f32[1024,1024]{1,0:T(8,128)}, f32[1024,1]{1,0:T(8,128)}) custom-call(bf16[1024,1024]{1,0:T(8,128)(2,1)} %fusion.2.refs_0_, bf16[1024,512]{1,0:T(8,128)(2,1)} %pad_maximum_fusion.5.refs_1_, bf16[1024,2048]{1,0:T(8,128)(2,1)} %constant_dynamic-update-slice_fusion.5.refs_2_), custom_call_target="tpu_custom_call" | custom-call | flops 2147483648 | bytes 5242880 | tf_op jit(solution)/shard_map/pallas_call | solution.py:668
  269.0 21.2 %shard_map.363 = (bf16[1024,1024]{1,0:T(8,128)(2,1)}, f32[8,640]{1,0:T(8,128)}, f32[8,128]{1,0:T(8,128)}) custom-call(s32[4]{0:T(128)} %fusion.35.order_ref, f32[1024,512]{1,0:T(8,128)} %fusion.13.x_ref.raw_ref, f32[1024,512]{1,0:T(8,128)} %fusion.11.bc_ref.key_ref.value_ref, f32[1024,512]{1,0:T(8,128)} %fusion.13.x_ref.raw_ref, s32[1024,1]{1,0:T(8,128)} %copy.118.doc_ref, ...), custom_call_target="tpu_custom_call" | custom-call | flops 23592960000 | bytes 7864320 | tf_op jit(solution)/shard_map/pallas_call | solution.py:393
  291.1 9.3 %shard_map.364 = (bf16[1024,1024]{1,0:T(8,128)(2,1)}, bf16[1024,1024]{1,0:T(8,128)(2,1)}, f32[1024,1]{1,0:T(8,128)}) custom-call(bf16[1024,1024]{1,0:T(8,128)(2,1)} %fusion.2.refs_0_, bf16[1024,1024]{1,0:T(8,128)(2,1)} %get-tuple-element.159.refs_1_, bf16[1024,2048]{1,0:T(8,128)(2,1)} %constant_dynamic-update-slice_fusion.5.refs_2_, ...), custom_call_target="tpu_custom_call" | custom-call | flops 4294967296 | bytes 6291456 | tf_op jit(solution)/shard_map/pallas_call | solution.py:668
  301.9 2.4 fusion.44
  304.8 1.7 constant_dynamic-slice_fusion.2
  306.5 1.6 collective-permute-start.33
  310.0 5.7 %all-to-all-start.2 = ((bf16[8,128,512]{2,1,0:T(8,128)(2,1)}), bf16[8,128,512]{2,1,0:T(8,128)(2,1)S(1)}, u32[]{:S(2)}, u32[]{:S(2)}) async-start(bf16[8,128,512]{2,1,0:T(8,128)(2,1)} %bitcast.47), calls=%async_computation.2 | async-start | bytes 2097152 | tf_op jit(solution)/shard_map/all_to_all | solution.py:961
  315.7 2.2 add_convert_fusion.1
  317.9 1.7 collective-permute-start.30
  320.6 2.0 add_convert_fusion
  323.0 2.0 add_convert_fusion.8
  324.9 3.1 collective-permute-start.37
  328.0 4.9 %collective-permute-done.30 = bf16[256,1024]{1,0:T(8,128)(2,1)S(1)} collective-permute-done((bf16[256,1024]{1,0:T(8,128)(2,1)}, bf16[256,1024]{1,0:T(8,128)(2,1)S(1)}, u32[]{:S(2)}, u32[]{:S(2)}) %collective-permute-start.30) | collective-permute-done | bytes 524320 | tf_op jit(solution)/shard_map/ppermute | solution.py:893
  333.0 2.5 convert_add_fusion.1.ffn_ref
  335.5 3.3 shard_map.360
  340.6 3.1 all-to-all-done.2
  344.5 3.4 all-to-all-start.3
  350.0 5.3 %all-to-all-done.3 = f32[32,1,512]{2,1,0:T(1,128)S(1)} async-done(((f32[32,1,512]{2,1,0:T(1,128)}), f32[32,1,512]{2,1,0:T(1,128)S(1)}, u32[]{:S(2)}, u32[]{:S(2)}) %all-to-all-start.3) | async-done | bytes 65568 | tf_op jit(solution)/shard_map/all_to_all | solution.py:961
  360.4 4.8 %collective-permute-done.40 = bf16[128,1024]{1,0:T(8,128)(2,1)S(1)} collective-permute-done((bf16[128,1024]{1,0:T(8,128)(2,1)S(1)}, bf16[128,1024]{1,0:T(8,128)(2,1)S(1)}, u32[]{:S(2)}, u32[]{:S(2)}) %collective-permute-start.40) | collective-permute-done | bytes 262176 | tf_op jit(solution)/shard_map/ppermute | solution.py:801
  368.9 2.4 fusion.7
  371.3 2.8 collective-permute-done.42
  (309 shorter events, 82.5 us)
Async XLA Ops:
  7.2 18.7 %copy-start.37 = (bf16[2,32]{1,0:T(2,128)(2,1)S(1)}, bf16[2,32]{1,0:T(2,128)(2,1)}, u32[]{:S(2)}) copy-start(bf16[2,32]{1,0:T(2,128)(2,1)} %param.26) | copy-start | bytes 388
  7.2 18.8 %copy-start.36 = (bf16[4,56]{1,0:T(4,128)(2,1)S(1)}, bf16[4,56]{1,0:T(4,128)(2,1)}, u32[]{:S(2)}) copy-start(bf16[4,56]{1,0:T(4,128)(2,1)} %param.27) | copy-start | bytes 1348
  7.2 18.8 %copy-start.35 = (bf16[56]{0:T(256)(128)(2,1)S(1)}, bf16[56]{0:T(256)(128)(2,1)}, u32[]{:S(2)}) copy-start(bf16[56]{0:T(256)(128)(2,1)} %param.28) | copy-start | bytes 340
  7.2 18.8 %copy-start.34 = (bf16[48]{0:T(256)(128)(2,1)S(1)}, bf16[48]{0:T(256)(128)(2,1)}, u32[]{:S(2)}) copy-start(bf16[48]{0:T(256)(128)(2,1)} %param.29) | copy-start | bytes 292
  7.2 27.5 %copy-start.38 = (f32[24]{0:T(128)S(1)}, f32[24]{0:T(128)}, u32[]{:S(2)}) copy-start(f32[24]{0:T(128)} %param.33) | copy-start | bytes 292
  14.1 28.4 %collective-permute-start = (bf16[256,1024]{1,0:T(8,128)(2,1)}, bf16[256,1024]{1,0:T(8,128)(2,1)S(1)}, u32[]{:S(2)}, u32[]{:S(2)}) collective-permute-start(bf16[256,1024]{1,0:T(8,128)(2,1)} %x_ref), channel_id=1, source_target_pairs={{0,1},{1,0},{2,3},{3,2},{4,5},{5,4},{6,7},{7,6},{8,9},{9,8},{10,11... | collective-permute-start | bytes 1572872 | tf_op jit(solution)/shard_map/ppermute | solution.py:888
  14.4 28.2 %collective-permute-start.1 = (bf16[256,1024]{1,0:T(8,128)(2,1)}, bf16[256,1024]{1,0:T(8,128)(2,1)S(1)}, u32[]{:S(2)}, u32[]{:S(2)}) collective-permute-start(bf16[256,1024]{1,0:T(8,128)(2,1)} %x_ref), channel_id=1, source_target_pairs={{0,2},{1,3},{2,0},{3,1},{4,6},{5,7},{6,4},{7,5},{8,10},{9,11},{10,... | collective-permute-start | bytes 1572872 | tf_op jit(solution)/shard_map/ppermute | solution.py:893
  21.7 21.0 %collective-permute-start.2 = (bf16[128,2048]{1,0:T(8,128)(2,1)S(1)}, bf16[128,2048]{1,0:T(8,128)(2,1)S(1)}, u32[]{:S(2)}, u32[]{:S(2)}) collective-permute-start(bf16[128,2048]{1,0:T(8,128)(2,1)S(1)} %constant_dynamic-update-slice_fusion), channel_id=1, source_target_pairs={{4,12},{12,20},{20,28},{28,24},{24,16},{16,8},{8,0},{0,4},{5,13},{... | collective-permute-start | bytes 1572872 | tf_op jit(solution)/shard_map/ppermute | solution.py:801
  23.3 19.4 %collective-permute-start.3 = (bf16[128,2048]{1,0:T(8,128)(2,1)S(1)}, bf16[128,2048]{1,0:T(8,128)(2,1)}, u32[]{:S(2)}, u32[]{:S(2)}) collective-permute-start(bf16[128,2048]{1,0:T(8,128)(2,1)S(1)} %constant_dynamic-update-slice_fusion), channel_id=1, source_target_pairs={{4,0},{12,4},{20,12},{28,20},{24,28},{16,24},{8,16},{0,8},{5,1},{1... | collective-permute-start | bytes 1572872 | tf_op jit(solution)/shard_map/ppermute | solution.py:801
  25.6 44.5 %collective-permute-start.10 = (bf16[256,1024]{1,0:T(8,128)(2,1)S(1)}, bf16[256,1024]{1,0:T(8,128)(2,1)}, u32[]{:S(2)}, u32[]{:S(2)}) collective-permute-start(bf16[256,1024]{1,0:T(8,128)(2,1)S(1)} %fusion.15), channel_id=1, source_target_pairs={{0,2},{1,3},{2,0},{3,1},{4,6},{5,7},{6,4},{7,5},{8,10},{9,11},{10,... | collective-permute-start | bytes 1572872 | tf_op jit(solution)/shard_map/ppermute | solution.py:893
  28.1 13.5 %all-to-all-start = ((bf16[32,2,256]{2,1,0:T(2,128)(2,1)}), bf16[32,2,256]{2,1,0:T(2,128)(2,1)S(1)}, u32[]{:S(2)}, u32[]{:S(2)}) async-start(bf16[32,2,256]{2,1,0:T(2,128)(2,1)} %reshape.262), calls=%async_computation | async-start | bytes 65536 | tf_op jit(solution)/shard_map/all_to_all | solution.py:961
  34.4 135.0 %all-gather.2.cloned.1.call-start = ((), (), s32[]{:S(2)}) async-start(), calls=%async_computation.5 | async-start | bytes 3538944 | tf_op jit(solution)/shard_map/all_gather | solution.py:1069
  37.5 22.1 %copy-start.27 = (bf16[512,128]{1,0:T(8,128)(2,1)S(1)}, bf16[512,128]{1,0:T(8,128)(2,1)}, u32[]{:S(2)}) copy-start(bf16[512,128]{1,0:T(8,128)(2,1)} %param.42) | copy-start | bytes 393220
  42.5 27.7 %collective-permute-start.9 = (bf16[256,1024]{1,0:T(8,128)(2,1)S(1)}, bf16[256,1024]{1,0:T(8,128)(2,1)}, u32[]{:S(2)}, u32[]{:S(2)}) collective-permute-start(bf16[256,1024]{1,0:T(8,128)(2,1)S(1)} %fusion.15), channel_id=1, source_target_pairs={{0,1},{1,0},{2,3},{3,2},{4,5},{5,4},{6,7},{7,6},{8,9},{9,8},{10,11... | collective-permute-start | bytes 1572872 | tf_op jit(solution)/shard_map/ppermute | solution.py:888
  42.7 6.1 %collective-permute-start.4 = (bf16[256,1024]{1,0:T(8,128)(2,1)S(1)}, bf16[256,1024]{1,0:T(8,128)(2,1)S(1)}, u32[]{:S(2)}, u32[]{:S(2)}) collective-permute-start(bf16[256,1024]{1,0:T(8,128)(2,1)S(1)} %collective-permute-done.1), channel_id=1, source_target_pairs={{0,1},{1,0},{2,3},{3,2},{4,5},{5,4},{6,7},{7,6},{8,9},{9,8},{10,11... | collective-permute-start | bytes 1572872 | tf_op jit(solution)/shard_map/ppermute | solution.py:888
  43.1 14.0 %collective-permute-start.5 = (bf16[128,2048]{1,0:T(8,128)(2,1)S(1)}, bf16[128,2048]{1,0:T(8,128)(2,1)}, u32[]{:S(2)}, u32[]{:S(2)}) collective-permute-start(bf16[128,2048]{1,0:T(8,128)(2,1)S(1)} %collective-permute-done.2), channel_id=1, source_target_pairs={{4,12},{12,20},{20,28},{28,24},{24,16},{16,8},{8,0},{0,4},{5,13},{... | collective-permute-start | bytes 1572872 | tf_op jit(solution)/shard_map/ppermute | solution.py:801
  43.7 14.0 %collective-permute-start.6 = (bf16[128,2048]{1,0:T(8,128)(2,1)}, bf16[128,2048]{1,0:T(8,128)(2,1)}, u32[]{:S(2)}, u32[]{:S(2)}) collective-permute-start(bf16[128,2048]{1,0:T(8,128)(2,1)} %collective-permute-done.3), channel_id=1, source_target_pairs={{4,0},{12,4},{20,12},{28,20},{24,28},{16,24},{8,16},{0,8},{5,1},{1... | collective-permute-start | bytes 1572872 | tf_op jit(solution)/shard_map/ppermute | solution.py:801
  46.0 17.6 %copy-start.1 = (bf16[256,1024]{1,0:T(8,128)(2,1)S(1)}, bf16[256,1024]{1,0:T(8,128)(2,1)}, u32[]{:S(2)}) copy-start(bf16[256,1024]{1,0:T(8,128)(2,1)} %x_ref) | copy-start | bytes 1572868
  57.6 13.0 %collective-permute-start.7 = (bf16[128,2048]{1,0:T(8,128)(2,1)}, bf16[128,2048]{1,0:T(8,128)(2,1)S(1)}, u32[]{:S(2)}, u32[]{:S(2)}) collective-permute-start(bf16[128,2048]{1,0:T(8,128)(2,1)} %collective-permute-done.5), channel_id=1, source_target_pairs={{4,12},{12,20},{20,28},{28,24},{24,16},{16,8},{8,0},{0,4},{5,13},{... | collective-permute-start | bytes 1572872 | tf_op jit(solution)/shard_map/ppermute | solution.py:801
  59.2 12.8 %collective-permute-start.8 = (bf16[128,2048]{1,0:T(8,128)(2,1)}, bf16[128,2048]{1,0:T(8,128)(2,1)}, u32[]{:S(2)}, u32[]{:S(2)}) collective-permute-start(bf16[128,2048]{1,0:T(8,128)(2,1)} %collective-permute-done.6), channel_id=1, source_target_pairs={{4,0},{12,4},{20,12},{28,20},{24,28},{16,24},{8,16},{0,8},{5,1},{1... | collective-permute-start | bytes 1572872 | tf_op jit(solution)/shard_map/ppermute | solution.py:801
  72.1 12.1 %collective-permute-start.13 = (bf16[256,1024]{1,0:T(8,128)(2,1)}, bf16[256,1024]{1,0:T(8,128)(2,1)S(1)}, u32[]{:S(2)}, u32[]{:S(2)}) collective-permute-start(bf16[256,1024]{1,0:T(8,128)(2,1)} %collective-permute-done.10), channel_id=1, source_target_pairs={{0,1},{1,0},{2,3},{3,2},{4,5},{5,4},{6,7},{7,6},{8,9},{9,8},{10,11... | collective-permute-start | bytes 1572872 | tf_op jit(solution)/shard_map/ppermute | solution.py:888
  73.1 8.8 %collective-permute-start.11 = (bf16[64,2048]{1,0:T(8,128)(2,1)S(1)}, bf16[64,2048]{1,0:T(8,128)(2,1)S(1)}, u32[]{:S(2)}, u32[]{:S(2)}) collective-permute-start(bf16[64,2048]{1,0:T(8,128)(2,1)S(1)} %slice.211), channel_id=1, source_target_pairs={{4,12},{12,20},{20,28},{28,24},{24,16},{16,8},{8,0},{0,4},{5,13},{... | collective-permute-start | bytes 786440 | tf_op jit(solution)/shard_map/ppermute | solution.py:801
  75.7 8.5 %collective-permute-start.12 = (bf16[64,2048]{1,0:T(8,128)(2,1)S(1)}, bf16[64,2048]{1,0:T(8,128)(2,1)S(1)}, u32[]{:S(2)}, u32[]{:S(2)}) collective-permute-start(bf16[64,2048]{1,0:T(8,128)(2,1)S(1)} %slice.212), channel_id=1, source_target_pairs={{4,0},{12,4},{20,12},{28,20},{24,28},{16,24},{8,16},{0,8},{5,1},{1... | collective-permute-start | bytes 786440 | tf_op jit(solution)/shard_map/ppermute | solution.py:801
  97.1 286.5 %reduce-scatter.2.cloned.1.call-start = ((), (), s32[]{:S(2)}) async-start(), calls=%async_computation.6 | async-start | bytes 3538944 | tf_op jit(solution)/shard_map/reduce_scatter | solution.py:1137
  112.7 3.2 collective-permute-start.14
  115.9 9.8 %collective-permute-start.15 = (f32[2,2,256]{2,1,0:T(2,128)S(1)}, f32[2,2,256]{2,1,0:T(2,128)S(1)}, u32[]{:S(2)}, u32[]{:S(2)}) collective-permute-start(f32[2,2,256]{2,1,0:T(2,128)S(1)} %add.589), channel_id=1, source_target_pairs={{0,2},{1,3},{2,0},{3,1},{4,6},{5,7},{6,4},{7,5},{8,10},{9,11},{10,... | collective-permute-start | bytes 12296 | tf_op jit(solution)/shard_map/ppermute | solution.py:893
  130.7 2.1 collective-permute-start.16
  131.0 2.4 collective-permute-start.17
  133.7 14.2 %collective-permute-start.18 = (bf16[256,1024]{1,0:T(8,128)(2,1)S(1)}, bf16[256,1024]{1,0:T(8,128)(2,1)}, u32[]{:S(2)}, u32[]{:S(2)}) collective-permute-start(bf16[256,1024]{1,0:T(8,128)(2,1)S(1)} %add_convert_fusion.3), channel_id=1, source_target_pairs={{0,2},{1,3},{2,0},{3,1},{4,6},{5,7},{6,4},{7,5},{8,10},{9,11},{10,... | collective-permute-start | bytes 1572872 | tf_op jit(solution)/shard_map/ppermute | solution.py:893
  134.3 30.8 %copy-start.16 = (bf16[256,1024]{1,0:T(8,128)(2,1)S(1)}, bf16[256,1024]{1,0:T(8,128)(2,1)}, u32[]{:S(2)}) copy-start(bf16[256,1024]{1,0:T(8,128)(2,1)} %copy-done.15) | copy-start | bytes 1572868
  134.3 30.8 %copy-start.22 = (bf16[256,1024]{1,0:T(8,128)(2,1)S(1)}, bf16[256,1024]{1,0:T(8,128)(2,1)}, u32[]{:S(2)}) copy-start(bf16[256,1024]{1,0:T(8,128)(2,1)} %copy-done.21) | copy-start | bytes 1572868
  150.5 56.0 %copy-start = (f32[256,1024]{1,0:T(8,128)}, f32[256,1024]{1,0:T(8,128)S(1)}, u32[]{:S(2)}) copy-start(f32[256,1024]{1,0:T(8,128)S(1)} %get-tuple-element.297.middle_ref) | copy-start | bytes 3145732
  150.7 2.0 collective-permute-start.19
  150.8 14.3 %collective-permute-start.20 = (bf16[256,1024]{1,0:T(8,128)(2,1)S(1)}, bf16[256,1024]{1,0:T(8,128)(2,1)S(1)}, u32[]{:S(2)}, u32[]{:S(2)}) collective-permute-start(bf16[256,1024]{1,0:T(8,128)(2,1)S(1)} %multiply_convert_fusion.2), channel_id=1, source_target_pairs={{0,2},{1,3},{2,0},{3,1},{4,6},{5,7},{6,4},{7,5},{8,10},{9,11},{10,... | collective-permute-start | bytes 1572872 | tf_op jit(solution)/shard_map/ppermute | solution.py:893
  165.1 2.7 collective-permute-start.21
  181.6 2.1 collective-permute-start.22
  182.1 2.3 collective-permute-start.23
  186.5 18.2 %collective-permute-start.24 = (bf16[256,1024]{1,0:T(8,128)(2,1)}, bf16[256,1024]{1,0:T(8,128)(2,1)}, u32[]{:S(2)}, u32[]{:S(2)}) collective-permute-start(bf16[256,1024]{1,0:T(8,128)(2,1)} %add_convert_fusion.2), channel_id=1, source_target_pairs={{0,2},{1,3},{2,0},{3,1},{4,6},{5,7},{6,4},{7,5},{8,10},{9,11},{10,... | collective-permute-start | bytes 1572872 | tf_op jit(solution)/shard_map/ppermute | solution.py:893
  209.4 2.0 collective-permute-start.25
  209.7 14.2 %collective-permute-start.26 = (bf16[256,1024]{1,0:T(8,128)(2,1)S(1)}, bf16[256,1024]{1,0:T(8,128)(2,1)}, u32[]{:S(2)}, u32[]{:S(2)}) collective-permute-start(bf16[256,1024]{1,0:T(8,128)(2,1)S(1)} %convert_element_type.243), channel_id=1, source_target_pairs={{0,2},{1,3},{2,0},{3,1},{4,6},{5,7},{6,4},{7,5},{8,10},{9,11},{10,... | collective-permute-start | bytes 1572872 | tf_op jit(solution)/shard_map/ppermute | solution.py:893
  223.9 2.3 collective-permute-start.27
  236.3 72.3 %all-to-all-start.1 = ((bf16[8,128,512]{2,1,0:T(8,128)(2,1)}), bf16[8,128,512]{2,1,0:T(8,128)(2,1)}, u32[]{:S(2)}, u32[]{:S(2)}) async-start(bf16[8,128,512]{2,1,0:T(8,128)(2,1)} %bitcast.46), calls=%async_computation.1 | async-start | bytes 2097152 | tf_op jit(solution)/shard_map/all_to_all | solution.py:961
  242.4 12.3 %collective-permute-start.31 = (f32[2,2,256]{2,1,0:T(2,128)S(1)}, f32[2,2,256]{2,1,0:T(2,128)S(1)}, u32[]{:S(2)}, u32[]{:S(2)}) collective-permute-start(f32[2,2,256]{2,1,0:T(2,128)S(1)} %reshape.231), channel_id=1, source_target_pairs={{0,1},{1,0},{2,3},{3,2},{4,5},{5,4},{6,7},{7,6},{8,9},{9,8},{10,11... | collective-permute-start | bytes 12296 | tf_op jit(solution)/shard_map/ppermute | solution.py:888
  245.1 63.0 %collective-permute-start.28 = (bf16[256,1024]{1,0:T(8,128)(2,1)}, bf16[256,1024]{1,0:T(8,128)(2,1)}, u32[]{:S(2)}, u32[]{:S(2)}) collective-permute-start(bf16[256,1024]{1,0:T(8,128)(2,1)} %get-tuple-element.314), channel_id=1, source_target_pairs={{0,1},{1,0},{2,3},{3,2},{4,5},{5,4},{6,7},{7,6},{8,9},{9,8},{10,11... | collective-permute-start | bytes 1572872 | tf_op jit(solution)/shard_map/ppermute | solution.py:888
  245.4 63.2 %collective-permute-start.29 = (bf16[256,1024]{1,0:T(8,128)(2,1)}, bf16[256,1024]{1,0:T(8,128)(2,1)}, u32[]{:S(2)}, u32[]{:S(2)}) collective-permute-start(bf16[256,1024]{1,0:T(8,128)(2,1)} %get-tuple-element.313), channel_id=1, source_target_pairs={{0,1},{1,0},{2,3},{3,2},{4,5},{5,4},{6,7},{7,6},{8,9},{9,8},{10,11... | collective-permute-start | bytes 1572872 | tf_op jit(solution)/shard_map/ppermute | solution.py:888
  254.8 3.7 collective-permute-start.32
  304.3 15.6 %collective-permute-start.35 = (bf16[256,1024]{1,0:T(8,128)(2,1)}, bf16[256,1024]{1,0:T(8,128)(2,1)S(1)}, u32[]{:S(2)}, u32[]{:S(2)}) collective-permute-start(bf16[256,1024]{1,0:T(8,128)(2,1)} %get-tuple-element.310), channel_id=1, source_target_pairs={{0,1},{1,0},{2,3},{3,2},{4,5},{5,4},{6,7},{7,6},{8,9},{9,8},{10,11... | collective-permute-start | bytes 1572872 | tf_op jit(solution)/shard_map/ppermute | solution.py:888
  304.3 15.7 %collective-permute-start.36 = (bf16[256,1024]{1,0:T(8,128)(2,1)}, bf16[256,1024]{1,0:T(8,128)(2,1)S(1)}, u32[]{:S(2)}, u32[]{:S(2)}) collective-permute-start(bf16[256,1024]{1,0:T(8,128)(2,1)} %get-tuple-element.309), channel_id=1, source_target_pairs={{0,1},{1,0},{2,3},{3,2},{4,5},{5,4},{6,7},{7,6},{8,9},{9,8},{10,11... | collective-permute-start | bytes 1572872 | tf_op jit(solution)/shard_map/ppermute | solution.py:888
  306.5 13.4 %collective-permute-start.33 = (bf16[64,1024]{1,0:T(8,128)(2,1)}, bf16[64,1024]{1,0:T(8,128)(2,1)S(1)}, u32[]{:S(2)}, u32[]{:S(2)}) collective-permute-start(bf16[64,1024]{1,0:T(8,128)(2,1)} %get-tuple-element.312), channel_id=1, source_target_pairs={{4,12},{12,20},{20,28},{28,24},{24,16},{16,8},{8,0},{0,4},{5,13},{... | collective-permute-start | bytes 393224 | tf_op jit(solution)/shard_map/ppermute | solution.py:801
  308.1 11.8 %collective-permute-start.34 = (bf16[64,1024]{1,0:T(8,128)(2,1)}, bf16[64,1024]{1,0:T(8,128)(2,1)S(1)}, u32[]{:S(2)}, u32[]{:S(2)}) collective-permute-start(bf16[64,1024]{1,0:T(8,128)(2,1)} %get-tuple-element.311), channel_id=1, source_target_pairs={{4,0},{12,4},{20,12},{28,20},{24,28},{16,24},{8,16},{0,8},{5,1},{1... | collective-permute-start | bytes 393224 | tf_op jit(solution)/shard_map/ppermute | solution.py:801
  310.0 33.7 %all-to-all-start.2 = ((bf16[8,128,512]{2,1,0:T(8,128)(2,1)}), bf16[8,128,512]{2,1,0:T(8,128)(2,1)S(1)}, u32[]{:S(2)}, u32[]{:S(2)}) async-start(bf16[8,128,512]{2,1,0:T(8,128)(2,1)} %bitcast.47), calls=%async_computation.2 | async-start | bytes 2097152 | tf_op jit(solution)/shard_map/all_to_all | solution.py:961
  317.9 15.1 %collective-permute-start.30 = (bf16[256,1024]{1,0:T(8,128)(2,1)}, bf16[256,1024]{1,0:T(8,128)(2,1)S(1)}, u32[]{:S(2)}, u32[]{:S(2)}) collective-permute-start(bf16[256,1024]{1,0:T(8,128)(2,1)} %add_convert_fusion.1), channel_id=1, source_target_pairs={{0,2},{1,3},{2,0},{3,1},{4,6},{5,7},{6,4},{7,5},{8,10},{9,11},{10,... | collective-permute-start | bytes 1572872 | tf_op jit(solution)/shard_map/ppermute | solution.py:893
  322.7 32.7 %collective-permute-start.39 = (bf16[256,1024]{1,0:T(8,128)(2,1)}, bf16[256,1024]{1,0:T(8,128)(2,1)S(1)}, u32[]{:S(2)}, u32[]{:S(2)}) collective-permute-start(bf16[256,1024]{1,0:T(8,128)(2,1)} %add_convert_fusion), channel_id=1, source_target_pairs={{0,2},{1,3},{2,0},{3,1},{4,6},{5,7},{6,4},{7,5},{8,10},{9,11},{10,... | collective-permute-start | bytes 1572872 | tf_op jit(solution)/shard_map/ppermute | solution.py:893
  324.9 30.4 %collective-permute-start.37 = (bf16[128,1024]{1,0:T(8,128)(2,1)}, bf16[128,1024]{1,0:T(8,128)(2,1)}, u32[]{:S(2)}, u32[]{:S(2)}) collective-permute-start(bf16[128,1024]{1,0:T(8,128)(2,1)} %get-tuple-element.308), channel_id=1, source_target_pairs={{4,12},{12,20},{20,28},{28,24},{24,16},{16,8},{8,0},{0,4},{5,13},{... | collective-permute-start | bytes 786440 | tf_op jit(solution)/shard_map/ppermute | solution.py:801
  328.0 27.3 %collective-permute-start.38 = (bf16[128,1024]{1,0:T(8,128)(2,1)}, bf16[128,1024]{1,0:T(8,128)(2,1)}, u32[]{:S(2)}, u32[]{:S(2)}) collective-permute-start(bf16[128,1024]{1,0:T(8,128)(2,1)} %get-tuple-element.307), channel_id=1, source_target_pairs={{4,0},{12,4},{20,12},{28,20},{24,28},{16,24},{8,16},{0,8},{5,1},{1... | collective-permute-start | bytes 786440 | tf_op jit(solution)/shard_map/ppermute | solution.py:801
  340.6 18.2 %copy-start.2 = (bf16[256,1024]{1,0:T(8,128)(2,1)S(1)}, bf16[256,1024]{1,0:T(8,128)(2,1)}, u32[]{:S(2)}) copy-start(bf16[256,1024]{1,0:T(8,128)(2,1)} %x_ref) | copy-start | bytes 1572868
  344.5 10.8 %all-to-all-start.3 = ((f32[32,1,512]{2,1,0:T(1,128)}), f32[32,1,512]{2,1,0:T(1,128)S(1)}, u32[]{:S(2)}, u32[]{:S(2)}) async-start(f32[32,1,512]{2,1,0:T(1,128)} %copy.129), calls=%async_computation.3 | async-start | bytes 131072 | tf_op jit(solution)/shard_map/all_to_all | solution.py:961
  356.8 8.4 %collective-permute-start.40 = (bf16[128,1024]{1,0:T(8,128)(2,1)S(1)}, bf16[128,1024]{1,0:T(8,128)(2,1)S(1)}, u32[]{:S(2)}, u32[]{:S(2)}) collective-permute-start(bf16[128,1024]{1,0:T(8,128)(2,1)S(1)} %get-tuple-element.306), channel_id=1, source_target_pairs={{4,12},{12,20},{20,28},{28,24},{24,16},{16,8},{8,0},{0,4},{5,13},{... | collective-permute-start | bytes 786440 | tf_op jit(solution)/shard_map/ppermute | solution.py:801
  357.4 8.1 %collective-permute-start.41 = (bf16[128,1024]{1,0:T(8,128)(2,1)S(1)}, bf16[128,1024]{1,0:T(8,128)(2,1)}, u32[]{:S(2)}, u32[]{:S(2)}) collective-permute-start(bf16[128,1024]{1,0:T(8,128)(2,1)S(1)} %get-tuple-element.305), channel_id=1, source_target_pairs={{4,0},{12,4},{20,12},{28,20},{24,28},{16,24},{8,16},{0,8},{5,1},{1... | collective-permute-start | bytes 786440 | tf_op jit(solution)/shard_map/ppermute | solution.py:801
  366.8 7.3 %collective-permute-start.42 = (bf16[128,1024]{1,0:T(8,128)(2,1)S(1)}, bf16[128,1024]{1,0:T(8,128)(2,1)S(1)}, u32[]{:S(2)}, u32[]{:S(2)}) collective-permute-start(bf16[128,1024]{1,0:T(8,128)(2,1)S(1)} %get-tuple-element.304), channel_id=1, source_target_pairs={{4,12},{12,20},{20,28},{28,24},{24,16},{16,8},{8,0},{0,4},{5,13},{... | collective-permute-start | bytes 786440 | tf_op jit(solution)/shard_map/ppermute | solution.py:801
  367.5 6.8 %collective-permute-start.43 = (bf16[128,1024]{1,0:T(8,128)(2,1)S(1)}, bf16[128,1024]{1,0:T(8,128)(2,1)S(1)}, u32[]{:S(2)}, u32[]{:S(2)}) collective-permute-start(bf16[128,1024]{1,0:T(8,128)(2,1)S(1)} %get-tuple-element.303), channel_id=1, source_target_pairs={{4,0},{12,4},{20,12},{28,20},{24,28},{16,24},{8,16},{0,8},{5,1},{1... | collective-permute-start | bytes 786440 | tf_op jit(solution)/shard_map/ppermute | solution.py:801
  375.4 2.4 collective-permute-start.44
  375.5 2.3 collective-permute-start.45
  377.9 5.1 %collective-permute-start.46 = (bf16[32,512]{1,0:T(8,128)(2,1)S(1)}, bf16[32,512]{1,0:T(8,128)(2,1)S(1)}, u32[]{:S(2)}, u32[]{:S(2)}) collective-permute-start(bf16[32,512]{1,0:T(8,128)(2,1)S(1)} %add_convert_fusion.10), channel_id=1, source_target_pairs={{0,2},{1,3},{2,0},{3,1},{4,6},{5,7},{6,4},{7,5},{8,10},{9,11},{10,... | collective-permute-start | bytes 98312 | tf_op jit(solution)/shard_map/ppermute | solution.py:893
  (28 other events, 182.6 us)
Sparse Core Ops, SparseCore 0:
  97.2 59.3 all-gather.1
  226.0 96.4 reduce-scatter.1
